TPU v7x, 32 devices: a whole 2x2x4 slice. The times are simulated.
32 devices in a mesh: row: 4 (over y, core), col: 8 (over z, x).
Axes of the slice: x: 2, y: 2, z: 4, core: 2. Of those that a mesh axis runs over, the one named last changes fastest.
Arguments:
- start_block: float32 [64, 65536], P(None, ('row', 'col')), may hold values from -6 to 6
- struct_blocks: bfloat16 [3, 512, 4, 128, 128], P(None, ('row', 'col'))
- block_ids: int32 [512, 4], P(('row', 'col')), may hold values from 0 to 17, as said below
- rim_rows: int32 [4096], P(('row', 'col')), may hold values from 0 to 2047, as said below
- wet_slots: int32 [32768], P(('row', 'col')), may hold values from 0 to 2047, as said below
- wet_counts: int32 [32], P(('row', 'col')), may hold values from 341 to 1024
- added_mass: bfloat16 [1024, 32768], P('col', 'row'), may hold values from -0.03125 to 0.03125
- coupling_rates: float32 [2], replicated, may hold values from 0.5 to 1.5
Outputs:
- lanczos_block: float32 [64, 65536], P(None, ('row', 'col'))
- coefficients: float32 [6, 3, 64, 64], replicated
Inputs may be any that keep to these rules, and one draw needn't show every extreme that they name: `block_ids`: each block row's first entry is its own local block row; the first local block row names 2048//128 (rim of the shard before) as its second entry and the last names 17; entries may repeat. `rim_rows`: local indices into a shard's 2048 degrees of freedom, distinct within one shard. `wet_slots`: local indices into a shard's 2048 degrees of freedom, distinct within one shard.
All inputs are finite; a program needn't handle non-finite values.
Results may differ from a plain program's by a relative error of at most 0.023.
Values may be sent and summed in bfloat16 or wider, within the bound.
No kernel may reach another device: no remote copies, remote signals or barrier semaphores. Data moves between devices by JAX's collectives and lax.ppermute only.
A program may use at most 128 MiB of HBM per device.

v0:
```python
import functools

import jax
import jax.numpy as jnp
from jax import lax
from jax.experimental import pallas as pl
from jax.experimental.pallas import tpu as pltpu
from jax.sharding import PartitionSpec as P

STEPS = 6
AXES = ("row", "col")
VMEM = pl.BlockSpec(memory_space=pltpu.VMEM)
SMEM = pl.BlockSpec(memory_space=pltpu.SMEM)
HBM = pl.BlockSpec(memory_space=pltpu.HBM)
ANY = pl.BlockSpec(memory_space=pl.ANY)
F32 = jnp.float32
BF16 = jnp.bfloat16
LIMIT = 40 * 1024 * 1024


def exact(left, right):
    return lax.dot_general(
        left, right, (((1,), (0,)), ((), ())), precision=lax.Precision.HIGHEST, preferred_element_type=F32
    )


def exact_rows(left, right):
    return lax.dot_general(
        left, right, (((1,), (1,)), ((), ())), precision=lax.Precision.HIGHEST, preferred_element_type=F32
    )


def rows(left, right):
    return lax.dot_general(left, right, (((1,), (1,)), ((), ())), preferred_element_type=F32)


def in_hbm(values):
    return pltpu.with_memory_space_constraint(values, pltpu.HBM)


def halves(values):
    high = values.astype(BF16)
    return high, (values - high.astype(F32)).astype(BF16)


def by_owner_kernel(mass, out, sems):
    wcap = out.shape[2]
    copies = [
        pltpu.make_async_copy(mass.at[:, pl.ds(c * wcap, wcap)], out.at[c], sems.at[c])
        for c in range(out.shape[0])
    ]
    for copy in copies:
        copy.start()
    for copy in copies:
        copy.wait()


def by_owner(mass, n_col, wcap):
    return pl.pallas_call(
        by_owner_kernel,
        in_specs=[HBM],
        out_specs=HBM,
        out_shape=pltpu.HBM((n_col, mass.shape[0], wcap), BF16),
        scratch_shapes=[pltpu.SemaphoreType.DMA((n_col,))],
        name="by_owner",
    )(mass)


def combine_kernel(rates, rim, wet, start, blocks, mixed, pick, place, halo):
    size = blocks.shape[-1]
    for k in range(blocks.shape[2]):
        whole = (
            blocks[0, 0, k].astype(F32)
            + rates[0] * blocks[1, 0, k].astype(F32)
            - rates[1] * blocks[2, 0, k].astype(F32)
        ).T
        high = whole.astype(BF16)
        mixed[0, k * size : (k + 1) * size, :size] = high
        mixed[0, k * size : (k + 1) * size, size:] = (whole - high.astype(F32)).astype(BF16)

    @pl.when(pl.program_id(0) == 0)
    def _():
        index = lax.broadcasted_iota(jnp.int32, pick.shape, 0)
        pick[...] = jnp.where(index == rim[...], 1.0, 0.0).astype(BF16)
        index = lax.broadcasted_iota(jnp.int32, place.shape, 1)
        place[...] = jnp.where(index == wet[...], 1.0, 0.0).astype(BF16)
        high, low = halves(start[...])
        halo[...] = jnp.dot(high, pick[...], preferred_element_type=F32) + jnp.dot(
            low, pick[...], preferred_element_type=F32
        )


def combine(rates, rim, wet, start, blocks):
    _, count, nnz, size, _ = blocks.shape
    vectors, width = start.shape
    whole = lambda shape: pl.BlockSpec(shape, lambda i: (0,) * len(shape))
    return pl.pallas_call(
        combine_kernel,
        grid=(count,),
        in_specs=[
            SMEM,
            whole(rim.shape),
            whole(wet.shape),
            whole(start.shape),
            pl.BlockSpec((3, 1, nnz, size, size), lambda i: (0, i, 0, 0, 0)),
        ],
        out_specs=[
            pl.BlockSpec((1, nnz * size, 2 * size), lambda i: (i, 0, 0)),
            whole((width, rim.shape[1])),
            whole((wet.shape[0], width)),
            whole((vectors, rim.shape[1])),
        ],
        out_shape=[
            pltpu.HBM((count, nnz * size, 2 * size), BF16),
            jax.ShapeDtypeStruct((width, rim.shape[1]), BF16),
            jax.ShapeDtypeStruct((wet.shape[0], width), BF16),
            jax.ShapeDtypeStruct((vectors, rim.shape[1]), F32),
        ],
        compiler_params=pltpu.CompilerParams(vmem_limit_bytes=LIMIT),
        name="combine",
    )(rates, rim, wet, start, blocks)


def live_slots(count, slots):
    slot = lax.broadcasted_iota(jnp.int32, slots.shape, 1)
    return jnp.where(slot < count[0], slots[...], -1)


def chosen(first, shape, live):
    index = lax.broadcasted_iota(jnp.int32, shape, 0) + first
    return jnp.where(index == live, 1.0, 0.0).astype(BF16)


def start_pressure_kernel(values, mass, part):
    n_col, n_row, _, half, wcap = mass.shape
    size, vectors = n_col * half, values.shape[0]
    for r in range(n_row):
        for h in range(2):
            own = mass[:, r, h].reshape(size, wcap)
            pressed = rows(own, values[...]).astype(BF16)
            part[r * size : (r + 1) * size, h * vectors : (h + 1) * vectors] = pressed


def start_pressure(values, mass, base):
    n_col, n_row, _, half, _ = mass.shape
    return pl.pallas_call(
        lambda values, mass, _base, part: start_pressure_kernel(values, mass, part),
        in_specs=[VMEM, VMEM, HBM],
        out_specs=VMEM,
        out_shape=jax.ShapeDtypeStruct((n_col * n_row * half, 2 * values.shape[0]), BF16),
        compiler_params=pltpu.CompilerParams(vmem_limit_bytes=LIMIT),
        name="start_pressure",
    )(values, mass, base)


def spread_kernel(count, slots, mass, spread, own):
    n_col, n_row, _, half, wcap = mass.shape
    size = n_col * half

    @pl.when(pl.program_id(0) == 0)
    def _():
        for h in range(2):
            for r in range(n_row):
                first = (h * n_row + r) * size
                own[first : first + size] = mass[:, r, h].reshape(size, wcap)

    columns = spread.shape[1]
    onehot = chosen(pl.program_id(0) * columns, (columns, wcap), live_slots(count, slots))
    spread[...] = rows(own[...], onehot).astype(BF16)


def spread_mass(count, slots, mass, width):
    n_col, n_row, _, half, wcap = mass.shape
    size = n_col * n_row * half
    columns = min(width, 512)
    return pl.pallas_call(
        spread_kernel,
        grid=(width // columns,),
        in_specs=[
            SMEM,
            pl.BlockSpec(slots.shape, lambda i: (0, 0)),
            pl.BlockSpec(mass.shape, lambda i: (0,) * 5),
        ],
        out_specs=pl.BlockSpec((2 * size, columns), lambda i: (0, i)),
        out_shape=pltpu.HBM((2 * size, width), BF16),
        scratch_shapes=[pltpu.VMEM((2 * size, wcap), BF16)],
        compiler_params=pltpu.CompilerParams(vmem_limit_bytes=LIMIT),
        cost_estimate=pl.CostEstimate(
            flops=4 * size * wcap * width, bytes_accessed=4 * size * width, transcendentals=0
        ),
        name="spread",
    )(count, slots, mass)


def halve_columns(top, low, s):
    a, b, c = top[:, s : s + 1], top[:, s + 1 : s + 2], low[:, s + 1 : s + 2]
    scale = 1.0 / (a * c - b * b)
    return (c * top - b * low) * scale, (a * low - b * top) * scale


def eliminate(matrix, beside, coef, factor_t):
    n = matrix.shape[0]
    groups = n // 8
    row_id = lax.broadcasted_iota(jnp.int32, (n, 2 * n), 0)
    lane_id = lax.broadcasted_iota(jnp.int32, (n, 2 * n), 1)
    factor_t[...] = jnp.where(row_id + n == lane_id, 1.0, 0.0)
    factor_t[:, :n] = matrix
    sub = lax.broadcasted_iota(jnp.int32, (8, 1), 0)
    if beside:
        work = [factor_t[g * 8 : (g + 1) * 8, :] for g in range(groups)]
        done = 0
        for j in range(0, n, 2):
            g, s = divmod(j, 8)
            new_top, new_low = halve_columns(work[g][s : s + 1, :], work[g][s + 1 : s + 2, :], j)
            for i in range(g, groups):
                left, right = work[i][:, j : j + 1], work[i][:, j + 1 : j + 2]
                if i == g:
                    left = jnp.where(sub > s + 1, left, 0.0)
                    right = jnp.where(sub > s + 1, right, 0.0)
                work[i] = work[i] - (left * new_top + right * new_low)
            goal = len(beside) * (j + 2) // n
            while done < goal:
                beside[done]()
                done += 1
        reduced = jnp.concatenate(work, 0)
    else:

        def group(step, _):
            work = [factor_t[g * 8 : (g + 1) * 8, :] for g in range(groups)]
            for s in range(0, 8, 2):
                new_top, new_low = halve_columns(work[0][s : s + 1, :], work[0][s + 1 : s + 2, :], s)
                for i in range(groups):
                    left, right = work[i][:, s : s + 1], work[i][:, s + 1 : s + 2]
                    keep = sub > s + 1 if i == 0 else step + i < groups
                    update = left * new_top + right * new_low
                    work[i] = work[i] - jnp.where(keep, update, 0.0)
            for i in range(groups):
                target = (i - 1) % groups
                factor_t[target * 8 : (target + 1) * 8, :] = pltpu.roll(work[i], 2 * n - 8, 1)
            return 0

        lax.fori_loop(0, groups, group, 0)
        reduced = pltpu.roll(factor_t[...], n, 1)
    above = pltpu.roll(reduced, 1, 0)
    odd = lax.broadcasted_iota(jnp.int32, (n, 1), 0) % 2 == 1
    pick = lambda values, where: jnp.sum(jnp.where(where, values, 0.0), 1, keepdims=True)
    under = pick(above, lane_id == row_id) / jnp.where(odd, pick(above, lane_id + 1 == row_id), 1.0)
    reduced = reduced - jnp.where(odd, under, 0.0) * above
    diagonal = pick(reduced, lane_id == row_id)
    scale = lax.rsqrt(diagonal)
    scale = scale * (1.5 - 0.5 * diagonal * scale * scale)
    reduced = reduced * scale
    factor_t[...] = reduced
    upper = jnp.where(row_id <= lane_id, reduced, 0.0)
    coef[2] = upper.T[:n, :]
    return factor_t[:, n:]


def congruent(factor, matrix):
    return exact(factor, exact_rows(matrix, factor))


def settle(total, gram, inner, lag, both, beside, coef, factor_t):
    n = gram.shape[0] // 2
    scale = 1.0 / total
    pull = lag[:, :n]
    aa = congruent(pull, gram[:n, :n] * scale)
    cc = congruent(pull, gram[n:, n:] * scale)
    self_ = both[:, :n]
    prev = both[:, n:]
    cp = inner[:, :n]
    pp = inner[:, n:]
    coef[0] = self_
    coef[1] = prev
    t_c = self_ - exact(self_, cc) - exact_rows(prev, cp)
    t_p = prev - exact(self_, cp) - exact(prev, pp)
    t_a = aa - exact_rows(self_, self_) - exact_rows(prev, prev)
    matrix = t_a - exact_rows(t_c, self_) - exact_rows(t_p, prev)
    inverse = eliminate(0.5 * (matrix + matrix.T), beside, coef, factor_t)
    return inverse, t_c, cc


def put_weights(weights, mix, pull):
    n = mix.shape[0]
    high, low = halves(mix)
    pull_high, pull_low = halves(pull)
    for k in range(3):
        cut = slice(k * n, (k + 1) * n)
        weights[:n, 2 * k * n : (2 * k + 1) * n] = high[:, cut]
        weights[:n, (2 * k + 1) * n : (2 * k + 2) * n] = high[:, cut]
        weights[n : 2 * n, 2 * k * n : (2 * k + 1) * n] = low[:, cut]
        weights[n : 2 * n, (2 * k + 1) * n : (2 * k + 2) * n] = jnp.zeros((n, n), BF16)
    if weights.shape[0] > 2 * n:
        weights[2 * n :, :] = jnp.zeros((2 * n, 6 * n), BF16)
        weights[2 * n : 3 * n, 2 * n : 3 * n] = pull_high
        weights[2 * n : 3 * n, 3 * n : 4 * n] = pull_high
        weights[3 * n :, 2 * n : 3 * n] = pull_low


def blend(total, gram, lag, both, mix):
    n = gram.shape[0] // 2
    scale = 1.0 / total
    pull, square = lag[:, :n], lag[:, n:]
    crossed = gram[:n, n:] * scale
    prev = exact(pull, gram[n:, :n] * scale)
    mix[:, :n] = pull
    mix[:, n : 2 * n] = -exact(pull, exact(crossed, square))
    mix[:, 2 * n :] = -prev
    both[:, :n] = congruent(pull, crossed)
    both[:, n:] = prev


def factor_kernel(total, gram, inner, lag, both, lag_out, inner_out, coef, factor_t):
    n = gram.shape[0] // 2
    inverse, t_c, cc = settle(total, gram, inner, lag, both, [], coef, factor_t)
    lag_out[:, :n] = inverse
    lag_out[:, n:] = exact(inverse.T, inverse)
    inner_out[:, :n] = exact(inverse, t_c)
    inner_out[:, n:] = cc


def factor(total, gram, inner, lag, both):
    n = gram.shape[0] // 2
    sds = jax.ShapeDtypeStruct
    return pl.pallas_call(
        functools.partial(factor_kernel, total),
        in_specs=[VMEM] * 4,
        out_specs=[VMEM] * 3,
        out_shape=[sds((n, 2 * n), F32), sds((n, 2 * n), F32), sds((3, n, n), F32)],
        scratch_shapes=[pltpu.VMEM((n, 2 * n), F32)],
        compiler_params=pltpu.CompilerParams(vmem_limit_bytes=LIMIT),
        cost_estimate=pl.CostEstimate(flops=100_000_000, bytes_accessed=10_000_000, transcendentals=0),
        name="factor",
    )(gram, inner, lag, both)


def thirds(values):
    high = values.astype(BF16)
    rest = values - high.astype(F32)
    return jnp.concatenate([high, *halves(rest)], 0)


def unpack(lines, received, target, lanes, offset):
    for s in range(received.shape[0]):
        if s * lines < target.shape[0]:
            target[s * lines : (s + 1) * lines, lanes] = received[s, offset : offset + lines]


def place_columns(extended, block, edge):
    size = extended.shape[2]
    count = extended.shape[0] - 2
    for i in range(count):
        extended[i] = block[:, i * size : (i + 1) * size]
    extended[count] = edge[:, :size].astype(BF16)
    extended[count + 1] = edge[:, size:].astype(BF16)


def block_row(ids, extended, mixed, i):
    picked = jnp.concatenate([extended[ids[i, k]] for k in range(ids.shape[1])], 1)
    pair = jnp.dot(picked, mixed[i], preferred_element_type=F32)
    size = pair.shape[1] // 2
    return pair[:, :size] + pair[:, size:]


def prepare_kernel(ids, count, slots, below, above, start, mixed, out, values, extended):
    size = below.shape[1]
    block = start[...].astype(BF16)
    place_columns(extended, block, jnp.concatenate([below[...], above[...]], 1))
    for i in range(out.shape[1] // size):
        out[:, i * size : (i + 1) * size] = block_row(ids, extended, mixed, i)
    live = live_slots(count, slots)
    columns = min(out.shape[1], 512)
    total = jnp.zeros(values.shape, F32)
    for first in range(0, out.shape[1], columns):
        picked = chosen(first, (columns, slots.shape[1]), live)
        total = total + jnp.dot(block[:, first : first + columns], picked, preferred_element_type=F32)
    values[...] = total.astype(BF16)


def prepare(ids, count, slots, below, above, start, mixed):
    vectors, width = start.shape
    size = below.shape[1]
    return pl.pallas_call(
        prepare_kernel,
        in_specs=[SMEM, SMEM] + [VMEM] * 5,
        out_specs=[VMEM] * 2,
        out_shape=[
            pltpu.HBM((vectors, width), F32),
            jax.ShapeDtypeStruct((vectors, slots.shape[1]), BF16),
        ],
        scratch_shapes=[pltpu.VMEM((width // size + 2, vectors, size), BF16)],
        compiler_params=pltpu.CompilerParams(vmem_limit_bytes=LIMIT),
        name="prepare",
    )(ids, count, slots, below, above, start, mixed)


def advance_kernel(mode, total, peers, *refs):
    it = iter(refs)
    take = lambda k: [next(it) for _ in range(k)]
    ids, rates = take(2)
    if mode == "first":
        arrived, below, above = take(3)
        held = take(2)
    else:
        received, pressed, lag, edges, wet_held = take(5)
        held = take(1)
    pick, place, mixed_in, spread_in = take(4)
    (state_out,) = take(1)
    if mode == "last":
        (gram_s,) = take(1)
    else:
        edges_out, wet_out, send = take(3)
    if mode != "first":
        both, gram_in = take(2)
    extended, terms, stack, mixed, spread, edge_in, sems = take(7)
    if mode != "last":
        gram_s, rest = take(2)
    if mode != "first":
        mix, weights = take(2)

    n = terms.shape[0] // 6
    width = terms.shape[1]
    size = edge_in.shape[1] // 2
    count = width // size
    glines = -(-2 * n // peers)
    hlines = -(-n // peers)
    loads = []
    for k, source in enumerate(held):
        target = stack.at[pl.ds(k * n, n)] if mode == "first" else stack
        loads.append(pltpu.make_async_copy(source, target, sems.at[k]))
        loads[-1].start()
    if mode != "first":
        load_mixed = pltpu.make_async_copy(mixed_in, mixed, sems.at[3])
        load_mixed.start()
    load_spread = []
    if mode != "last":
        for h in range(2):
            part = spread_in.at[pl.ds(h * spread.shape[1], spread.shape[1])]
            load_spread.append(pltpu.make_async_copy(part, spread.at[h], sems.at[4 + h]))
            load_spread[-1].start()

    if mode == "first":
        edge = jnp.concatenate([below[...], above[...]], 1)
        summed = jnp.sum(arrived[...].astype(F32), 0)
        wet = jnp.concatenate([summed[:, :n], summed[:, n:]], 0)
        edges_out[:n, :] = edge
        edges_out[n:, :] = jnp.zeros_like(edge)
        wet_out[:, :n] = wet
        wet_out[:, n:] = jnp.zeros_like(wet)
        for copy in loads:
            copy.wait()
        residual = stack[n : 2 * n, :]
        terms[4 * n :, :] = jnp.zeros((2 * n, width), BF16)
    else:
        unpack(glines, received, gram_in, slice(None), 0)
        unpack(hlines, received, edge_in.at[pl.ds(0, n)], slice(0, size), glines)
        unpack(hlines, received, edge_in.at[pl.ds(0, n)], slice(size, 2 * size), glines + hlines)
        edge_in[n:, :] = edges[...]
        blend(total, gram_in, lag, both, mix)
        pull = lag[:, :n]
        put_weights(weights, mix[...], pull)
        edge = exact(mix[...], edge_in[...])
        summed = pressed[...]
        wet = exact_rows(jnp.concatenate([summed[:, :n], summed[:, n:]], 0), pull)
        wet = wet + exact_rows(wet_held[...], mix[:, n:])
        if mode != "last":
            edges_out[:n, :] = edge
            edges_out[n:, :] = exact(pull, edges[:n, :])
            wet_out[:, :n] = wet
            wet_out[:, n:] = exact_rows(wet_held[:, :n], pull)
        for copy in loads:
            copy.wait()
        mixture = jnp.dot(weights[...], stack[...], preferred_element_type=F32)
        residual = mixture[:n] + mixture[n : 2 * n]
        terms[4 * n : 5 * n, :], terms[5 * n :, :] = halves(mixture[2 * n : 3 * n] + mixture[3 * n :])
    high, low = halves(residual)
    terms[2 * n : 3 * n, :] = high
    terms[3 * n : 4 * n, :] = low
    force = thirds(wet.T * rates[1])
    if mode != "first":
        place_columns(extended, high, edge)
        load_mixed.wait()
    for i in range(count):
        lanes = slice(i * size, (i + 1) * size)
        added = jnp.dot(force, place[:, lanes], preferred_element_type=F32)
        applied = stack[:n, lanes] if mode == "first" else block_row(ids, extended, mixed, i)
        applied = applied - (added[:n] + added[n : 2 * n] + added[2 * n :])
        terms[:n, lanes], terms[n : 2 * n, lanes] = halves(applied)
    store = pltpu.make_async_copy(terms, state_out, sems.at[2])
    store.start()

    known = 4 * n if mode == "first" else 6 * n
    products = rows(terms[: 2 * n, :], terms[:known, :])
    products = products[:n] + products[n:]
    gram_s[:n, :n] = products[:, :n] + products[:, n : 2 * n]
    gram_s[:n, n:] = products[:, 2 * n : 3 * n] + products[:, 3 * n : 4 * n]
    if mode == "first":
        gram_s[n:, :n] = jnp.zeros((n, n), F32)
    else:
        gram_s[n:, :n] = products[:, 4 * n : 5 * n] + products[:, 5 * n :]
    squares = rows(terms[2 * n : 4 * n, :], terms[2 * n : 4 * n, :])
    squares = squares[:n] + squares[n:]
    gram_s[n:, n:] = squares[:, :n] + squares[:, n:]
    if mode != "last":
        rim = jnp.dot(terms[: 2 * n, :], pick[...], preferred_element_type=F32)
        edge_in[:n, :size] = rim[:n] + rim[n:]
        wets = wet_out.shape[0] // 2
        for copy in load_spread:
            copy.wait()
        tops = rows(spread[0], terms[: 2 * n, :])
        tops = tops + pltpu.roll(tops, n, 1)
        ends = rows(spread[1], terms[: 2 * n, :])
        ends = ends + pltpu.roll(ends, n, 1)
        lane = lax.broadcasted_iota(jnp.int32, tops.shape, 1)
        send[:, :wets, :] = jnp.where(lane < n, tops, ends).astype(BF16).reshape(peers, wets, 2 * n)
        left = gram_s[...]
        offset = 0
        for _ in range(3):
            term = left.astype(BF16).astype(F32)
            left = left - term
            gram_s[...] = term
            for d in range(peers):
                if d * glines < 2 * n:
                    rest[d, offset : offset + glines] = gram_s[d * glines : (d + 1) * glines, :]
            offset += glines
        left = edge_in[:n, :size]
        for _ in range(2):
            term = left.astype(BF16).astype(F32)
            left = left - term
            edge_in[:n, :size] = term
            for d in range(peers):
                if d * hlines < n:
                    rest[d, offset : offset + hlines] = edge_in[d * hlines : (d + 1) * hlines, :size]
                else:
                    rest[d, offset : offset + hlines] = jnp.zeros((hlines, size), F32)
            offset += hlines
        if offset < rest.shape[1]:
            rest[:, offset:, :] = jnp.zeros((peers, rest.shape[1] - offset, 2 * n), F32)
        send[:, wets:, :] = rest[...].astype(BF16)
    store.wait()


def advance(mode, total, peers, ids, rates, state, fixed):
    mixed, pick, place, spread = fixed
    width, size = pick.shape
    wets = place.shape[0]
    vectors = state[3].shape[0] if mode == "first" else state[2].shape[0]
    extra = 3 * -(-2 * vectors // peers) + 2 * -(-vectors // peers)
    extra = -(-extra // 16) * 16
    sds = jax.ShapeDtypeStruct
    block = pltpu.HBM((6 * vectors, width), BF16)
    small = sds((2 * vectors, 2 * vectors), F32)
    shapes, specs = [block], [HBM]
    if mode == "last":
        shapes += [small]
        specs += [VMEM]
    else:
        shapes += [
            sds((2 * vectors, 2 * size), F32),
            sds((wets, 2 * vectors), F32),
            sds((peers, wets // 2 + extra, 2 * vectors), BF16),
        ]
        specs += [VMEM] * 3
    if mode != "first":
        shapes += [sds((vectors, 2 * vectors), F32), small]
        specs += [VMEM, VMEM]
    scratch = [
        pltpu.VMEM((width // size + 2, vectors, size), BF16),
        pltpu.VMEM((6 * vectors, width), BF16),
        pltpu.VMEM((2 * vectors, width), F32) if mode == "first" else pltpu.VMEM((6 * vectors, width), BF16),
        pltpu.VMEM(mixed.shape if mode != "first" else (16, 128), BF16),
        pltpu.VMEM((2, spread.shape[0] // 2, spread.shape[1]) if mode != "last" else (16, 128), BF16),
        pltpu.VMEM((3 * vectors, 2 * size), F32),
        pltpu.SemaphoreType.DMA((6,)),
    ]
    if mode != "last":
        scratch += [pltpu.VMEM(small.shape, F32), pltpu.VMEM((peers, extra, 2 * vectors), F32)]
    if mode != "first":
        scratch += [pltpu.VMEM((vectors, 3 * vectors), F32), pltpu.VMEM((4 * vectors, 6 * vectors), BF16)]
    held = 2 if mode == "first" else 1
    return pl.pallas_call(
        functools.partial(advance_kernel, mode, total, peers),
        in_specs=[SMEM, SMEM] + [VMEM] * (len(state) - held) + [HBM] * held + [VMEM, VMEM, HBM, HBM],
        out_specs=specs,
        out_shape=shapes,
        scratch_shapes=scratch,
        compiler_params=pltpu.CompilerParams(vmem_limit_bytes=LIMIT),
        name="advance_" + mode,
    )(ids, rates, *state, pick, place, mixed, spread)


def route_kernel(vectors, wets, received, _lag, pressed, send, rest):
    peers = received.shape[0]
    glines = -(-2 * vectors // peers)
    hlines = -(-vectors // peers)
    pressed[...] = jnp.sum(received[:, :wets, :].astype(F32), 0)
    rest[...] = received[:, wets:, :].astype(F32)
    sums = jnp.sum(rest[...], 0)
    mine = sums[:glines] + sums[glines : 2 * glines] + sums[2 * glines : 3 * glines]
    edge = 3 * glines
    nothing = jnp.zeros((hlines, 2 * vectors), F32)

    def halo(t):
        if not 0 <= t < peers:
            return nothing
        return rest[t, edge : edge + hlines] + rest[t, edge + hlines : edge + 2 * hlines]

    send[...] = jnp.zeros(send.shape, F32)
    for t in range(peers):
        send[t, :glines] = mine
        send[t, glines : glines + hlines] = halo(t - 1)
        send[t, glines + hlines : glines + 2 * hlines] = halo(t + 1)


def route(vectors, wets, received, lag):
    peers, lines, lanes = received.shape
    return pl.pallas_call(
        functools.partial(route_kernel, vectors, wets),
        in_specs=[VMEM, VMEM],
        out_specs=[VMEM] * 2,
        out_shape=[
            jax.ShapeDtypeStruct((wets, 2 * vectors), F32),
            jax.ShapeDtypeStruct((peers, 8, 2 * vectors), F32),
        ],
        scratch_shapes=[pltpu.VMEM((peers, lines - wets, lanes), F32)],
        compiler_params=pltpu.CompilerParams(vmem_limit_bytes=LIMIT),
        name="route",
    )(received, lag)


def repeat_sum_kernel(received, _lag, send):
    mine = jnp.sum(received[...], 0)
    for t in range(send.shape[0]):
        send[t] = mine


def repeat_sum(received, lag):
    return pl.pallas_call(
        repeat_sum_kernel,
        in_specs=[VMEM, VMEM],
        out_specs=VMEM,
        out_shape=jax.ShapeDtypeStruct(received.shape, F32),
        compiler_params=pltpu.CompilerParams(vmem_limit_bytes=LIMIT),
        name="repeat_sum",
    )(received, lag)


def finish_kernel(total, gram, inner, lag, state, *refs):
    *earlier, out, coefs, factor_t, mix, weights, both, stack, fresh, sem = refs
    coef = coefs.at[len(earlier)]
    n = inner.shape[0]
    load = pltpu.make_async_copy(state, stack, sem)
    load.start()
    blend(total, gram, lag, both, mix)
    for k, known in enumerate(earlier):
        coefs[k] = known[...]
    put_weights(weights, mix[...], lag[:, :n])
    load.wait()

    def next_residual():
        mixture = jnp.dot(weights[...], stack[...], preferred_element_type=F32)
        fresh[...] = mixture[:n] + mixture[n:]

    inverse, _, _ = settle(total, gram, inner, lag, both, [next_residual], coef, factor_t)
    out[...] = exact(inverse, fresh[...])


def finish(total, gram, inner, lag, state, earlier):
    vectors, width = lag.shape[0], state.shape[1]
    return pl.pallas_call(
        functools.partial(finish_kernel, total),
        in_specs=[VMEM] * 3 + [HBM] + [VMEM] * len(earlier),
        out_specs=[VMEM] * 2,
        out_shape=[
            pltpu.HBM((vectors, width), F32),
            pltpu.HBM((len(earlier) + 1, 3, vectors, vectors), F32),
        ],
        scratch_shapes=[
            pltpu.VMEM((vectors, 2 * vectors), F32),
            pltpu.VMEM((vectors, 3 * vectors), F32),
            pltpu.VMEM((2 * vectors, 6 * vectors), BF16),
            pltpu.VMEM((vectors, 2 * vectors), F32),
            pltpu.VMEM((6 * vectors, width), BF16),
            pltpu.VMEM((vectors, width), F32),
            pltpu.SemaphoreType.DMA,
        ],
        compiler_params=pltpu.CompilerParams(vmem_limit_bytes=LIMIT),
        name="finish",
    )(gram, inner, lag, state, *earlier)


def local(n_row, n_col, start_block, struct_blocks, block_ids, rim_rows, wet_slots, wet_counts, added_mass, rates):
    peers = n_row * n_col
    vectors, width = start_block.shape
    total = float(width * peers)
    wcap = wet_slots.shape[0]
    wets = added_mass.shape[0] // n_row

    def exchange(parts):
        return lax.all_to_all(parts, AXES, 0, 0, tiled=True)

    def neighbours(halo):
        up = [(i, i + 1) for i in range(peers - 1)]
        down = [(i + 1, i) for i in range(peers - 1)]
        return lax.ppermute(halo, AXES, up), lax.ppermute(halo, AXES, down)

    def summed(gram, lag):
        lines = gram.shape[0] // peers
        return exchange(repeat_sum(exchange(gram.reshape(peers, lines, -1)), lag)).reshape(gram.shape)

    blocks = by_owner(in_hbm(added_mass), n_col, wcap)
    mass = lax.all_to_all(blocks, "col", 0, 0, tiled=True)
    mass = mass.reshape(n_col, n_row, 2, wets // 2, wcap)
    mixed, pick, place, halo = combine(
        rates, rim_rows[None, :], wet_slots[:wets, None], start_block, struct_blocks
    )
    below, above = neighbours(halo)
    slots = wet_slots[None, :]
    base, values = prepare(block_ids, wet_counts, slots, below, above, start_block, mixed)
    base = in_hbm(base)
    part = start_pressure(values, mass, base)
    spread = spread_mass(wet_counts, slots, mass, width)
    fixed = (in_hbm(mixed), pick, place, in_hbm(spread))
    arrived = exchange(part.reshape(peers, wets // 2, 2 * vectors))
    step = functools.partial(advance, total=total, peers=peers, ids=block_ids, rates=rates, fixed=fixed)
    state, edges, wet_held, send = step("first", state=(arrived, below, above, base, in_hbm(start_block)))
    inner = jnp.zeros((vectors, 2 * vectors), F32)
    unit = jnp.eye(vectors, dtype=F32)
    lag = jnp.concatenate([unit, unit], 1)
    coefficients = []
    for number in range(1, STEPS):
        pressed, again = route(vectors, wets // 2, exchange(send), lag)
        received = exchange(again)
        known = (received, pressed, lag, edges, wet_held, in_hbm(state))
        if number < STEPS - 1:
            state, edges, wet_held, send, both, gram = step("mid", state=known)
        else:
            state, products, both, gram = step("last", state=known)
        lag, inner, coef = factor(total, gram, inner, lag, both)
        coefficients.append(coef)
    final, coefs = finish(total, summed(products, lag), inner, lag, in_hbm(state), coefficients)
    return final, coefs


def solution(mesh):
    return jax.shard_map(
        functools.partial(local, mesh.shape["row"], mesh.shape["col"]),
        mesh=mesh,
        in_specs=(
            P(None, AXES),
            P(None, AXES, None, None, None),
            P(AXES, None),
            P(AXES),
            P(AXES),
            P(AXES),
            P("col", "row"),
            P(),
        ),
        out_specs=(P(None, AXES), P()),
        check_vma=False,
    )
```

profile of v0, /device:TPU:0, one launch (start us, length us, event | category | flops | bytes accessed | tf_op | source)
XLA Modules:
  0.0 334.4 jit_solution(10544838582363556046)
XLA Ops:
  0.6 64.7 %by_owner.1 = bf16[8,128,1024]{2,1,0:T(8,128)(2,1)} custom-call(bf16[128,8192]{1,0:T(8,128)(2,1)} %mass.1), custom_call_target="tpu_custom_call" | custom-call | tf_op jit(solution)/shard_map/by_owner/pallas_call | solution.py:59
  65.3 0.0 copy-start.4
  65.4 0.0 copy-start.2
  65.4 0.0 copy-start.3
  65.4 0.0 copy-start.5
  65.4 7.4 %all-to-all-start = ((bf16[8,128,1024]{2,1,0:T(8,128)(2,1)}), bf16[8,128,1024]{2,1,0:T(8,128)(2,1)S(1)}, u32[]{:S(2)}, u32[]{:S(2)}) async-start(bf16[8,128,1024]{2,1,0:T(8,128)(2,1)} %by_owner.1), calls=%async_computation | async-start | bytes 4194304 | tf_op jit(solution)/shard_map/all_to_all | solution.py:712
  72.8 0.0 copy-done.4
  72.8 0.1 copy.10.wet
  72.9 0.0 copy-done.2
  72.9 0.0 copy-done.3
  72.9 0.0 copy-done.5
  72.9 0.0 copy-start.1
  72.9 2.8 copy-done.1
  75.7 0.0 copy-start.6
  75.7 8.2 %combine.1 = (bf16[16,512,256]{2,1,0:T(8,128)(2,1)}, bf16[2048,128]{1,0:T(8,128)(2,1)S(1)}, bf16[32,2048]{1,0:T(8,128)(2,1)S(1)}, f32[64,128]{1,0:T(8,128)S(1)}) custom-call(f32[2]{0:T(128)S(1)} %copy-done.3, s32[1,128]{1,0:T(1,128)S(1)} %bitcast.13, s32[32,1]{1,0:T(8,128)S(1)} %copy.10.wet, f32[64,2048]{1,0:T(8,128)S(1)} %copy-done.2, ...), custom_call_target="tpu_custom_call" | custom-call | tf_op jit(solution)/shard_map/combine/pallas_call | solution.py:97
  83.9 1.3 collective-permute-start.1
  85.2 4.5 %collective-permute-start = (f32[64,128]{1,0:T(8,128)S(1)}, f32[64,128]{1,0:T(8,128)S(1)}, u32[]{:S(2)}, u32[]{:S(2)}) collective-permute-start(f32[64,128]{1,0:T(8,128)S(1)} %get-tuple-element.65), channel_id=1, source_target_pairs={{0,1},{1,2},{2,3},{3,4},{4,5},{5,6},{6,7},{7,8},{8,9},{9,10},{10,1... | collective-permute-start | bytes 98312 | tf_op jit(solution)/shard_map/ppermute | solution.py:705
  90.4 0.0 copy-done.6
  90.4 0.1 copy.17.ids.refs_0_
  90.5 0.0 collective-permute-done.1.above.refs_4_
  90.5 0.9 collective-permute-done.below.refs_3_
  91.4 2.2 copy-done
  93.6 2.4 prepare.1
  95.9 25.4 %all-to-all-done = bf16[8,128,1024]{2,1,0:T(8,128)(2,1)S(1)} async-done(((bf16[8,128,1024]{2,1,0:T(8,128)(2,1)}), bf16[8,128,1024]{2,1,0:T(8,128)(2,1)S(1)}, u32[]{:S(2)}, u32[]{:S(2)}) %all-to-all-start) | async-done | bytes 2097184 | tf_op jit(solution)/shard_map/all_to_all | solution.py:712
  121.4 1.4 start_pressure.1
  122.8 7.7 %all-to-all-start.1 = ((bf16[32,16,128]{2,1,0:T(8,128)(2,1)}), bf16[32,16,128]{2,1,0:T(8,128)(2,1)S(1)}, u32[]{:S(2)}, u32[]{:S(2)}) async-start(bf16[32,16,128]{2,1,0:T(8,128)(2,1)} %bitcast.4), calls=%async_computation.1 | async-start | bytes 262144 | tf_op jit(solution)/shard_map/all_to_all | solution.py:700
  130.5 6.4 %spread.1.refs_10_.refs_11_ = bf16[1024,2048]{1,0:T(8,128)(2,1)} custom-call(s32[1]{0:T(128)S(6)} %copy.18.count, s32[1,1024]{1,0:T(1,128)S(1)} %bitcast.12, bf16[8,4,2,16,1024]{4,3,2,1,0:T(8,128)(2,1)S(1)} %bitcast.9), custom_call_target="tpu_custom_call" | custom-call | flops 4294967296 | bytes 4194304 | tf_op jit(solution)/shard_map/spread/pallas_call | solution.py:176
  137.0 1.3 all-to-all-done.1.refs_2_
  138.3 5.4 %advance_first.1 = (bf16[384,2048]{1,0:T(8,128)(2,1)}, f32[128,256]{1,0:T(8,128)S(1)}, f32[32,128]{1,0:T(8,128)S(1)}, bf16[32,32,128]{2,1,0:T(8,128)(2,1)}) custom-call(s32[16,4]{1,0:T(8,128)S(1)} %copy.17.ids.refs_0_, f32[2]{0:T(128)S(1)} %copy-done.3, bf16[32,16,128]{2,1,0:T(8,128)(2,1)S(1)} %all-to-all-done.1.refs_2_, ...), custom_call_target="tpu_custom_call" | custom-call | tf_op jit(solution)/shard_map/advance_first/pallas_call | solution.py:581
  143.7 4.6 %all-to-all-start.2 = ((bf16[32,32,128]{2,1,0:T(8,128)(2,1)}), bf16[32,32,128]{2,1,0:T(8,128)(2,1)S(1)}, u32[]{:S(2)}, u32[]{:S(2)}) async-start(bf16[32,32,128]{2,1,0:T(8,128)(2,1)} %get-tuple-element.71), calls=%async_computation.2 | async-start | bytes 524288 | tf_op jit(solution)/shard_map/all_to_all | solution.py:700
  148.2 0.1 add_convert_fusion._lag.refs_4_.lag
  148.3 10.6 %all-to-all-done.2.received = bf16[32,32,128]{2,1,0:T(8,128)(2,1)S(1)} async-done(((bf16[32,32,128]{2,1,0:T(8,128)(2,1)}), bf16[32,32,128]{2,1,0:T(8,128)(2,1)S(1)}, u32[]{:S(2)}, u32[]{:S(2)}) %all-to-all-start.2) | async-done | bytes 262176 | tf_op jit(solution)/shard_map/all_to_all | solution.py:700
  158.9 0.1 route.5
  158.9 9.9 %all_to_all.70.refs_2_ = f32[32,8,128]{2,1,0:T(8,128)S(1)} all-to-all(f32[32,8,128]{2,1,0:T(8,128)S(1)} %get-tuple-element.72), channel_id=1, replica_groups=mesh['row'=4,'col'=8] {'row','col'}, dimensions={0} | all-to-all | bytes 262144 | tf_op jit(solution)/shard_map/all_to_all | solution.py:700
  168.9 7.7 %advance_mid.4 = (bf16[384,2048]{1,0:T(8,128)(2,1)}, f32[128,256]{1,0:T(8,128)S(1)}, f32[32,128]{1,0:T(8,128)S(1)}, bf16[32,32,128]{2,1,0:T(8,128)(2,1)}, f32[64,128]{1,0:T(8,128)S(1)}, /*index=5*/f32[128,128]{1,0:T(8,128)S(1)}) custom-call(s32[16,4]{1,0:T(8,128)S(1)} %copy.17.ids.refs_0_, f32[2]{0:T(128)S(1)} %copy-done.3, ...), custom_call_target="tpu_custom_call" | custom-call | tf_op jit(solution)/shard_map/advance_mid/pallas_call | solution.py:581
  176.6 2.6 all-to-all-start.4
  179.2 7.6 %factor.5 = (f32[64,128]{1,0:T(8,128)S(1)}, f32[64,128]{1,0:T(8,128)S(1)}, f32[3,64,64]{2,1,0:T(8,128)S(1)}) custom-call(f32[128,128]{1,0:T(8,128)S(1)} %get-tuple-element.78.gram, f32[64,128]{1,0:T(8,128)S(1)} %broadcast_in_dim.15.inner, f32[64,128]{1,0:T(8,128)S(1)} %add_convert_fusion._lag.refs_4_.lag, f32[64,128]{1,0:T(8,128)S(1)} %get-tuple-element.79.both), custom_call_target="tpu_custom_call" | custom-call | flops 100000000 | bytes 10000000 | tf_op jit(solution)/shard_map/factor/pallas_call | solution.py:325
  186.9 3.0 all-to-all-done.4.received
  189.9 0.1 route.6
  189.9 10.4 %all_to_all.71.refs_2_ = f32[32,8,128]{2,1,0:T(8,128)S(1)} all-to-all(f32[32,8,128]{2,1,0:T(8,128)S(1)} %get-tuple-element.81), channel_id=1, replica_groups=mesh['row'=4,'col'=8] {'row','col'}, dimensions={0} | all-to-all | bytes 262144 | tf_op jit(solution)/shard_map/all_to_all | solution.py:700
  200.3 7.7 %advance_mid.5 = (bf16[384,2048]{1,0:T(8,128)(2,1)}, f32[128,256]{1,0:T(8,128)S(1)}, f32[32,128]{1,0:T(8,128)S(1)}, bf16[32,32,128]{2,1,0:T(8,128)(2,1)}, f32[64,128]{1,0:T(8,128)S(1)}, /*index=5*/f32[128,128]{1,0:T(8,128)S(1)}) custom-call(s32[16,4]{1,0:T(8,128)S(1)} %copy.17.ids.refs_0_, f32[2]{0:T(128)S(1)} %copy-done.3, ...), custom_call_target="tpu_custom_call" | custom-call | tf_op jit(solution)/shard_map/advance_mid/pallas_call | solution.py:581
  208.1 2.6 all-to-all-start.6
  210.7 7.6 %factor.6 = (f32[64,128]{1,0:T(8,128)S(1)}, f32[64,128]{1,0:T(8,128)S(1)}, f32[3,64,64]{2,1,0:T(8,128)S(1)}) custom-call(f32[128,128]{1,0:T(8,128)S(1)} %get-tuple-element.87.gram, f32[64,128]{1,0:T(8,128)S(1)} %get-tuple-element.88.inner, f32[64,128]{1,0:T(8,128)S(1)} %get-tuple-element.80._lag.refs_4_.lag, f32[64,128]{1,0:T(8,128)S(1)} %get-tuple-element.89.both), custom_call_target="tpu_custom_call" | custom-call | flops 100000000 | bytes 10000000 | tf_op jit(solution)/shard_map/factor/pallas_call | solution.py:325
  218.3 3.0 all-to-all-done.6.received
  221.3 0.1 route.7
  221.4 10.4 %all_to_all.72.refs_2_ = f32[32,8,128]{2,1,0:T(8,128)S(1)} all-to-all(f32[32,8,128]{2,1,0:T(8,128)S(1)} %get-tuple-element.91), channel_id=1, replica_groups=mesh['row'=4,'col'=8] {'row','col'}, dimensions={0} | all-to-all | bytes 262144 | tf_op jit(solution)/shard_map/all_to_all | solution.py:700
  231.8 7.7 %advance_mid.6 = (bf16[384,2048]{1,0:T(8,128)(2,1)}, f32[128,256]{1,0:T(8,128)S(1)}, f32[32,128]{1,0:T(8,128)S(1)}, bf16[32,32,128]{2,1,0:T(8,128)(2,1)}, f32[64,128]{1,0:T(8,128)S(1)}, /*index=5*/f32[128,128]{1,0:T(8,128)S(1)}) custom-call(s32[16,4]{1,0:T(8,128)S(1)} %copy.17.ids.refs_0_, f32[2]{0:T(128)S(1)} %copy-done.3, ...), custom_call_target="tpu_custom_call" | custom-call | tf_op jit(solution)/shard_map/advance_mid/pallas_call | solution.py:581
  239.5 2.6 all-to-all-start.8
  242.2 7.6 %factor.7 = (f32[64,128]{1,0:T(8,128)S(1)}, f32[64,128]{1,0:T(8,128)S(1)}, f32[3,64,64]{2,1,0:T(8,128)S(1)}) custom-call(f32[128,128]{1,0:T(8,128)S(1)} %get-tuple-element.97.gram, f32[64,128]{1,0:T(8,128)S(1)} %get-tuple-element.98.inner, f32[64,128]{1,0:T(8,128)S(1)} %get-tuple-element.90._lag.refs_4_.lag, f32[64,128]{1,0:T(8,128)S(1)} %get-tuple-element.99.both), custom_call_target="tpu_custom_call" | custom-call | flops 100000000 | bytes 10000000 | tf_op jit(solution)/shard_map/factor/pallas_call | solution.py:325
  249.8 3.0 all-to-all-done.8.received
  252.8 0.1 route.8
  252.9 10.4 %all_to_all.73.refs_2_ = f32[32,8,128]{2,1,0:T(8,128)S(1)} all-to-all(f32[32,8,128]{2,1,0:T(8,128)S(1)} %get-tuple-element.101), channel_id=1, replica_groups=mesh['row'=4,'col'=8] {'row','col'}, dimensions={0} | all-to-all | bytes 262144 | tf_op jit(solution)/shard_map/all_to_all | solution.py:700
  263.3 7.7 %advance_mid.7 = (bf16[384,2048]{1,0:T(8,128)(2,1)}, f32[128,256]{1,0:T(8,128)S(1)}, f32[32,128]{1,0:T(8,128)S(1)}, bf16[32,32,128]{2,1,0:T(8,128)(2,1)}, f32[64,128]{1,0:T(8,128)S(1)}, /*index=5*/f32[128,128]{1,0:T(8,128)S(1)}) custom-call(s32[16,4]{1,0:T(8,128)S(1)} %copy.17.ids.refs_0_, f32[2]{0:T(128)S(1)} %copy-done.3, ...), custom_call_target="tpu_custom_call" | custom-call | tf_op jit(solution)/shard_map/advance_mid/pallas_call | solution.py:581
  271.0 2.6 all-to-all-start.10
  273.6 7.6 %factor.8 = (f32[64,128]{1,0:T(8,128)S(1)}, f32[64,128]{1,0:T(8,128)S(1)}, f32[3,64,64]{2,1,0:T(8,128)S(1)}) custom-call(f32[128,128]{1,0:T(8,128)S(1)} %get-tuple-element.107.gram, f32[64,128]{1,0:T(8,128)S(1)} %get-tuple-element.108.inner, f32[64,128]{1,0:T(8,128)S(1)} %get-tuple-element.100._lag.refs_4_.lag, f32[64,128]{1,0:T(8,128)S(1)} %get-tuple-element.109.both), custom_call_target="tpu_custom_call" | custom-call | flops 100000000 | bytes 10000000 | tf_op jit(solution)/shard_map/factor/pallas_call | solution.py:325
  281.3 3.0 all-to-all-done.10.received
  284.3 0.1 route.9
  284.3 10.4 %all_to_all.74.refs_2_ = f32[32,8,128]{2,1,0:T(8,128)S(1)} all-to-all(f32[32,8,128]{2,1,0:T(8,128)S(1)} %get-tuple-element.111), channel_id=1, replica_groups=mesh['row'=4,'col'=8] {'row','col'}, dimensions={0} | all-to-all | bytes 262144 | tf_op jit(solution)/shard_map/all_to_all | solution.py:700
  294.7 6.9 %advance_last.1 = (bf16[384,2048]{1,0:T(8,128)(2,1)}, f32[128,128]{1,0:T(8,128)}, f32[64,128]{1,0:T(8,128)S(1)}, f32[128,128]{1,0:T(8,128)S(1)}) custom-call(s32[16,4]{1,0:T(8,128)S(1)} %copy.17.ids.refs_0_, f32[2]{0:T(128)S(1)} %copy-done.3, f32[32,8,128]{2,1,0:T(8,128)S(1)} %all_to_all.74.refs_2_, f32[16,128]{1,0:T(8,128)S(1)} %get-tuple-element.112.refs_3_, ...), custom_call_target="tpu_custom_call" | custom-call | tf_op jit(solution)/shard_map/advance_last/pallas_call | solution.py:581
  301.6 2.6 all-to-all-start.12
  304.2 7.6 %factor.9 = (f32[64,128]{1,0:T(8,128)S(1)}, f32[64,128]{1,0:T(8,128)S(1)}, f32[3,64,64]{2,1,0:T(8,128)S(1)}) custom-call(f32[128,128]{1,0:T(8,128)S(1)} %get-tuple-element.117.gram, f32[64,128]{1,0:T(8,128)S(1)} %get-tuple-element.118.inner, f32[64,128]{1,0:T(8,128)S(1)} %get-tuple-element.110._lag.refs_4_.lag, f32[64,128]{1,0:T(8,128)S(1)} %get-tuple-element.119.both), custom_call_target="tpu_custom_call" | custom-call | flops 100000000 | bytes 10000000 | tf_op jit(solution)/shard_map/factor/pallas_call | solution.py:325
  311.9 0.0 all-to-all-done.12.received
  311.9 12.9 %all_to_all.75 = f32[32,4,128]{2,1,0:T(4,128)S(1)} all-to-all(f32[32,4,128]{2,1,0:T(4,128)S(1)} %repeat_sum.1), channel_id=1, replica_groups=mesh['row'=4,'col'=8] {'row','col'}, dimensions={0} | all-to-all | bytes 131072 | tf_op jit(solution)/shard_map/all_to_all | solution.py:700
  324.9 9.3 %finish.1 = (f32[64,2048]{1,0:T(8,128)}, f32[6,3,64,64]{3,2,1,0:T(8,128)}) custom-call(f32[128,128]{1,0:T(8,128)S(1)} %bitcast.10, f32[64,128]{1,0:T(8,128)S(1)} %get-tuple-element.121.inner, f32[64,128]{1,0:T(8,128)S(1)} %get-tuple-element.120._lag.lag, bf16[384,2048]{1,0:T(8,128)(2,1)} %get-tuple-element.122.state, ...), custom_call_target="tpu_custom_call" | custom-call | tf_op jit(solution)/shard_map/finish/pallas_call | solution.py:670
  (5 shorter events, 0.1 us)
Async XLA Ops:
  65.3 7.4 %copy-start.4 = (s32[1024]{0:T(1024)S(1)}, s32[1024]{0:T(1024)}, u32[]{:S(2)}) copy-start(s32[1024]{0:T(1024)} %param.12) | copy-start | bytes 12292
  65.4 7.5 %copy-start.2 = (f32[64,2048]{1,0:T(8,128)S(1)}, f32[64,2048]{1,0:T(8,128)}, u32[]{:S(2)}) copy-start(f32[64,2048]{1,0:T(8,128)} %refs_6_.1) | copy-start | bytes 1572868
  65.4 7.5 %copy-start.3 = (f32[2]{0:T(128)S(1)}, f32[2]{0:T(128)}, u32[]{:S(2)}) copy-start(f32[2]{0:T(128)} %refs_1_.11) | copy-start | bytes 28
  65.4 7.5 %copy-start.5 = (s32[128]{0:T(128)S(1)}, s32[128]{0:T(128)}, u32[]{:S(2)}) copy-start(s32[128]{0:T(128)} %param.11) | copy-start | bytes 1540
  65.4 56.0 %all-to-all-start = ((bf16[8,128,1024]{2,1,0:T(8,128)(2,1)}), bf16[8,128,1024]{2,1,0:T(8,128)(2,1)S(1)}, u32[]{:S(2)}, u32[]{:S(2)}) async-start(bf16[8,128,1024]{2,1,0:T(8,128)(2,1)} %by_owner.1), calls=%async_computation | async-start | bytes 4194304 | tf_op jit(solution)/shard_map/all_to_all | solution.py:712
  72.9 2.8 copy-start.1
  75.7 14.7 %copy-start.6 = (s32[16,4]{0,1:T(4,128)S(1)}, s32[16,4]{0,1:T(4,128)}, u32[]{:S(2)}) copy-start(s32[16,4]{0,1:T(4,128)} %param.10) | copy-start | bytes 772
  83.9 6.6 %collective-permute-start.1 = (f32[64,128]{1,0:T(8,128)S(1)}, f32[64,128]{1,0:T(8,128)S(1)}, u32[]{:S(2)}, u32[]{:S(2)}) collective-permute-start(f32[64,128]{1,0:T(8,128)S(1)} %get-tuple-element.65), channel_id=1, source_target_pairs={{1,0},{2,1},{3,2},{4,3},{5,4},{6,5},{7,6},{8,7},{9,8},{10,9},{11,1... | collective-permute-start | bytes 98312 | tf_op jit(solution)/shard_map/ppermute | solution.py:705
  85.2 6.2 %collective-permute-start = (f32[64,128]{1,0:T(8,128)S(1)}, f32[64,128]{1,0:T(8,128)S(1)}, u32[]{:S(2)}, u32[]{:S(2)}) collective-permute-start(f32[64,128]{1,0:T(8,128)S(1)} %get-tuple-element.65), channel_id=1, source_target_pairs={{0,1},{1,2},{2,3},{3,4},{4,5},{5,6},{6,7},{7,8},{8,9},{9,10},{10,1... | collective-permute-start | bytes 98312 | tf_op jit(solution)/shard_map/ppermute | solution.py:705
  91.4 2.2 copy-start
  122.8 15.5 %all-to-all-start.1 = ((bf16[32,16,128]{2,1,0:T(8,128)(2,1)}), bf16[32,16,128]{2,1,0:T(8,128)(2,1)S(1)}, u32[]{:S(2)}, u32[]{:S(2)}) async-start(bf16[32,16,128]{2,1,0:T(8,128)(2,1)} %bitcast.4), calls=%async_computation.1 | async-start | bytes 262144 | tf_op jit(solution)/shard_map/all_to_all | solution.py:700
  143.7 15.2 %all-to-all-start.2 = ((bf16[32,32,128]{2,1,0:T(8,128)(2,1)}), bf16[32,32,128]{2,1,0:T(8,128)(2,1)S(1)}, u32[]{:S(2)}, u32[]{:S(2)}) async-start(bf16[32,32,128]{2,1,0:T(8,128)(2,1)} %get-tuple-element.71), calls=%async_computation.2 | async-start | bytes 524288 | tf_op jit(solution)/shard_map/all_to_all | solution.py:700
  176.6 13.3 %all-to-all-start.4 = ((bf16[32,32,128]{2,1,0:T(8,128)(2,1)}), bf16[32,32,128]{2,1,0:T(8,128)(2,1)S(1)}, u32[]{:S(2)}, u32[]{:S(2)}) async-start(bf16[32,32,128]{2,1,0:T(8,128)(2,1)} %get-tuple-element.77), calls=%async_computation.4 | async-start | bytes 524288 | tf_op jit(solution)/shard_map/all_to_all | solution.py:700
  208.1 13.3 %all-to-all-start.6 = ((bf16[32,32,128]{2,1,0:T(8,128)(2,1)}), bf16[32,32,128]{2,1,0:T(8,128)(2,1)S(1)}, u32[]{:S(2)}, u32[]{:S(2)}) async-start(bf16[32,32,128]{2,1,0:T(8,128)(2,1)} %get-tuple-element.86), calls=%async_computation.6 | async-start | bytes 524288 | tf_op jit(solution)/shard_map/all_to_all | solution.py:700
  239.5 13.3 %all-to-all-start.8 = ((bf16[32,32,128]{2,1,0:T(8,128)(2,1)}), bf16[32,32,128]{2,1,0:T(8,128)(2,1)S(1)}, u32[]{:S(2)}, u32[]{:S(2)}) async-start(bf16[32,32,128]{2,1,0:T(8,128)(2,1)} %get-tuple-element.96), calls=%async_computation.8 | async-start | bytes 524288 | tf_op jit(solution)/shard_map/all_to_all | solution.py:700
  271.0 13.3 %all-to-all-start.10 = ((bf16[32,32,128]{2,1,0:T(8,128)(2,1)}), bf16[32,32,128]{2,1,0:T(8,128)(2,1)S(1)}, u32[]{:S(2)}, u32[]{:S(2)}) async-start(bf16[32,32,128]{2,1,0:T(8,128)(2,1)} %get-tuple-element.106), calls=%async_computation.10 | async-start | bytes 524288 | tf_op jit(solution)/shard_map/all_to_all | solution.py:700
  301.6 10.2 %all-to-all-start.12 = ((f32[32,4,128]{2,1,0:T(4,128)}), f32[32,4,128]{2,1,0:T(4,128)S(1)}, u32[]{:S(2)}, u32[]{:S(2)}) async-start(f32[32,4,128]{2,1,0:T(4,128)} %bitcast.5), calls=%async_computation.12 | async-start | bytes 131072 | tf_op jit(solution)/shard_map/all_to_all | solution.py:700
where the time goes:
time: 335 us; the launch traced here: 334 us
  Pallas kernels  174 us (52%)
  blocking collectives  64.4 us (19%)
  waiting for transfers between devices  50.2 us (15%)
  starting transfers between devices  38.5 us (11%)
  local copies, waits for them, and re-layouts  5.17 us (2%)
    pallas_call x1, Pallas kernels, by_owner(): pl.pallas_call(by_owner_kernel, in_specs=[HBM], out_specs=HBM, out_shape=...  64.7 us
    all_to_all x6, blocking collectives, exchange(): return lax.all_to_all(parts, AXES, 0, 0, tiled=True)  64.4 us
    pallas_call x6, Pallas kernels, advance(): pl.pallas_call(functools.partial(advance_kernel, mode, total, peers), in_...  43.2 us
    pallas_call x5, Pallas kernels, factor(): pl.pallas_call(functools.partial(factor_kernel, total), in_specs=[VMEM] *...  38.2 us
    all_to_all x1, waiting for transfers between devices, local(): mass = lax.all_to_all(blocks, 'col', 0, 0, tiled=True)  25.4 us
    all_to_all x7, starting transfers between devices, exchange(): return lax.all_to_all(parts, AXES, 0, 0, tiled=True)  25.3 us
    all_to_all x7, waiting for transfers between devices, exchange(): return lax.all_to_all(parts, AXES, 0, 0, tiled=True)  23.9 us
    pallas_call x1, Pallas kernels, finish(): pl.pallas_call(functools.partial(finish_kernel, total), in_specs=[VMEM] *...  9.32 us
  transfers between devices with their start and end apart: 10, of which 8 were waited for; matrix products, arithmetic and copies ran while one was open for 0% of the time, Pallas kernels for 17%

commit v1 on v0

--- a/solution.py
+++ b/solution.py
@@ -43,25 +43,19 @@
     return high, (values - high.astype(F32)).astype(BF16)
 
 
-def by_owner_kernel(mass, out, sems):
-    wcap = out.shape[2]
-    copies = [
-        pltpu.make_async_copy(mass.at[:, pl.ds(c * wcap, wcap)], out.at[c], sems.at[c])
-        for c in range(out.shape[0])
-    ]
-    for copy in copies:
-        copy.start()
-    for copy in copies:
-        copy.wait()
+def by_owner_kernel(mass, out):
+    out[0] = mass[...]
 
 
 def by_owner(mass, n_col, wcap):
+    size = mass.shape[0]
     return pl.pallas_call(
         by_owner_kernel,
-        in_specs=[HBM],
-        out_specs=HBM,
-        out_shape=pltpu.HBM((n_col, mass.shape[0], wcap), BF16),
-        scratch_shapes=[pltpu.SemaphoreType.DMA((n_col,))],
+        grid=(n_col,),
+        in_specs=[pl.BlockSpec((size, wcap), lambda c: (0, c))],
+        out_specs=pl.BlockSpec((1, size, wcap), lambda c: (c, 0, 0)),
+        out_shape=jax.ShapeDtypeStruct((n_col, size, wcap), BF16),
+        compiler_params=pltpu.CompilerParams(vmem_limit_bytes=LIMIT),
         name="by_owner",
     )(mass)
 
@@ -708,7 +702,7 @@
         lines = gram.shape[0] // peers
         return exchange(repeat_sum(exchange(gram.reshape(peers, lines, -1)), lag)).reshape(gram.shape)
 
-    blocks = by_owner(in_hbm(added_mass), n_col, wcap)
+    blocks = by_owner(added_mass, n_col, wcap)
     mass = lax.all_to_all(blocks, "col", 0, 0, tiled=True)
     mass = mass.reshape(n_col, n_row, 2, wets // 2, wcap)
     mixed, pick, place, halo = combine(

time: 335 us -> 274 us (0.82)
  Pallas kernels: 174 us -> 110 us
    pallas_call x1, Pallas kernels: 64.7 us -> 0.44 us  [by_owner(): pl.pallas_call(by_owner_kernel, grid=(n_col,), in_specs=[pl.BlockSpec((si...]
    unnamed x15 -> x19, local copies, waits for them, and re-layouts: 5.08 us -> 8.03 us
  transfers between devices with their start and end apart: 10 -> 10, of which waited for: 8 -> 8; matrix products, arithmetic and copies ran while one was open for 0% -> 0% of each run, Pallas kernels for 17% -> 20%
where the time goes in v1:
time: 274 us; the launch traced here: 273 us
  Pallas kernels  110 us (40%)
  blocking collectives  64.4 us (24%)
  waiting for transfers between devices  50.1 us (18%)
  starting transfers between devices  38.5 us (14%)
  local copies, waits for them, and re-layouts  8.12 us (3%)
    all_to_all x6, blocking collectives, exchange(): return lax.all_to_all(parts, AXES, 0, 0, tiled=True)  64.4 us
    pallas_call x6, Pallas kernels, advance(): pl.pallas_call(functools.partial(advance_kernel, mode, total, peers), in_...  43.1 us
    pallas_call x5, Pallas kernels, factor(): pl.pallas_call(functools.partial(factor_kernel, total), in_specs=[VMEM] *...  38.2 us
    all_to_all x1, waiting for transfers between devices, local(): mass = lax.all_to_all(blocks, 'col', 0, 0, tiled=True)  25.4 us
    all_to_all x7, starting transfers between devices, exchange(): return lax.all_to_all(parts, AXES, 0, 0, tiled=True)  25.3 us
    all_to_all x7, waiting for transfers between devices, exchange(): return lax.all_to_all(parts, AXES, 0, 0, tiled=True)  23.9 us
    pallas_call x1, Pallas kernels, finish(): pl.pallas_call(functools.partial(finish_kernel, total), in_specs=[VMEM] *...  9.32 us
    pallas_call x1, Pallas kernels, combine(): pl.pallas_call(combine_kernel, grid=(count,), in_specs=[SMEM, whole(rim.s...  8.28 us
  transfers between devices with their start and end apart: 10, of which 8 were waited for; matrix products, arithmetic and copies ran while one was open for 0% of the time, Pallas kernels for 20%

profile of v1, /device:TPU:0, one launch (start us, length us, event | category | flops | bytes accessed | tf_op | source)
XLA Modules:
  0.0 273.0 jit_solution(17352839267329131688)
XLA Ops:
  0.6 0.0 copy-start.4
  0.6 1.6 copy-done.4
  2.2 0.4 by_owner.1
  2.7 0.0 copy-start.1
  2.7 1.4 copy-done.1
  4.0 0.0 copy-start.6
  4.1 7.4 %all-to-all-start = ((bf16[8,128,1024]{2,1,0:T(8,128)(2,1)}), bf16[8,128,1024]{2,1,0:T(8,128)(2,1)S(1)}, u32[]{:S(2)}, u32[]{:S(2)}) async-start(bf16[8,128,1024]{2,1,0:T(8,128)(2,1)} %copy-done.1), calls=%async_computation | async-start | bytes 4194304 | tf_op jit(solution)/shard_map/all_to_all | solution.py:706
  11.5 0.0 copy-done.6
  11.5 0.1 copy.10.wet
  11.6 0.0 copy-done.3
  11.6 0.0 copy-done.5
  11.6 0.0 copy-done.7
  11.6 0.0 copy-start.2
  11.6 2.8 %copy-done.2 = bf16[3,16,4,128,128]{4,3,2,1,0:T(8,128)(2,1)S(1)} copy-done((bf16[3,16,4,128,128]{4,3,2,1,0:T(8,128)(2,1)S(1)}, bf16[3,16,4,128,128]{4,3,2,1,0:T(8,128)(2,1)}, u32[]{:S(2)}) %copy-start.2) | copy-done | bytes 6291480
  14.4 8.3 %combine.1 = (bf16[16,512,256]{2,1,0:T(8,128)(2,1)}, bf16[2048,128]{1,0:T(8,128)(2,1)S(1)}, bf16[32,2048]{1,0:T(8,128)(2,1)S(1)}, f32[64,128]{1,0:T(8,128)S(1)}) custom-call(f32[2]{0:T(128)S(1)} %copy-done.5, s32[1,128]{1,0:T(1,128)S(1)} %bitcast.13, s32[32,1]{1,0:T(8,128)S(1)} %copy.10.wet, f32[64,2048]{1,0:T(8,128)S(1)} %copy-done.3, ...), custom_call_target="tpu_custom_call" | custom-call | tf_op jit(solution)/shard_map/combine/pallas_call | solution.py:91
  22.6 1.3 collective-permute-start.1
  23.9 4.5 %collective-permute-start = (f32[64,128]{1,0:T(8,128)S(1)}, f32[64,128]{1,0:T(8,128)S(1)}, u32[]{:S(2)}, u32[]{:S(2)}) collective-permute-start(f32[64,128]{1,0:T(8,128)S(1)} %get-tuple-element.65), channel_id=1, source_target_pairs={{0,1},{1,2},{2,3},{3,4},{4,5},{5,6},{6,7},{7,8},{8,9},{9,10},{10,1... | collective-permute-start | bytes 98312 | tf_op jit(solution)/shard_map/ppermute | solution.py:699
  29.1 0.0 copy-done.8
  29.1 0.1 copy.17.ids.refs_0_
  29.2 0.0 collective-permute-done.1.above.refs_4_
  29.2 0.9 collective-permute-done.below.refs_3_
  30.1 2.2 copy-done
  32.3 2.4 prepare.1
  34.7 25.4 %all-to-all-done = bf16[8,128,1024]{2,1,0:T(8,128)(2,1)S(1)} async-done(((bf16[8,128,1024]{2,1,0:T(8,128)(2,1)}), bf16[8,128,1024]{2,1,0:T(8,128)(2,1)S(1)}, u32[]{:S(2)}, u32[]{:S(2)}) %all-to-all-start) | async-done | bytes 2097184 | tf_op jit(solution)/shard_map/all_to_all | solution.py:706
  60.0 1.4 start_pressure.1
  61.5 7.7 %all-to-all-start.1 = ((bf16[32,16,128]{2,1,0:T(8,128)(2,1)}), bf16[32,16,128]{2,1,0:T(8,128)(2,1)S(1)}, u32[]{:S(2)}, u32[]{:S(2)}) async-start(bf16[32,16,128]{2,1,0:T(8,128)(2,1)} %bitcast.4), calls=%async_computation.1 | async-start | bytes 262144 | tf_op jit(solution)/shard_map/all_to_all | solution.py:694
  69.2 6.4 %spread.1.refs_10_.refs_11_ = bf16[1024,2048]{1,0:T(8,128)(2,1)} custom-call(s32[1]{0:T(128)S(6)} %copy.18.count, s32[1,1024]{1,0:T(1,128)S(1)} %bitcast.12, bf16[8,4,2,16,1024]{4,3,2,1,0:T(8,128)(2,1)S(1)} %bitcast.9), custom_call_target="tpu_custom_call" | custom-call | flops 4294967296 | bytes 4194304 | tf_op jit(solution)/shard_map/spread/pallas_call | solution.py:170
  75.7 1.3 all-to-all-done.1.refs_2_
  77.0 5.4 %advance_first.1 = (bf16[384,2048]{1,0:T(8,128)(2,1)}, f32[128,256]{1,0:T(8,128)S(1)}, f32[32,128]{1,0:T(8,128)S(1)}, bf16[32,32,128]{2,1,0:T(8,128)(2,1)}) custom-call(s32[16,4]{1,0:T(8,128)S(1)} %copy.17.ids.refs_0_, f32[2]{0:T(128)S(1)} %copy-done.5, bf16[32,16,128]{2,1,0:T(8,128)(2,1)S(1)} %all-to-all-done.1.refs_2_, ...), custom_call_target="tpu_custom_call" | custom-call | tf_op jit(solution)/shard_map/advance_first/pallas_call | solution.py:575
  82.3 4.5 %all-to-all-start.2 = ((bf16[32,32,128]{2,1,0:T(8,128)(2,1)}), bf16[32,32,128]{2,1,0:T(8,128)(2,1)S(1)}, u32[]{:S(2)}, u32[]{:S(2)}) async-start(bf16[32,32,128]{2,1,0:T(8,128)(2,1)} %get-tuple-element.71), calls=%async_computation.2 | async-start | bytes 524288 | tf_op jit(solution)/shard_map/all_to_all | solution.py:694
  86.9 0.1 add_convert_fusion._lag.refs_4_.lag
  87.0 10.6 %all-to-all-done.2.received = bf16[32,32,128]{2,1,0:T(8,128)(2,1)S(1)} async-done(((bf16[32,32,128]{2,1,0:T(8,128)(2,1)}), bf16[32,32,128]{2,1,0:T(8,128)(2,1)S(1)}, u32[]{:S(2)}, u32[]{:S(2)}) %all-to-all-start.2) | async-done | bytes 262176 | tf_op jit(solution)/shard_map/all_to_all | solution.py:694
  97.6 0.1 route.5
  97.6 9.9 %all_to_all.70.refs_2_ = f32[32,8,128]{2,1,0:T(8,128)S(1)} all-to-all(f32[32,8,128]{2,1,0:T(8,128)S(1)} %get-tuple-element.72), channel_id=1, replica_groups=mesh['row'=4,'col'=8] {'row','col'}, dimensions={0} | all-to-all | bytes 262144 | tf_op jit(solution)/shard_map/all_to_all | solution.py:694
  107.5 7.7 %advance_mid.4 = (bf16[384,2048]{1,0:T(8,128)(2,1)}, f32[128,256]{1,0:T(8,128)S(1)}, f32[32,128]{1,0:T(8,128)S(1)}, bf16[32,32,128]{2,1,0:T(8,128)(2,1)}, f32[64,128]{1,0:T(8,128)S(1)}, /*index=5*/f32[128,128]{1,0:T(8,128)S(1)}) custom-call(s32[16,4]{1,0:T(8,128)S(1)} %copy.17.ids.refs_0_, f32[2]{0:T(128)S(1)} %copy-done.5, ...), custom_call_target="tpu_custom_call" | custom-call | tf_op jit(solution)/shard_map/advance_mid/pallas_call | solution.py:575
  115.3 2.6 all-to-all-start.4
  117.9 7.6 %factor.5 = (f32[64,128]{1,0:T(8,128)S(1)}, f32[64,128]{1,0:T(8,128)S(1)}, f32[3,64,64]{2,1,0:T(8,128)S(1)}) custom-call(f32[128,128]{1,0:T(8,128)S(1)} %get-tuple-element.78.gram, f32[64,128]{1,0:T(8,128)S(1)} %broadcast_in_dim.15.inner, f32[64,128]{1,0:T(8,128)S(1)} %add_convert_fusion._lag.refs_4_.lag, f32[64,128]{1,0:T(8,128)S(1)} %get-tuple-element.79.both), custom_call_target="tpu_custom_call" | custom-call | flops 100000000 | bytes 10000000 | tf_op jit(solution)/shard_map/factor/pallas_call | solution.py:319
  125.5 3.0 %all-to-all-done.4.received = bf16[32,32,128]{2,1,0:T(8,128)(2,1)S(1)} async-done(((bf16[32,32,128]{2,1,0:T(8,128)(2,1)}), bf16[32,32,128]{2,1,0:T(8,128)(2,1)S(1)}, u32[]{:S(2)}, u32[]{:S(2)}) %all-to-all-start.4) | async-done | bytes 262176 | tf_op jit(solution)/shard_map/all_to_all | solution.py:694
  128.5 0.1 route.6
  128.6 10.4 %all_to_all.71.refs_2_ = f32[32,8,128]{2,1,0:T(8,128)S(1)} all-to-all(f32[32,8,128]{2,1,0:T(8,128)S(1)} %get-tuple-element.81), channel_id=1, replica_groups=mesh['row'=4,'col'=8] {'row','col'}, dimensions={0} | all-to-all | bytes 262144 | tf_op jit(solution)/shard_map/all_to_all | solution.py:694
  139.0 7.7 %advance_mid.5 = (bf16[384,2048]{1,0:T(8,128)(2,1)}, f32[128,256]{1,0:T(8,128)S(1)}, f32[32,128]{1,0:T(8,128)S(1)}, bf16[32,32,128]{2,1,0:T(8,128)(2,1)}, f32[64,128]{1,0:T(8,128)S(1)}, /*index=5*/f32[128,128]{1,0:T(8,128)S(1)}) custom-call(s32[16,4]{1,0:T(8,128)S(1)} %copy.17.ids.refs_0_, f32[2]{0:T(128)S(1)} %copy-done.5, ...), custom_call_target="tpu_custom_call" | custom-call | tf_op jit(solution)/shard_map/advance_mid/pallas_call | solution.py:575
  146.7 2.6 all-to-all-start.6
  149.3 7.6 %factor.6 = (f32[64,128]{1,0:T(8,128)S(1)}, f32[64,128]{1,0:T(8,128)S(1)}, f32[3,64,64]{2,1,0:T(8,128)S(1)}) custom-call(f32[128,128]{1,0:T(8,128)S(1)} %get-tuple-element.87.gram, f32[64,128]{1,0:T(8,128)S(1)} %get-tuple-element.88.inner, f32[64,128]{1,0:T(8,128)S(1)} %get-tuple-element.80._lag.refs_4_.lag, f32[64,128]{1,0:T(8,128)S(1)} %get-tuple-element.89.both), custom_call_target="tpu_custom_call" | custom-call | flops 100000000 | bytes 10000000 | tf_op jit(solution)/shard_map/factor/pallas_call | solution.py:319
  157.0 3.0 %all-to-all-done.6.received = bf16[32,32,128]{2,1,0:T(8,128)(2,1)S(1)} async-done(((bf16[32,32,128]{2,1,0:T(8,128)(2,1)}), bf16[32,32,128]{2,1,0:T(8,128)(2,1)S(1)}, u32[]{:S(2)}, u32[]{:S(2)}) %all-to-all-start.6) | async-done | bytes 262176 | tf_op jit(solution)/shard_map/all_to_all | solution.py:694
  160.0 0.1 route.7
  160.1 10.4 %all_to_all.72.refs_2_ = f32[32,8,128]{2,1,0:T(8,128)S(1)} all-to-all(f32[32,8,128]{2,1,0:T(8,128)S(1)} %get-tuple-element.91), channel_id=1, replica_groups=mesh['row'=4,'col'=8] {'row','col'}, dimensions={0} | all-to-all | bytes 262144 | tf_op jit(solution)/shard_map/all_to_all | solution.py:694
  170.5 7.7 %advance_mid.6 = (bf16[384,2048]{1,0:T(8,128)(2,1)}, f32[128,256]{1,0:T(8,128)S(1)}, f32[32,128]{1,0:T(8,128)S(1)}, bf16[32,32,128]{2,1,0:T(8,128)(2,1)}, f32[64,128]{1,0:T(8,128)S(1)}, /*index=5*/f32[128,128]{1,0:T(8,128)S(1)}) custom-call(s32[16,4]{1,0:T(8,128)S(1)} %copy.17.ids.refs_0_, f32[2]{0:T(128)S(1)} %copy-done.5, ...), custom_call_target="tpu_custom_call" | custom-call | tf_op jit(solution)/shard_map/advance_mid/pallas_call | solution.py:575
  178.2 2.6 all-to-all-start.8
  180.8 7.6 %factor.7 = (f32[64,128]{1,0:T(8,128)S(1)}, f32[64,128]{1,0:T(8,128)S(1)}, f32[3,64,64]{2,1,0:T(8,128)S(1)}) custom-call(f32[128,128]{1,0:T(8,128)S(1)} %get-tuple-element.97.gram, f32[64,128]{1,0:T(8,128)S(1)} %get-tuple-element.98.inner, f32[64,128]{1,0:T(8,128)S(1)} %get-tuple-element.90._lag.refs_4_.lag, f32[64,128]{1,0:T(8,128)S(1)} %get-tuple-element.99.both), custom_call_target="tpu_custom_call" | custom-call | flops 100000000 | bytes 10000000 | tf_op jit(solution)/shard_map/factor/pallas_call | solution.py:319
  188.4 3.0 %all-to-all-done.8.received = bf16[32,32,128]{2,1,0:T(8,128)(2,1)S(1)} async-done(((bf16[32,32,128]{2,1,0:T(8,128)(2,1)}), bf16[32,32,128]{2,1,0:T(8,128)(2,1)S(1)}, u32[]{:S(2)}, u32[]{:S(2)}) %all-to-all-start.8) | async-done | bytes 262176 | tf_op jit(solution)/shard_map/all_to_all | solution.py:694
  191.4 0.1 route.8
  191.5 10.4 %all_to_all.73.refs_2_ = f32[32,8,128]{2,1,0:T(8,128)S(1)} all-to-all(f32[32,8,128]{2,1,0:T(8,128)S(1)} %get-tuple-element.101), channel_id=1, replica_groups=mesh['row'=4,'col'=8] {'row','col'}, dimensions={0} | all-to-all | bytes 262144 | tf_op jit(solution)/shard_map/all_to_all | solution.py:694
  201.9 7.7 %advance_mid.7 = (bf16[384,2048]{1,0:T(8,128)(2,1)}, f32[128,256]{1,0:T(8,128)S(1)}, f32[32,128]{1,0:T(8,128)S(1)}, bf16[32,32,128]{2,1,0:T(8,128)(2,1)}, f32[64,128]{1,0:T(8,128)S(1)}, /*index=5*/f32[128,128]{1,0:T(8,128)S(1)}) custom-call(s32[16,4]{1,0:T(8,128)S(1)} %copy.17.ids.refs_0_, f32[2]{0:T(128)S(1)} %copy-done.5, ...), custom_call_target="tpu_custom_call" | custom-call | tf_op jit(solution)/shard_map/advance_mid/pallas_call | solution.py:575
  209.6 2.6 all-to-all-start.10
  212.2 7.6 %factor.8 = (f32[64,128]{1,0:T(8,128)S(1)}, f32[64,128]{1,0:T(8,128)S(1)}, f32[3,64,64]{2,1,0:T(8,128)S(1)}) custom-call(f32[128,128]{1,0:T(8,128)S(1)} %get-tuple-element.107.gram, f32[64,128]{1,0:T(8,128)S(1)} %get-tuple-element.108.inner, f32[64,128]{1,0:T(8,128)S(1)} %get-tuple-element.100._lag.refs_4_.lag, f32[64,128]{1,0:T(8,128)S(1)} %get-tuple-element.109.both), custom_call_target="tpu_custom_call" | custom-call | flops 100000000 | bytes 10000000 | tf_op jit(solution)/shard_map/factor/pallas_call | solution.py:319
  219.9 3.0 %all-to-all-done.10.received = bf16[32,32,128]{2,1,0:T(8,128)(2,1)S(1)} async-done(((bf16[32,32,128]{2,1,0:T(8,128)(2,1)}), bf16[32,32,128]{2,1,0:T(8,128)(2,1)S(1)}, u32[]{:S(2)}, u32[]{:S(2)}) %all-to-all-start.10) | async-done | bytes 262176 | tf_op jit(solution)/shard_map/all_to_all | solution.py:694
  222.9 0.1 route.9
  223.0 10.4 %all_to_all.74.refs_2_ = f32[32,8,128]{2,1,0:T(8,128)S(1)} all-to-all(f32[32,8,128]{2,1,0:T(8,128)S(1)} %get-tuple-element.111), channel_id=1, replica_groups=mesh['row'=4,'col'=8] {'row','col'}, dimensions={0} | all-to-all | bytes 262144 | tf_op jit(solution)/shard_map/all_to_all | solution.py:694
  233.4 6.9 %advance_last.1 = (bf16[384,2048]{1,0:T(8,128)(2,1)}, f32[128,128]{1,0:T(8,128)}, f32[64,128]{1,0:T(8,128)S(1)}, f32[128,128]{1,0:T(8,128)S(1)}) custom-call(s32[16,4]{1,0:T(8,128)S(1)} %copy.17.ids.refs_0_, f32[2]{0:T(128)S(1)} %copy-done.5, f32[32,8,128]{2,1,0:T(8,128)S(1)} %all_to_all.74.refs_2_, f32[16,128]{1,0:T(8,128)S(1)} %get-tuple-element.112.refs_3_, ...), custom_call_target="tpu_custom_call" | custom-call | tf_op jit(solution)/shard_map/advance_last/pallas_call | solution.py:575
  240.2 2.6 all-to-all-start.12
  242.8 7.6 %factor.9 = (f32[64,128]{1,0:T(8,128)S(1)}, f32[64,128]{1,0:T(8,128)S(1)}, f32[3,64,64]{2,1,0:T(8,128)S(1)}) custom-call(f32[128,128]{1,0:T(8,128)S(1)} %get-tuple-element.117.gram, f32[64,128]{1,0:T(8,128)S(1)} %get-tuple-element.118.inner, f32[64,128]{1,0:T(8,128)S(1)} %get-tuple-element.110._lag.refs_4_.lag, f32[64,128]{1,0:T(8,128)S(1)} %get-tuple-element.119.both), custom_call_target="tpu_custom_call" | custom-call | flops 100000000 | bytes 10000000 | tf_op jit(solution)/shard_map/factor/pallas_call | solution.py:319
  250.5 0.0 all-to-all-done.12.received
  250.5 12.9 %all_to_all.75 = f32[32,4,128]{2,1,0:T(4,128)S(1)} all-to-all(f32[32,4,128]{2,1,0:T(4,128)S(1)} %repeat_sum.1), channel_id=1, replica_groups=mesh['row'=4,'col'=8] {'row','col'}, dimensions={0} | all-to-all | bytes 131072 | tf_op jit(solution)/shard_map/all_to_all | solution.py:694
  263.5 9.3 %finish.1 = (f32[64,2048]{1,0:T(8,128)}, f32[6,3,64,64]{3,2,1,0:T(8,128)}) custom-call(f32[128,128]{1,0:T(8,128)S(1)} %bitcast.10, f32[64,128]{1,0:T(8,128)S(1)} %get-tuple-element.121.inner, f32[64,128]{1,0:T(8,128)S(1)} %get-tuple-element.120._lag.lag, bf16[384,2048]{1,0:T(8,128)(2,1)} %get-tuple-element.122.state, ...), custom_call_target="tpu_custom_call" | custom-call | tf_op jit(solution)/shard_map/finish/pallas_call | solution.py:664
  (9 shorter events, 0.1 us)
Async XLA Ops:
  0.6 1.6 copy-start.4
  2.7 1.4 copy-start.1
  4.0 7.4 %copy-start.6 = (s32[1024]{0:T(1024)S(1)}, s32[1024]{0:T(1024)}, u32[]{:S(2)}) copy-start(s32[1024]{0:T(1024)} %param.12) | copy-start | bytes 12292
  4.1 7.5 %copy-start.3 = (f32[64,2048]{1,0:T(8,128)S(1)}, f32[64,2048]{1,0:T(8,128)}, u32[]{:S(2)}) copy-start(f32[64,2048]{1,0:T(8,128)} %refs_6_.1) | copy-start | bytes 1572868
  4.1 7.5 %copy-start.5 = (f32[2]{0:T(128)S(1)}, f32[2]{0:T(128)}, u32[]{:S(2)}) copy-start(f32[2]{0:T(128)} %refs_1_.11) | copy-start | bytes 28
  4.1 7.5 %copy-start.7 = (s32[128]{0:T(128)S(1)}, s32[128]{0:T(128)}, u32[]{:S(2)}) copy-start(s32[128]{0:T(128)} %param.11) | copy-start | bytes 1540
  4.1 56.0 %all-to-all-start = ((bf16[8,128,1024]{2,1,0:T(8,128)(2,1)}), bf16[8,128,1024]{2,1,0:T(8,128)(2,1)S(1)}, u32[]{:S(2)}, u32[]{:S(2)}) async-start(bf16[8,128,1024]{2,1,0:T(8,128)(2,1)} %copy-done.1), calls=%async_computation | async-start | bytes 4194304 | tf_op jit(solution)/shard_map/all_to_all | solution.py:706
  11.6 2.8 %copy-start.2 = (bf16[3,16,4,128,128]{4,3,2,1,0:T(8,128)(2,1)S(1)}, bf16[3,16,4,128,128]{4,3,2,1,0:T(8,128)(2,1)}, u32[]{:S(2)}) copy-start(bf16[3,16,4,128,128]{4,3,2,1,0:T(8,128)(2,1)} %blocks.1) | copy-start | bytes 18874372
  14.4 14.8 %copy-start.8 = (s32[16,4]{0,1:T(4,128)S(1)}, s32[16,4]{0,1:T(4,128)}, u32[]{:S(2)}) copy-start(s32[16,4]{0,1:T(4,128)} %param.10) | copy-start | bytes 772
  22.6 6.6 %collective-permute-start.1 = (f32[64,128]{1,0:T(8,128)S(1)}, f32[64,128]{1,0:T(8,128)S(1)}, u32[]{:S(2)}, u32[]{:S(2)}) collective-permute-start(f32[64,128]{1,0:T(8,128)S(1)} %get-tuple-element.65), channel_id=1, source_target_pairs={{1,0},{2,1},{3,2},{4,3},{5,4},{6,5},{7,6},{8,7},{9,8},{10,9},{11,1... | collective-permute-start | bytes 98312 | tf_op jit(solution)/shard_map/ppermute | solution.py:699
  23.9 6.2 %collective-permute-start = (f32[64,128]{1,0:T(8,128)S(1)}, f32[64,128]{1,0:T(8,128)S(1)}, u32[]{:S(2)}, u32[]{:S(2)}) collective-permute-start(f32[64,128]{1,0:T(8,128)S(1)} %get-tuple-element.65), channel_id=1, source_target_pairs={{0,1},{1,2},{2,3},{3,4},{4,5},{5,6},{6,7},{7,8},{8,9},{9,10},{10,1... | collective-permute-start | bytes 98312 | tf_op jit(solution)/shard_map/ppermute | solution.py:699
  30.1 2.2 copy-start
  61.5 15.5 %all-to-all-start.1 = ((bf16[32,16,128]{2,1,0:T(8,128)(2,1)}), bf16[32,16,128]{2,1,0:T(8,128)(2,1)S(1)}, u32[]{:S(2)}, u32[]{:S(2)}) async-start(bf16[32,16,128]{2,1,0:T(8,128)(2,1)} %bitcast.4), calls=%async_computation.1 | async-start | bytes 262144 | tf_op jit(solution)/shard_map/all_to_all | solution.py:694
  82.3 15.2 %all-to-all-start.2 = ((bf16[32,32,128]{2,1,0:T(8,128)(2,1)}), bf16[32,32,128]{2,1,0:T(8,128)(2,1)S(1)}, u32[]{:S(2)}, u32[]{:S(2)}) async-start(bf16[32,32,128]{2,1,0:T(8,128)(2,1)} %get-tuple-element.71), calls=%async_computation.2 | async-start | bytes 524288 | tf_op jit(solution)/shard_map/all_to_all | solution.py:694
  115.3 13.3 %all-to-all-start.4 = ((bf16[32,32,128]{2,1,0:T(8,128)(2,1)}), bf16[32,32,128]{2,1,0:T(8,128)(2,1)S(1)}, u32[]{:S(2)}, u32[]{:S(2)}) async-start(bf16[32,32,128]{2,1,0:T(8,128)(2,1)} %get-tuple-element.77), calls=%async_computation.4 | async-start | bytes 524288 | tf_op jit(solution)/shard_map/all_to_all | solution.py:694
  146.7 13.3 %all-to-all-start.6 = ((bf16[32,32,128]{2,1,0:T(8,128)(2,1)}), bf16[32,32,128]{2,1,0:T(8,128)(2,1)S(1)}, u32[]{:S(2)}, u32[]{:S(2)}) async-start(bf16[32,32,128]{2,1,0:T(8,128)(2,1)} %get-tuple-element.86), calls=%async_computation.6 | async-start | bytes 524288 | tf_op jit(solution)/shard_map/all_to_all | solution.py:694
  178.2 13.3 %all-to-all-start.8 = ((bf16[32,32,128]{2,1,0:T(8,128)(2,1)}), bf16[32,32,128]{2,1,0:T(8,128)(2,1)S(1)}, u32[]{:S(2)}, u32[]{:S(2)}) async-start(bf16[32,32,128]{2,1,0:T(8,128)(2,1)} %get-tuple-element.96), calls=%async_computation.8 | async-start | bytes 524288 | tf_op jit(solution)/shard_map/all_to_all | solution.py:694
  209.6 13.3 %all-to-all-start.10 = ((bf16[32,32,128]{2,1,0:T(8,128)(2,1)}), bf16[32,32,128]{2,1,0:T(8,128)(2,1)S(1)}, u32[]{:S(2)}, u32[]{:S(2)}) async-start(bf16[32,32,128]{2,1,0:T(8,128)(2,1)} %get-tuple-element.106), calls=%async_computation.10 | async-start | bytes 524288 | tf_op jit(solution)/shard_map/all_to_all | solution.py:694
  240.2 10.2 %all-to-all-start.12 = ((f32[32,4,128]{2,1,0:T(4,128)}), f32[32,4,128]{2,1,0:T(4,128)S(1)}, u32[]{:S(2)}, u32[]{:S(2)}) async-start(f32[32,4,128]{2,1,0:T(4,128)} %bitcast.5), calls=%async_computation.12 | async-start | bytes 131072 | tf_op jit(solution)/shard_map/all_to_all | solution.py:694

commit v2 on v1

--- a/solution.py
+++ b/solution.py
@@ -186,10 +186,44 @@
     )(count, slots, mass)
 
 
-def halve_columns(top, low, s):
-    a, b, c = top[:, s : s + 1], top[:, s + 1 : s + 2], low[:, s + 1 : s + 2]
+def pivot_rows(top, s):
+    lanes = top[0].shape[1]
+    at = lambda i, j: jnp.broadcast_to(top[i][:, s + j : s + j + 1], (1, lanes))
+    a, b, c = at(0, 0), at(0, 1), at(1, 1)
+    p2, q2, p3, q3 = at(2, 0), at(2, 1), at(3, 0), at(3, 1)
+    d22, d23, d33 = at(2, 2), at(2, 3), at(3, 3)
     scale = 1.0 / (a * c - b * b)
-    return (c * top - b * low) * scale, (a * low - b * top) * scale
+    first = ((c * top[0] - b * top[1]) * scale, (a * top[1] - b * top[0]) * scale)
+    y02, y03 = (c * p2 - b * q2) * scale, (c * p3 - b * q3) * scale
+    y12, y13 = (a * q2 - b * p2) * scale, (a * q3 - b * p3) * scale
+    a2 = d22 - p2 * y02 - q2 * y12
+    b2 = d23 - p2 * y03 - q2 * y13
+    c2 = d33 - p3 * y03 - q3 * y13
+    scale2 = 1.0 / (a2 * c2 - b2 * b2)
+    third = top[2] - p2 * first[0] - q2 * first[1]
+    fourth = top[3] - p3 * first[0] - q3 * first[1]
+    v2 = (c2 * third - b2 * fourth) * scale2
+    v3 = (a2 * fourth - b2 * third) * scale2
+    v0 = first[0] - y02 * v2 - y03 * v3
+    v1 = first[1] - y12 * v2 - y13 * v3
+    return first, (v0, v1, v2, v3)
+
+
+def eliminate_four(work, s, j, keep):
+    sub = lax.broadcasted_iota(jnp.int32, (8, 1), 0)
+    first, full = pivot_rows([work[0][s + k : s + k + 1, :] for k in range(4)], j)
+    out = []
+    for i, group in enumerate(work):
+        columns = [group[:, j + k : j + k + 1] for k in range(4)]
+        half = columns[0] * full[0] + columns[1] * full[1]
+        update = half + (columns[2] * full[2] + columns[3] * full[3])
+        if i == 0:
+            pair = columns[0] * first[0] + columns[1] * first[1]
+            update = jnp.where(sub > s + 3, update, jnp.where(sub > s + 1, pair, 0.0))
+        elif keep is not None:
+            update = jnp.where(keep(i), update, 0.0)
+        out.append(group - update)
+    return out
 
 
 def eliminate(matrix, beside, coef, factor_t):
@@ -199,20 +233,13 @@
     lane_id = lax.broadcasted_iota(jnp.int32, (n, 2 * n), 1)
     factor_t[...] = jnp.where(row_id + n == lane_id, 1.0, 0.0)
     factor_t[:, :n] = matrix
-    sub = lax.broadcasted_iota(jnp.int32, (8, 1), 0)
     if beside:
         work = [factor_t[g * 8 : (g + 1) * 8, :] for g in range(groups)]
         done = 0
-        for j in range(0, n, 2):
+        for j in range(0, n, 4):
             g, s = divmod(j, 8)
-            new_top, new_low = halve_columns(work[g][s : s + 1, :], work[g][s + 1 : s + 2, :], j)
-            for i in range(g, groups):
-                left, right = work[i][:, j : j + 1], work[i][:, j + 1 : j + 2]
-                if i == g:
-                    left = jnp.where(sub > s + 1, left, 0.0)
-                    right = jnp.where(sub > s + 1, right, 0.0)
-                work[i] = work[i] - (left * new_top + right * new_low)
-            goal = len(beside) * (j + 2) // n
+            work[g:] = eliminate_four(work[g:], s, j, None)
+            goal = len(beside) * (j + 4) // n
             while done < goal:
                 beside[done]()
                 done += 1
@@ -221,13 +248,8 @@
 
         def group(step, _):
             work = [factor_t[g * 8 : (g + 1) * 8, :] for g in range(groups)]
-            for s in range(0, 8, 2):
-                new_top, new_low = halve_columns(work[0][s : s + 1, :], work[0][s + 1 : s + 2, :], s)
-                for i in range(groups):
-                    left, right = work[i][:, s : s + 1], work[i][:, s + 1 : s + 2]
-                    keep = sub > s + 1 if i == 0 else step + i < groups
-                    update = left * new_top + right * new_low
-                    work[i] = work[i] - jnp.where(keep, update, 0.0)
+            for s in range(0, 8, 4):
+                work = eliminate_four(work, s, s, lambda i: step + i < groups)
             for i in range(groups):
                 target = (i - 1) % groups
                 factor_t[target * 8 : (target + 1) * 8, :] = pltpu.roll(work[i], 2 * n - 8, 1)

time: 274 us -> 265 us (0.967)
  Pallas kernels: 110 us -> 90.7 us
  waiting for transfers between devices: 50.1 us -> 66.1 us
  blocking collectives: 64.4 us -> 59.2 us
    pallas_call x5, Pallas kernels: 38.2 us -> 21.9 us  [factor(): pl.pallas_call(functools.partial(factor_kernel, total), in_specs=[VMEM] *...]
    all_to_all x7, waiting for transfers between devices: 23.9 us -> 39.8 us  [exchange(): return lax.all_to_all(parts, AXES, 0, 0, tiled=True)]
    all_to_all x6, blocking collectives: 64.4 us -> 59.2 us  [exchange(): return lax.all_to_all(parts, AXES, 0, 0, tiled=True)]
    pallas_call x1, Pallas kernels: 9.32 us -> 6.37 us  [finish(): pl.pallas_call(functools.partial(finish_kernel, total), in_specs=[VMEM] *...]
  transfers between devices with their start and end apart: 10 -> 10, of which waited for: 8 -> 9; matrix products, arithmetic and copies ran while one was open for 0% -> 0% of each run, Pallas kernels for 20% -> 15%
where the time goes in v2:
time: 265 us; the launch traced here: 264 us
  Pallas kernels  90.7 us (34%)
  waiting for transfers between devices  66.1 us (25%)
  blocking collectives  59.2 us (22%)
  starting transfers between devices  38.5 us (15%)
  local copies, waits for them, and re-layouts  8.12 us (3%)
    all_to_all x6, blocking collectives, exchange(): return lax.all_to_all(parts, AXES, 0, 0, tiled=True)  59.2 us
    pallas_call x6, Pallas kernels, advance(): pl.pallas_call(functools.partial(advance_kernel, mode, total, peers), in_...  43.1 us
    all_to_all x7, waiting for transfers between devices, exchange(): return lax.all_to_all(parts, AXES, 0, 0, tiled=True)  39.8 us
    all_to_all x1, waiting for transfers between devices, local(): mass = lax.all_to_all(blocks, 'col', 0, 0, tiled=True)  25.4 us
    all_to_all x7, starting transfers between devices, exchange(): return lax.all_to_all(parts, AXES, 0, 0, tiled=True)  25.3 us
    pallas_call x5, Pallas kernels, factor(): pl.pallas_call(functools.partial(factor_kernel, total), in_specs=[VMEM] *...  21.9 us
    pallas_call x1, Pallas kernels, combine(): pl.pallas_call(combine_kernel, grid=(count,), in_specs=[SMEM, whole(rim.s...  8.28 us
    unnamed x19, local copies, waits for them, and re-layouts  8.03 us
  transfers between devices with their start and end apart: 10, of which 9 were waited for; matrix products, arithmetic and copies ran while one was open for 0% of the time, Pallas kernels for 15%

profile of v2, /device:TPU:0, one launch (start us, length us, event | category | flops | bytes accessed | tf_op | source)
XLA Modules:
  0.0 264.4 jit_solution(12459442075694563544)
XLA Ops:
  0.6 0.0 copy-start.4
  0.6 1.6 copy-done.4
  2.2 0.4 by_owner.1
  2.7 0.0 copy-start.1
  2.7 1.4 copy-done.1
  4.0 0.0 copy-start.6
  4.1 7.4 %all-to-all-start = ((bf16[8,128,1024]{2,1,0:T(8,128)(2,1)}), bf16[8,128,1024]{2,1,0:T(8,128)(2,1)S(1)}, u32[]{:S(2)}, u32[]{:S(2)}) async-start(bf16[8,128,1024]{2,1,0:T(8,128)(2,1)} %copy-done.1), calls=%async_computation | async-start | bytes 4194304 | tf_op jit(solution)/shard_map/all_to_all | solution.py:728
  11.5 0.0 copy-done.6
  11.5 0.1 copy.10.wet
  11.6 0.0 copy-done.3
  11.6 0.0 copy-done.5
  11.6 0.0 copy-done.7
  11.6 0.0 copy-start.2
  11.6 2.8 %copy-done.2 = bf16[3,16,4,128,128]{4,3,2,1,0:T(8,128)(2,1)S(1)} copy-done((bf16[3,16,4,128,128]{4,3,2,1,0:T(8,128)(2,1)S(1)}, bf16[3,16,4,128,128]{4,3,2,1,0:T(8,128)(2,1)}, u32[]{:S(2)}) %copy-start.2) | copy-done | bytes 6291480
  14.4 8.3 %combine.1 = (bf16[16,512,256]{2,1,0:T(8,128)(2,1)}, bf16[2048,128]{1,0:T(8,128)(2,1)S(1)}, bf16[32,2048]{1,0:T(8,128)(2,1)S(1)}, f32[64,128]{1,0:T(8,128)S(1)}) custom-call(f32[2]{0:T(128)S(1)} %copy-done.5, s32[1,128]{1,0:T(1,128)S(1)} %bitcast.13, s32[32,1]{1,0:T(8,128)S(1)} %copy.10.wet, f32[64,2048]{1,0:T(8,128)S(1)} %copy-done.3, ...), custom_call_target="tpu_custom_call" | custom-call | tf_op jit(solution)/shard_map/combine/pallas_call | solution.py:91
  22.6 1.3 collective-permute-start.1
  23.9 4.5 %collective-permute-start = (f32[64,128]{1,0:T(8,128)S(1)}, f32[64,128]{1,0:T(8,128)S(1)}, u32[]{:S(2)}, u32[]{:S(2)}) collective-permute-start(f32[64,128]{1,0:T(8,128)S(1)} %get-tuple-element.65), channel_id=1, source_target_pairs={{0,1},{1,2},{2,3},{3,4},{4,5},{5,6},{6,7},{7,8},{8,9},{9,10},{10,1... | collective-permute-start | bytes 98312 | tf_op jit(solution)/shard_map/ppermute | solution.py:721
  29.1 0.0 copy-done.8
  29.1 0.1 copy.17.ids.refs_0_
  29.2 0.0 collective-permute-done.1.above.refs_4_
  29.2 0.9 collective-permute-done.below.refs_3_
  30.1 2.2 copy-done
  32.3 2.4 prepare.1
  34.7 25.4 %all-to-all-done = bf16[8,128,1024]{2,1,0:T(8,128)(2,1)S(1)} async-done(((bf16[8,128,1024]{2,1,0:T(8,128)(2,1)}), bf16[8,128,1024]{2,1,0:T(8,128)(2,1)S(1)}, u32[]{:S(2)}, u32[]{:S(2)}) %all-to-all-start) | async-done | bytes 2097184 | tf_op jit(solution)/shard_map/all_to_all | solution.py:728
  60.0 1.4 start_pressure.1
  61.5 7.7 %all-to-all-start.1 = ((bf16[32,16,128]{2,1,0:T(8,128)(2,1)}), bf16[32,16,128]{2,1,0:T(8,128)(2,1)S(1)}, u32[]{:S(2)}, u32[]{:S(2)}) async-start(bf16[32,16,128]{2,1,0:T(8,128)(2,1)} %bitcast.4), calls=%async_computation.1 | async-start | bytes 262144 | tf_op jit(solution)/shard_map/all_to_all | solution.py:716
  69.2 6.4 %spread.1.refs_10_.refs_11_ = bf16[1024,2048]{1,0:T(8,128)(2,1)} custom-call(s32[1]{0:T(128)S(6)} %copy.18.count, s32[1,1024]{1,0:T(1,128)S(1)} %bitcast.12, bf16[8,4,2,16,1024]{4,3,2,1,0:T(8,128)(2,1)S(1)} %bitcast.9), custom_call_target="tpu_custom_call" | custom-call | flops 4294967296 | bytes 4194304 | tf_op jit(solution)/shard_map/spread/pallas_call | solution.py:170
  75.7 1.3 all-to-all-done.1.refs_2_
  77.0 5.4 %advance_first.1 = (bf16[384,2048]{1,0:T(8,128)(2,1)}, f32[128,256]{1,0:T(8,128)S(1)}, f32[32,128]{1,0:T(8,128)S(1)}, bf16[32,32,128]{2,1,0:T(8,128)(2,1)}) custom-call(s32[16,4]{1,0:T(8,128)S(1)} %copy.17.ids.refs_0_, f32[2]{0:T(128)S(1)} %copy-done.5, bf16[32,16,128]{2,1,0:T(8,128)(2,1)S(1)} %all-to-all-done.1.refs_2_, ...), custom_call_target="tpu_custom_call" | custom-call | tf_op jit(solution)/shard_map/advance_first/pallas_call | solution.py:597
  82.3 4.5 %all-to-all-start.2 = ((bf16[32,32,128]{2,1,0:T(8,128)(2,1)}), bf16[32,32,128]{2,1,0:T(8,128)(2,1)S(1)}, u32[]{:S(2)}, u32[]{:S(2)}) async-start(bf16[32,32,128]{2,1,0:T(8,128)(2,1)} %get-tuple-element.71), calls=%async_computation.2 | async-start | bytes 524288 | tf_op jit(solution)/shard_map/all_to_all | solution.py:716
  86.9 0.1 add_convert_fusion._lag.refs_4_.lag
  87.0 10.6 %all-to-all-done.2.received = bf16[32,32,128]{2,1,0:T(8,128)(2,1)S(1)} async-done(((bf16[32,32,128]{2,1,0:T(8,128)(2,1)}), bf16[32,32,128]{2,1,0:T(8,128)(2,1)S(1)}, u32[]{:S(2)}, u32[]{:S(2)}) %all-to-all-start.2) | async-done | bytes 262176 | tf_op jit(solution)/shard_map/all_to_all | solution.py:716
  97.6 0.1 route.5
  97.6 9.9 %all_to_all.70.refs_2_ = f32[32,8,128]{2,1,0:T(8,128)S(1)} all-to-all(f32[32,8,128]{2,1,0:T(8,128)S(1)} %get-tuple-element.72), channel_id=1, replica_groups=mesh['row'=4,'col'=8] {'row','col'}, dimensions={0} | all-to-all | bytes 262144 | tf_op jit(solution)/shard_map/all_to_all | solution.py:716
  107.5 7.7 %advance_mid.4 = (bf16[384,2048]{1,0:T(8,128)(2,1)}, f32[128,256]{1,0:T(8,128)S(1)}, f32[32,128]{1,0:T(8,128)S(1)}, bf16[32,32,128]{2,1,0:T(8,128)(2,1)}, f32[64,128]{1,0:T(8,128)S(1)}, /*index=5*/f32[128,128]{1,0:T(8,128)S(1)}) custom-call(s32[16,4]{1,0:T(8,128)S(1)} %copy.17.ids.refs_0_, f32[2]{0:T(128)S(1)} %copy-done.5, ...), custom_call_target="tpu_custom_call" | custom-call | tf_op jit(solution)/shard_map/advance_mid/pallas_call | solution.py:597
  115.3 2.6 all-to-all-start.4
  117.9 4.4 %factor.5 = (f32[64,128]{1,0:T(8,128)S(1)}, f32[64,128]{1,0:T(8,128)S(1)}, f32[3,64,64]{2,1,0:T(8,128)S(1)}) custom-call(f32[128,128]{1,0:T(8,128)S(1)} %get-tuple-element.78.gram, f32[64,128]{1,0:T(8,128)S(1)} %broadcast_in_dim.15.inner, f32[64,128]{1,0:T(8,128)S(1)} %add_convert_fusion._lag.refs_4_.lag, f32[64,128]{1,0:T(8,128)S(1)} %get-tuple-element.79.both), custom_call_target="tpu_custom_call" | custom-call | flops 100000000 | bytes 10000000 | tf_op jit(solution)/shard_map/factor/pallas_call | solution.py:341
  122.3 6.3 %all-to-all-done.4.received = bf16[32,32,128]{2,1,0:T(8,128)(2,1)S(1)} async-done(((bf16[32,32,128]{2,1,0:T(8,128)(2,1)}), bf16[32,32,128]{2,1,0:T(8,128)(2,1)S(1)}, u32[]{:S(2)}, u32[]{:S(2)}) %all-to-all-start.4) | async-done | bytes 262176 | tf_op jit(solution)/shard_map/all_to_all | solution.py:716
  128.5 0.1 route.6
  128.6 9.8 %all_to_all.71.refs_2_ = f32[32,8,128]{2,1,0:T(8,128)S(1)} all-to-all(f32[32,8,128]{2,1,0:T(8,128)S(1)} %get-tuple-element.81), channel_id=1, replica_groups=mesh['row'=4,'col'=8] {'row','col'}, dimensions={0} | all-to-all | bytes 262144 | tf_op jit(solution)/shard_map/all_to_all | solution.py:716
  138.4 7.7 %advance_mid.5 = (bf16[384,2048]{1,0:T(8,128)(2,1)}, f32[128,256]{1,0:T(8,128)S(1)}, f32[32,128]{1,0:T(8,128)S(1)}, bf16[32,32,128]{2,1,0:T(8,128)(2,1)}, f32[64,128]{1,0:T(8,128)S(1)}, /*index=5*/f32[128,128]{1,0:T(8,128)S(1)}) custom-call(s32[16,4]{1,0:T(8,128)S(1)} %copy.17.ids.refs_0_, f32[2]{0:T(128)S(1)} %copy-done.5, ...), custom_call_target="tpu_custom_call" | custom-call | tf_op jit(solution)/shard_map/advance_mid/pallas_call | solution.py:597
  146.1 2.6 all-to-all-start.6
  148.7 4.4 %factor.6 = (f32[64,128]{1,0:T(8,128)S(1)}, f32[64,128]{1,0:T(8,128)S(1)}, f32[3,64,64]{2,1,0:T(8,128)S(1)}) custom-call(f32[128,128]{1,0:T(8,128)S(1)} %get-tuple-element.87.gram, f32[64,128]{1,0:T(8,128)S(1)} %get-tuple-element.88.inner, f32[64,128]{1,0:T(8,128)S(1)} %get-tuple-element.80._lag.refs_4_.lag, f32[64,128]{1,0:T(8,128)S(1)} %get-tuple-element.89.both), custom_call_target="tpu_custom_call" | custom-call | flops 100000000 | bytes 10000000 | tf_op jit(solution)/shard_map/factor/pallas_call | solution.py:341
  153.1 6.3 %all-to-all-done.6.received = bf16[32,32,128]{2,1,0:T(8,128)(2,1)S(1)} async-done(((bf16[32,32,128]{2,1,0:T(8,128)(2,1)}), bf16[32,32,128]{2,1,0:T(8,128)(2,1)S(1)}, u32[]{:S(2)}, u32[]{:S(2)}) %all-to-all-start.6) | async-done | bytes 262176 | tf_op jit(solution)/shard_map/all_to_all | solution.py:716
  159.4 0.1 route.7
  159.5 9.8 %all_to_all.72.refs_2_ = f32[32,8,128]{2,1,0:T(8,128)S(1)} all-to-all(f32[32,8,128]{2,1,0:T(8,128)S(1)} %get-tuple-element.91), channel_id=1, replica_groups=mesh['row'=4,'col'=8] {'row','col'}, dimensions={0} | all-to-all | bytes 262144 | tf_op jit(solution)/shard_map/all_to_all | solution.py:716
  169.3 7.7 %advance_mid.6 = (bf16[384,2048]{1,0:T(8,128)(2,1)}, f32[128,256]{1,0:T(8,128)S(1)}, f32[32,128]{1,0:T(8,128)S(1)}, bf16[32,32,128]{2,1,0:T(8,128)(2,1)}, f32[64,128]{1,0:T(8,128)S(1)}, /*index=5*/f32[128,128]{1,0:T(8,128)S(1)}) custom-call(s32[16,4]{1,0:T(8,128)S(1)} %copy.17.ids.refs_0_, f32[2]{0:T(128)S(1)} %copy-done.5, ...), custom_call_target="tpu_custom_call" | custom-call | tf_op jit(solution)/shard_map/advance_mid/pallas_call | solution.py:597
  177.0 2.6 all-to-all-start.8
  179.6 4.4 %factor.7 = (f32[64,128]{1,0:T(8,128)S(1)}, f32[64,128]{1,0:T(8,128)S(1)}, f32[3,64,64]{2,1,0:T(8,128)S(1)}) custom-call(f32[128,128]{1,0:T(8,128)S(1)} %get-tuple-element.97.gram, f32[64,128]{1,0:T(8,128)S(1)} %get-tuple-element.98.inner, f32[64,128]{1,0:T(8,128)S(1)} %get-tuple-element.90._lag.refs_4_.lag, f32[64,128]{1,0:T(8,128)S(1)} %get-tuple-element.99.both), custom_call_target="tpu_custom_call" | custom-call | flops 100000000 | bytes 10000000 | tf_op jit(solution)/shard_map/factor/pallas_call | solution.py:341
  184.0 6.3 %all-to-all-done.8.received = bf16[32,32,128]{2,1,0:T(8,128)(2,1)S(1)} async-done(((bf16[32,32,128]{2,1,0:T(8,128)(2,1)}), bf16[32,32,128]{2,1,0:T(8,128)(2,1)S(1)}, u32[]{:S(2)}, u32[]{:S(2)}) %all-to-all-start.8) | async-done | bytes 262176 | tf_op jit(solution)/shard_map/all_to_all | solution.py:716
  190.2 0.1 route.8
  190.3 9.8 %all_to_all.73.refs_2_ = f32[32,8,128]{2,1,0:T(8,128)S(1)} all-to-all(f32[32,8,128]{2,1,0:T(8,128)S(1)} %get-tuple-element.101), channel_id=1, replica_groups=mesh['row'=4,'col'=8] {'row','col'}, dimensions={0} | all-to-all | bytes 262144 | tf_op jit(solution)/shard_map/all_to_all | solution.py:716
  200.1 7.7 %advance_mid.7 = (bf16[384,2048]{1,0:T(8,128)(2,1)}, f32[128,256]{1,0:T(8,128)S(1)}, f32[32,128]{1,0:T(8,128)S(1)}, bf16[32,32,128]{2,1,0:T(8,128)(2,1)}, f32[64,128]{1,0:T(8,128)S(1)}, /*index=5*/f32[128,128]{1,0:T(8,128)S(1)}) custom-call(s32[16,4]{1,0:T(8,128)S(1)} %copy.17.ids.refs_0_, f32[2]{0:T(128)S(1)} %copy-done.5, ...), custom_call_target="tpu_custom_call" | custom-call | tf_op jit(solution)/shard_map/advance_mid/pallas_call | solution.py:597
  207.9 2.6 all-to-all-start.10
  210.5 4.4 %factor.8 = (f32[64,128]{1,0:T(8,128)S(1)}, f32[64,128]{1,0:T(8,128)S(1)}, f32[3,64,64]{2,1,0:T(8,128)S(1)}) custom-call(f32[128,128]{1,0:T(8,128)S(1)} %get-tuple-element.107.gram, f32[64,128]{1,0:T(8,128)S(1)} %get-tuple-element.108.inner, f32[64,128]{1,0:T(8,128)S(1)} %get-tuple-element.100._lag.refs_4_.lag, f32[64,128]{1,0:T(8,128)S(1)} %get-tuple-element.109.both), custom_call_target="tpu_custom_call" | custom-call | flops 100000000 | bytes 10000000 | tf_op jit(solution)/shard_map/factor/pallas_call | solution.py:341
  214.8 6.3 %all-to-all-done.10.received = bf16[32,32,128]{2,1,0:T(8,128)(2,1)S(1)} async-done(((bf16[32,32,128]{2,1,0:T(8,128)(2,1)}), bf16[32,32,128]{2,1,0:T(8,128)(2,1)S(1)}, u32[]{:S(2)}, u32[]{:S(2)}) %all-to-all-start.10) | async-done | bytes 262176 | tf_op jit(solution)/shard_map/all_to_all | solution.py:716
  221.1 0.1 route.9
  221.2 9.8 %all_to_all.74.refs_2_ = f32[32,8,128]{2,1,0:T(8,128)S(1)} all-to-all(f32[32,8,128]{2,1,0:T(8,128)S(1)} %get-tuple-element.111), channel_id=1, replica_groups=mesh['row'=4,'col'=8] {'row','col'}, dimensions={0} | all-to-all | bytes 262144 | tf_op jit(solution)/shard_map/all_to_all | solution.py:716
  231.0 6.9 %advance_last.1 = (bf16[384,2048]{1,0:T(8,128)(2,1)}, f32[128,128]{1,0:T(8,128)}, f32[64,128]{1,0:T(8,128)S(1)}, f32[128,128]{1,0:T(8,128)S(1)}) custom-call(s32[16,4]{1,0:T(8,128)S(1)} %copy.17.ids.refs_0_, f32[2]{0:T(128)S(1)} %copy-done.5, f32[32,8,128]{2,1,0:T(8,128)S(1)} %all_to_all.74.refs_2_, f32[16,128]{1,0:T(8,128)S(1)} %get-tuple-element.112.refs_3_, ...), custom_call_target="tpu_custom_call" | custom-call | tf_op jit(solution)/shard_map/advance_last/pallas_call | solution.py:597
  237.9 2.6 all-to-all-start.12
  240.5 4.4 %factor.9 = (f32[64,128]{1,0:T(8,128)S(1)}, f32[64,128]{1,0:T(8,128)S(1)}, f32[3,64,64]{2,1,0:T(8,128)S(1)}) custom-call(f32[128,128]{1,0:T(8,128)S(1)} %get-tuple-element.117.gram, f32[64,128]{1,0:T(8,128)S(1)} %get-tuple-element.118.inner, f32[64,128]{1,0:T(8,128)S(1)} %get-tuple-element.110._lag.refs_4_.lag, f32[64,128]{1,0:T(8,128)S(1)} %get-tuple-element.119.both), custom_call_target="tpu_custom_call" | custom-call | flops 100000000 | bytes 10000000 | tf_op jit(solution)/shard_map/factor/pallas_call | solution.py:341
  244.9 2.9 %all-to-all-done.12.received = f32[32,4,128]{2,1,0:T(4,128)S(1)} async-done(((f32[32,4,128]{2,1,0:T(4,128)}), f32[32,4,128]{2,1,0:T(4,128)S(1)}, u32[]{:S(2)}, u32[]{:S(2)}) %all-to-all-start.12) | async-done | bytes 65568 | tf_op jit(solution)/shard_map/all_to_all | solution.py:716
  247.8 10.0 %all_to_all.75 = f32[32,4,128]{2,1,0:T(4,128)S(1)} all-to-all(f32[32,4,128]{2,1,0:T(4,128)S(1)} %repeat_sum.1), channel_id=1, replica_groups=mesh['row'=4,'col'=8] {'row','col'}, dimensions={0} | all-to-all | bytes 131072 | tf_op jit(solution)/shard_map/all_to_all | solution.py:716
  257.8 6.4 %finish.1 = (f32[64,2048]{1,0:T(8,128)}, f32[6,3,64,64]{3,2,1,0:T(8,128)}) custom-call(f32[128,128]{1,0:T(8,128)S(1)} %bitcast.10, f32[64,128]{1,0:T(8,128)S(1)} %get-tuple-element.121.inner, f32[64,128]{1,0:T(8,128)S(1)} %get-tuple-element.120._lag.lag, bf16[384,2048]{1,0:T(8,128)(2,1)} %get-tuple-element.122.state, ...), custom_call_target="tpu_custom_call" | custom-call | tf_op jit(solution)/shard_map/finish/pallas_call | solution.py:686
  (9 shorter events, 0.1 us)
Async XLA Ops:
  0.6 1.6 copy-start.4
  2.7 1.4 copy-start.1
  4.0 7.4 %copy-start.6 = (s32[1024]{0:T(1024)S(1)}, s32[1024]{0:T(1024)}, u32[]{:S(2)}) copy-start(s32[1024]{0:T(1024)} %param.12) | copy-start | bytes 12292
  4.1 7.5 %copy-start.3 = (f32[64,2048]{1,0:T(8,128)S(1)}, f32[64,2048]{1,0:T(8,128)}, u32[]{:S(2)}) copy-start(f32[64,2048]{1,0:T(8,128)} %refs_6_.1) | copy-start | bytes 1572868
  4.1 7.5 %copy-start.5 = (f32[2]{0:T(128)S(1)}, f32[2]{0:T(128)}, u32[]{:S(2)}) copy-start(f32[2]{0:T(128)} %refs_1_.11) | copy-start | bytes 28
  4.1 7.5 %copy-start.7 = (s32[128]{0:T(128)S(1)}, s32[128]{0:T(128)}, u32[]{:S(2)}) copy-start(s32[128]{0:T(128)} %param.11) | copy-start | bytes 1540
  4.1 56.0 %all-to-all-start = ((bf16[8,128,1024]{2,1,0:T(8,128)(2,1)}), bf16[8,128,1024]{2,1,0:T(8,128)(2,1)S(1)}, u32[]{:S(2)}, u32[]{:S(2)}) async-start(bf16[8,128,1024]{2,1,0:T(8,128)(2,1)} %copy-done.1), calls=%async_computation | async-start | bytes 4194304 | tf_op jit(solution)/shard_map/all_to_all | solution.py:728
  11.6 2.8 %copy-start.2 = (bf16[3,16,4,128,128]{4,3,2,1,0:T(8,128)(2,1)S(1)}, bf16[3,16,4,128,128]{4,3,2,1,0:T(8,128)(2,1)}, u32[]{:S(2)}) copy-start(bf16[3,16,4,128,128]{4,3,2,1,0:T(8,128)(2,1)} %blocks.1) | copy-start | bytes 18874372
  14.4 14.8 %copy-start.8 = (s32[16,4]{0,1:T(4,128)S(1)}, s32[16,4]{0,1:T(4,128)}, u32[]{:S(2)}) copy-start(s32[16,4]{0,1:T(4,128)} %param.10) | copy-start | bytes 772
  22.6 6.6 %collective-permute-start.1 = (f32[64,128]{1,0:T(8,128)S(1)}, f32[64,128]{1,0:T(8,128)S(1)}, u32[]{:S(2)}, u32[]{:S(2)}) collective-permute-start(f32[64,128]{1,0:T(8,128)S(1)} %get-tuple-element.65), channel_id=1, source_target_pairs={{1,0},{2,1},{3,2},{4,3},{5,4},{6,5},{7,6},{8,7},{9,8},{10,9},{11,1... | collective-permute-start | bytes 98312 | tf_op jit(solution)/shard_map/ppermute | solution.py:721
  23.9 6.2 %collective-permute-start = (f32[64,128]{1,0:T(8,128)S(1)}, f32[64,128]{1,0:T(8,128)S(1)}, u32[]{:S(2)}, u32[]{:S(2)}) collective-permute-start(f32[64,128]{1,0:T(8,128)S(1)} %get-tuple-element.65), channel_id=1, source_target_pairs={{0,1},{1,2},{2,3},{3,4},{4,5},{5,6},{6,7},{7,8},{8,9},{9,10},{10,1... | collective-permute-start | bytes 98312 | tf_op jit(solution)/shard_map/ppermute | solution.py:721
  30.1 2.2 copy-start
  61.5 15.5 %all-to-all-start.1 = ((bf16[32,16,128]{2,1,0:T(8,128)(2,1)}), bf16[32,16,128]{2,1,0:T(8,128)(2,1)S(1)}, u32[]{:S(2)}, u32[]{:S(2)}) async-start(bf16[32,16,128]{2,1,0:T(8,128)(2,1)} %bitcast.4), calls=%async_computation.1 | async-start | bytes 262144 | tf_op jit(solution)/shard_map/all_to_all | solution.py:716
  82.3 15.2 %all-to-all-start.2 = ((bf16[32,32,128]{2,1,0:T(8,128)(2,1)}), bf16[32,32,128]{2,1,0:T(8,128)(2,1)S(1)}, u32[]{:S(2)}, u32[]{:S(2)}) async-start(bf16[32,32,128]{2,1,0:T(8,128)(2,1)} %get-tuple-element.71), calls=%async_computation.2 | async-start | bytes 524288 | tf_op jit(solution)/shard_map/all_to_all | solution.py:716
  115.3 13.3 %all-to-all-start.4 = ((bf16[32,32,128]{2,1,0:T(8,128)(2,1)}), bf16[32,32,128]{2,1,0:T(8,128)(2,1)S(1)}, u32[]{:S(2)}, u32[]{:S(2)}) async-start(bf16[32,32,128]{2,1,0:T(8,128)(2,1)} %get-tuple-element.77), calls=%async_computation.4 | async-start | bytes 524288 | tf_op jit(solution)/shard_map/all_to_all | solution.py:716
  146.1 13.3 %all-to-all-start.6 = ((bf16[32,32,128]{2,1,0:T(8,128)(2,1)}), bf16[32,32,128]{2,1,0:T(8,128)(2,1)S(1)}, u32[]{:S(2)}, u32[]{:S(2)}) async-start(bf16[32,32,128]{2,1,0:T(8,128)(2,1)} %get-tuple-element.86), calls=%async_computation.6 | async-start | bytes 524288 | tf_op jit(solution)/shard_map/all_to_all | solution.py:716
  177.0 13.3 %all-to-all-start.8 = ((bf16[32,32,128]{2,1,0:T(8,128)(2,1)}), bf16[32,32,128]{2,1,0:T(8,128)(2,1)S(1)}, u32[]{:S(2)}, u32[]{:S(2)}) async-start(bf16[32,32,128]{2,1,0:T(8,128)(2,1)} %get-tuple-element.96), calls=%async_computation.8 | async-start | bytes 524288 | tf_op jit(solution)/shard_map/all_to_all | solution.py:716
  207.9 13.3 %all-to-all-start.10 = ((bf16[32,32,128]{2,1,0:T(8,128)(2,1)}), bf16[32,32,128]{2,1,0:T(8,128)(2,1)S(1)}, u32[]{:S(2)}, u32[]{:S(2)}) async-start(bf16[32,32,128]{2,1,0:T(8,128)(2,1)} %get-tuple-element.106), calls=%async_computation.10 | async-start | bytes 524288 | tf_op jit(solution)/shard_map/all_to_all | solution.py:716
  237.9 9.9 %all-to-all-start.12 = ((f32[32,4,128]{2,1,0:T(4,128)}), f32[32,4,128]{2,1,0:T(4,128)S(1)}, u32[]{:S(2)}, u32[]{:S(2)}) async-start(f32[32,4,128]{2,1,0:T(4,128)} %bitcast.5), calls=%async_computation.12 | async-start | bytes 131072 | tf_op jit(solution)/shard_map/all_to_all | solution.py:716

commit v3 on v2

--- a/solution.py
+++ b/solution.py
@@ -54,13 +54,13 @@
         grid=(n_col,),
         in_specs=[pl.BlockSpec((size, wcap), lambda c: (0, c))],
         out_specs=pl.BlockSpec((1, size, wcap), lambda c: (c, 0, 0)),
-        out_shape=jax.ShapeDtypeStruct((n_col, size, wcap), BF16),
+        out_shape=pltpu.HBM((n_col, size, wcap), BF16),
         compiler_params=pltpu.CompilerParams(vmem_limit_bytes=LIMIT),
         name="by_owner",
     )(mass)
 
 
-def combine_kernel(rates, rim, wet, start, blocks, mixed, pick, place, halo):
+def combine_kernel(rates, count, rim, wet, slots, start, blocks, mixed, pick, place, halo, values):
     size = blocks.shape[-1]
     for k in range(blocks.shape[2]):
         whole = (
@@ -82,19 +82,28 @@
         halo[...] = jnp.dot(high, pick[...], preferred_element_type=F32) + jnp.dot(
             low, pick[...], preferred_element_type=F32
         )
-
-
-def combine(rates, rim, wet, start, blocks):
-    _, count, nnz, size, _ = blocks.shape
+        live = live_slots(count, slots)
+        columns = min(start.shape[1], 512)
+        total = jnp.zeros(values.shape, F32)
+        for first in range(0, start.shape[1], columns):
+            picked = chosen(first, (columns, slots.shape[1]), live)
+            total = total + jnp.dot(high[:, first : first + columns], picked, preferred_element_type=F32)
+        values[...] = total.astype(BF16)
+
+
+def combine(rates, count, rim, wet, slots, start, blocks):
+    _, block_rows, nnz, size, _ = blocks.shape
     vectors, width = start.shape
     whole = lambda shape: pl.BlockSpec(shape, lambda i: (0,) * len(shape))
     return pl.pallas_call(
         combine_kernel,
-        grid=(count,),
+        grid=(block_rows,),
         in_specs=[
+            SMEM,
             SMEM,
             whole(rim.shape),
             whole(wet.shape),
+            whole(slots.shape),
             whole(start.shape),
             pl.BlockSpec((3, 1, nnz, size, size), lambda i: (0, i, 0, 0, 0)),
         ],
@@ -103,16 +112,18 @@
             whole((width, rim.shape[1])),
             whole((wet.shape[0], width)),
             whole((vectors, rim.shape[1])),
+            whole((vectors, slots.shape[1])),
         ],
         out_shape=[
-            pltpu.HBM((count, nnz * size, 2 * size), BF16),
+            pltpu.HBM((block_rows, nnz * size, 2 * size), BF16),
             jax.ShapeDtypeStruct((width, rim.shape[1]), BF16),
             jax.ShapeDtypeStruct((wet.shape[0], width), BF16),
             jax.ShapeDtypeStruct((vectors, rim.shape[1]), F32),
+            jax.ShapeDtypeStruct((vectors, slots.shape[1]), BF16),
         ],
         compiler_params=pltpu.CompilerParams(vmem_limit_bytes=LIMIT),
         name="combine",
-    )(rates, rim, wet, start, blocks)
+    )(rates, count, rim, wet, slots, start, blocks)
 
 
 def live_slots(count, slots):
@@ -135,16 +146,16 @@
             part[r * size : (r + 1) * size, h * vectors : (h + 1) * vectors] = pressed
 
 
-def start_pressure(values, mass, base):
+def start_pressure(values, mass):
     n_col, n_row, _, half, _ = mass.shape
     return pl.pallas_call(
-        lambda values, mass, _base, part: start_pressure_kernel(values, mass, part),
-        in_specs=[VMEM, VMEM, HBM],
+        start_pressure_kernel,
+        in_specs=[VMEM, VMEM],
         out_specs=VMEM,
         out_shape=jax.ShapeDtypeStruct((n_col * n_row * half, 2 * values.shape[0]), BF16),
         compiler_params=pltpu.CompilerParams(vmem_limit_bytes=LIMIT),
         name="start_pressure",
-    )(values, mass, base)
+    )(values, mass)
 
 
 def spread_kernel(count, slots, mass, spread, own):
@@ -378,48 +389,15 @@
     return pair[:, :size] + pair[:, size:]
 
 
-def prepare_kernel(ids, count, slots, below, above, start, mixed, out, values, extended):
-    size = below.shape[1]
-    block = start[...].astype(BF16)
-    place_columns(extended, block, jnp.concatenate([below[...], above[...]], 1))
-    for i in range(out.shape[1] // size):
-        out[:, i * size : (i + 1) * size] = block_row(ids, extended, mixed, i)
-    live = live_slots(count, slots)
-    columns = min(out.shape[1], 512)
-    total = jnp.zeros(values.shape, F32)
-    for first in range(0, out.shape[1], columns):
-        picked = chosen(first, (columns, slots.shape[1]), live)
-        total = total + jnp.dot(block[:, first : first + columns], picked, preferred_element_type=F32)
-    values[...] = total.astype(BF16)
-
-
-def prepare(ids, count, slots, below, above, start, mixed):
-    vectors, width = start.shape
-    size = below.shape[1]
-    return pl.pallas_call(
-        prepare_kernel,
-        in_specs=[SMEM, SMEM] + [VMEM] * 5,
-        out_specs=[VMEM] * 2,
-        out_shape=[
-            pltpu.HBM((vectors, width), F32),
-            jax.ShapeDtypeStruct((vectors, slots.shape[1]), BF16),
-        ],
-        scratch_shapes=[pltpu.VMEM((width // size + 2, vectors, size), BF16)],
-        compiler_params=pltpu.CompilerParams(vmem_limit_bytes=LIMIT),
-        name="prepare",
-    )(ids, count, slots, below, above, start, mixed)
-
-
 def advance_kernel(mode, total, peers, *refs):
     it = iter(refs)
     take = lambda k: [next(it) for _ in range(k)]
     ids, rates = take(2)
     if mode == "first":
         arrived, below, above = take(3)
-        held = take(2)
     else:
         received, pressed, lag, edges, wet_held = take(5)
-        held = take(1)
+    (held,) = take(1)
     pick, place, mixed_in, spread_in = take(4)
     (state_out,) = take(1)
     if mode == "last":
@@ -440,19 +418,15 @@
     count = width // size
     glines = -(-2 * n // peers)
     hlines = -(-n // peers)
-    loads = []
-    for k, source in enumerate(held):
-        target = stack.at[pl.ds(k * n, n)] if mode == "first" else stack
-        loads.append(pltpu.make_async_copy(source, target, sems.at[k]))
-        loads[-1].start()
-    if mode != "first":
-        load_mixed = pltpu.make_async_copy(mixed_in, mixed, sems.at[3])
-        load_mixed.start()
+    load = pltpu.make_async_copy(held, stack, sems.at[0])
+    load.start()
+    load_mixed = pltpu.make_async_copy(mixed_in, mixed, sems.at[1])
+    load_mixed.start()
     load_spread = []
     if mode != "last":
         for h in range(2):
             part = spread_in.at[pl.ds(h * spread.shape[1], spread.shape[1])]
-            load_spread.append(pltpu.make_async_copy(part, spread.at[h], sems.at[4 + h]))
+            load_spread.append(pltpu.make_async_copy(part, spread.at[h], sems.at[3 + h]))
             load_spread[-1].start()
 
     if mode == "first":
@@ -463,9 +437,8 @@
         edges_out[n:, :] = jnp.zeros_like(edge)
         wet_out[:, :n] = wet
         wet_out[:, n:] = jnp.zeros_like(wet)
-        for copy in loads:
-            copy.wait()
-        residual = stack[n : 2 * n, :]
+        load.wait()
+        residual = stack[...]
         terms[4 * n :, :] = jnp.zeros((2 * n, width), BF16)
     else:
         unpack(glines, received, gram_in, slice(None), 0)
@@ -484,8 +457,7 @@
             edges_out[n:, :] = exact(pull, edges[:n, :])
             wet_out[:, :n] = wet
             wet_out[:, n:] = exact_rows(wet_held[:, :n], pull)
-        for copy in loads:
-            copy.wait()
+        load.wait()
         mixture = jnp.dot(weights[...], stack[...], preferred_element_type=F32)
         residual = mixture[:n] + mixture[n : 2 * n]
         terms[4 * n : 5 * n, :], terms[5 * n :, :] = halves(mixture[2 * n : 3 * n] + mixture[3 * n :])
@@ -493,14 +465,12 @@
     terms[2 * n : 3 * n, :] = high
     terms[3 * n : 4 * n, :] = low
     force = thirds(wet.T * rates[1])
-    if mode != "first":
-        place_columns(extended, high, edge)
-        load_mixed.wait()
+    place_columns(extended, high, edge)
+    load_mixed.wait()
     for i in range(count):
         lanes = slice(i * size, (i + 1) * size)
         added = jnp.dot(force, place[:, lanes], preferred_element_type=F32)
-        applied = stack[:n, lanes] if mode == "first" else block_row(ids, extended, mixed, i)
-        applied = applied - (added[:n] + added[n : 2 * n] + added[2 * n :])
+        applied = block_row(ids, extended, mixed, i) - (added[:n] + added[n : 2 * n] + added[2 * n :])
         terms[:n, lanes], terms[n : 2 * n, lanes] = halves(applied)
     store = pltpu.make_async_copy(terms, state_out, sems.at[2])
     store.start()
@@ -583,20 +553,19 @@
     scratch = [
         pltpu.VMEM((width // size + 2, vectors, size), BF16),
         pltpu.VMEM((6 * vectors, width), BF16),
-        pltpu.VMEM((2 * vectors, width), F32) if mode == "first" else pltpu.VMEM((6 * vectors, width), BF16),
-        pltpu.VMEM(mixed.shape if mode != "first" else (16, 128), BF16),
+        pltpu.VMEM((vectors, width), F32) if mode == "first" else pltpu.VMEM((6 * vectors, width), BF16),
+        pltpu.VMEM(mixed.shape, BF16),
         pltpu.VMEM((2, spread.shape[0] // 2, spread.shape[1]) if mode != "last" else (16, 128), BF16),
         pltpu.VMEM((3 * vectors, 2 * size), F32),
-        pltpu.SemaphoreType.DMA((6,)),
+        pltpu.SemaphoreType.DMA((5,)),
     ]
     if mode != "last":
         scratch += [pltpu.VMEM(small.shape, F32), pltpu.VMEM((peers, extra, 2 * vectors), F32)]
     if mode != "first":
         scratch += [pltpu.VMEM((vectors, 3 * vectors), F32), pltpu.VMEM((4 * vectors, 6 * vectors), BF16)]
-    held = 2 if mode == "first" else 1
     return pl.pallas_call(
         functools.partial(advance_kernel, mode, total, peers),
-        in_specs=[SMEM, SMEM] + [VMEM] * (len(state) - held) + [HBM] * held + [VMEM, VMEM, HBM, HBM],
+        in_specs=[SMEM, SMEM] + [VMEM] * (len(state) - 1) + [HBM, VMEM, VMEM, HBM, HBM],
         out_specs=specs,
         out_shape=shapes,
         scratch_shapes=scratch,
@@ -724,22 +693,20 @@
         lines = gram.shape[0] // peers
         return exchange(repeat_sum(exchange(gram.reshape(peers, lines, -1)), lag)).reshape(gram.shape)
 
-    blocks = by_owner(added_mass, n_col, wcap)
+    blocks = by_owner(in_hbm(added_mass), n_col, wcap)
     mass = lax.all_to_all(blocks, "col", 0, 0, tiled=True)
     mass = mass.reshape(n_col, n_row, 2, wets // 2, wcap)
-    mixed, pick, place, halo = combine(
-        rates, rim_rows[None, :], wet_slots[:wets, None], start_block, struct_blocks
+    slots = wet_slots[None, :]
+    mixed, pick, place, halo, values = combine(
+        rates, wet_counts, rim_rows[None, :], wet_slots[:wets, None], slots, start_block, struct_blocks
     )
     below, above = neighbours(halo)
-    slots = wet_slots[None, :]
-    base, values = prepare(block_ids, wet_counts, slots, below, above, start_block, mixed)
-    base = in_hbm(base)
-    part = start_pressure(values, mass, base)
+    part = start_pressure(values, mass)
     spread = spread_mass(wet_counts, slots, mass, width)
     fixed = (in_hbm(mixed), pick, place, in_hbm(spread))
     arrived = exchange(part.reshape(peers, wets // 2, 2 * vectors))
     step = functools.partial(advance, total=total, peers=peers, ids=block_ids, rates=rates, fixed=fixed)
-    state, edges, wet_held, send = step("first", state=(arrived, below, above, base, in_hbm(start_block)))
+    state, edges, wet_held, send = step("first", state=(arrived, below, above, in_hbm(start_block)))
     inner = jnp.zeros((vectors, 2 * vectors), F32)
     unit = jnp.eye(vectors, dtype=F32)
     lag = jnp.concatenate([unit, unit], 1)

time: 265 us -> 265 us (level)
  local copies, waits for them, and re-layouts: 8.12 us -> 2.98 us
  Pallas kernels: 90.7 us -> 95.8 us
  waiting for transfers between devices: 66.1 us -> 69.9 us
  starting transfers between devices: 38.5 us -> 34.7 us
    pallas_call x1, Pallas kernels: 0.44 us -> 5.66 us  [by_owner(): pl.pallas_call(by_owner_kernel, grid=(n_col,), in_specs=[pl.BlockSpec((si...]
    unnamed x19 -> x13, local copies, waits for them, and re-layouts: 8.03 us -> 2.88 us
    all_to_all x1, waiting for transfers between devices: 25.4 us -> 30.1 us  [local(): mass = lax.all_to_all(blocks, 'col', 0, 0, tiled=True)]
    all_to_all x7, starting transfers between devices: 25.3 us -> 21.5 us  [exchange(): return lax.all_to_all(parts, AXES, 0, 0, tiled=True)]
    pallas_call x3 -> x2, Pallas kernels: 12.1 us -> 10.4 us  [the longest x1 9 us: combine(): pl.pallas_call(combine_kernel, grid=(block_rows,), in_specs=[SMEM, SMEM,...]
  transfers between devices with their start and end apart: 10 -> 10, of which waited for: 9 -> 8; matrix products, arithmetic and copies ran while one was open for 0% -> 0% of each run, Pallas kernels for 15% -> 15%
where the time goes in v3:
time: 265 us; the launch traced here: 264 us
  Pallas kernels  95.8 us (36%)
  waiting for transfers between devices  69.9 us (26%)
  blocking collectives  59.2 us (22%)
  starting transfers between devices  34.7 us (13%)
  local copies, waits for them, and re-layouts  2.98 us (1%)
    all_to_all x6, blocking collectives, exchange(): return lax.all_to_all(parts, AXES, 0, 0, tiled=True)  59.2 us
    pallas_call x6, Pallas kernels, advance(): pl.pallas_call(functools.partial(advance_kernel, mode, total, peers), in_...  44.7 us
    all_to_all x7, waiting for transfers between devices, exchange(): return lax.all_to_all(parts, AXES, 0, 0, tiled=True)  39.8 us
    all_to_all x1, waiting for transfers between devices, local(): mass = lax.all_to_all(blocks, 'col', 0, 0, tiled=True)  30.1 us
    pallas_call x5, Pallas kernels, factor(): pl.pallas_call(functools.partial(factor_kernel, total), in_specs=[VMEM] *...  21.9 us
    all_to_all x7, starting transfers between devices, exchange(): return lax.all_to_all(parts, AXES, 0, 0, tiled=True)  21.5 us
    pallas_call x1, Pallas kernels, combine(): pl.pallas_call(combine_kernel, grid=(block_rows,), in_specs=[SMEM, SMEM,...  9 us
    all_to_all x1, starting transfers between devices, local(): mass = lax.all_to_all(blocks, 'col', 0, 0, tiled=True)  7.4 us
  transfers between devices with their start and end apart: 10, of which 8 were waited for; matrix products, arithmetic and copies ran while one was open for 0% of the time, Pallas kernels for 15%

profile of v3, /device:TPU:0, one launch (start us, length us, event | category | flops | bytes accessed | tf_op | source)
XLA Modules:
  0.0 264.4 jit_solution(12391959012364380542)
XLA Ops:
  0.6 5.7 %by_owner.1 = bf16[8,128,1024]{2,1,0:T(8,128)(2,1)} custom-call(bf16[128,8192]{1,0:T(8,128)(2,1)} %mass.1), custom_call_target="tpu_custom_call" | custom-call | tf_op jit(solution)/shard_map/by_owner/pallas_call | solution.py:52
  6.3 0.0 copy-start.3
  6.3 0.0 copy-start.1
  6.3 0.0 copy-start.2
  6.3 0.0 copy-start.4
  6.3 7.4 %all-to-all-start = ((bf16[8,128,1024]{2,1,0:T(8,128)(2,1)}), bf16[8,128,1024]{2,1,0:T(8,128)(2,1)S(1)}, u32[]{:S(2)}, u32[]{:S(2)}) async-start(bf16[8,128,1024]{2,1,0:T(8,128)(2,1)} %by_owner.1), calls=%async_computation | async-start | bytes 4194304 | tf_op jit(solution)/shard_map/all_to_all | solution.py:697
  14.4 0.0 copy-done.3
  14.4 0.1 copy.10.wet
  14.5 0.0 copy-done.1
  14.5 0.0 copy-done.2
  14.5 0.0 copy-done.4
  14.5 0.0 copy-start
  14.5 2.8 %copy-done = bf16[3,16,4,128,128]{4,3,2,1,0:T(8,128)(2,1)S(1)} copy-done((bf16[3,16,4,128,128]{4,3,2,1,0:T(8,128)(2,1)S(1)}, bf16[3,16,4,128,128]{4,3,2,1,0:T(8,128)(2,1)}, u32[]{:S(2)}) %copy-start) | copy-done | bytes 6291480
  17.3 0.0 copy-start.5
  17.3 9.0 %combine.1 = (bf16[16,512,256]{2,1,0:T(8,128)(2,1)}, bf16[2048,128]{1,0:T(8,128)(2,1)S(1)}, bf16[32,2048]{1,0:T(8,128)(2,1)S(1)}, f32[64,128]{1,0:T(8,128)S(1)}, bf16[64,1024]{1,0:T(8,128)(2,1)S(1)}) custom-call(f32[2]{0:T(128)S(1)} %copy-done.2, s32[1]{0:T(128)S(6)} %copy.17.count, s32[1,128]{1,0:T(1,128)S(1)} %bitcast.13, s32[32,1]{1,0:T(8,128)S(1)} %copy.10.wet, ...), custom_call_target="tpu_custom_call" | custom-call | tf_op jit(solution)/shard_map/combine/pallas_call | solution.py:98
  26.3 1.3 collective-permute-start.1
  27.5 4.6 %collective-permute-start = (f32[64,128]{1,0:T(8,128)S(1)}, f32[64,128]{1,0:T(8,128)S(1)}, u32[]{:S(2)}, u32[]{:S(2)}) collective-permute-start(f32[64,128]{1,0:T(8,128)S(1)} %get-tuple-element.65), channel_id=1, source_target_pairs={{0,1},{1,2},{2,3},{3,4},{4,5},{5,6},{6,7},{7,8},{8,9},{9,10},{10,1... | collective-permute-start | bytes 98312 | tf_op jit(solution)/shard_map/ppermute | solution.py:690
  32.1 0.0 copy-done.5
  32.1 0.1 copy.16.refs_0_
  32.2 30.1 %all-to-all-done = bf16[8,128,1024]{2,1,0:T(8,128)(2,1)S(1)} async-done(((bf16[8,128,1024]{2,1,0:T(8,128)(2,1)}), bf16[8,128,1024]{2,1,0:T(8,128)(2,1)S(1)}, u32[]{:S(2)}, u32[]{:S(2)}) %all-to-all-start) | async-done | bytes 2097184 | tf_op jit(solution)/shard_map/all_to_all | solution.py:697
  62.3 1.4 start_pressure.1
  63.7 3.9 %all-to-all-start.1 = ((bf16[32,16,128]{2,1,0:T(8,128)(2,1)}), bf16[32,16,128]{2,1,0:T(8,128)(2,1)S(1)}, u32[]{:S(2)}, u32[]{:S(2)}) async-start(bf16[32,16,128]{2,1,0:T(8,128)(2,1)} %bitcast.4), calls=%async_computation.1 | async-start | bytes 262144 | tf_op jit(solution)/shard_map/all_to_all | solution.py:685
  67.7 6.4 %spread.1.refs_9_.refs_11_ = bf16[1024,2048]{1,0:T(8,128)(2,1)} custom-call(s32[1]{0:T(128)S(6)} %copy.17.count, s32[1,1024]{1,0:T(1,128)S(1)} %bitcast.12, bf16[8,4,2,16,1024]{4,3,2,1,0:T(8,128)(2,1)S(1)} %bitcast.9), custom_call_target="tpu_custom_call" | custom-call | flops 4294967296 | bytes 4194304 | tf_op jit(solution)/shard_map/spread/pallas_call | solution.py:181
  74.1 0.0 collective-permute-done.1.refs_4_
  74.1 0.0 collective-permute-done.refs_3_
  74.1 1.3 all-to-all-done.1.refs_2_
  75.4 6.9 %advance_first.1 = (bf16[384,2048]{1,0:T(8,128)(2,1)}, f32[128,256]{1,0:T(8,128)S(1)}, f32[32,128]{1,0:T(8,128)S(1)}, bf16[32,32,128]{2,1,0:T(8,128)(2,1)}) custom-call(s32[16,4]{1,0:T(8,128)S(1)} %copy.16.refs_0_, f32[2]{0:T(128)S(1)} %copy-done.2, bf16[32,16,128]{2,1,0:T(8,128)(2,1)S(1)} %all-to-all-done.1.refs_2_, ...), custom_call_target="tpu_custom_call" | custom-call | tf_op jit(solution)/shard_map/advance_first/pallas_call | solution.py:566
  82.3 4.6 %all-to-all-start.2 = ((bf16[32,32,128]{2,1,0:T(8,128)(2,1)}), bf16[32,32,128]{2,1,0:T(8,128)(2,1)S(1)}, u32[]{:S(2)}, u32[]{:S(2)}) async-start(bf16[32,32,128]{2,1,0:T(8,128)(2,1)} %get-tuple-element.69), calls=%async_computation.2 | async-start | bytes 524288 | tf_op jit(solution)/shard_map/all_to_all | solution.py:685
  86.9 0.1 add_convert_fusion._lag.refs_4_.lag
  86.9 10.6 %all-to-all-done.2.received = bf16[32,32,128]{2,1,0:T(8,128)(2,1)S(1)} async-done(((bf16[32,32,128]{2,1,0:T(8,128)(2,1)}), bf16[32,32,128]{2,1,0:T(8,128)(2,1)S(1)}, u32[]{:S(2)}, u32[]{:S(2)}) %all-to-all-start.2) | async-done | bytes 262176 | tf_op jit(solution)/shard_map/all_to_all | solution.py:685
  97.5 0.1 route.5
  97.6 9.9 %all_to_all.70.refs_2_ = f32[32,8,128]{2,1,0:T(8,128)S(1)} all-to-all(f32[32,8,128]{2,1,0:T(8,128)S(1)} %get-tuple-element.70), channel_id=1, replica_groups=mesh['row'=4,'col'=8] {'row','col'}, dimensions={0} | all-to-all | bytes 262144 | tf_op jit(solution)/shard_map/all_to_all | solution.py:685
  107.5 7.7 %advance_mid.4 = (bf16[384,2048]{1,0:T(8,128)(2,1)}, f32[128,256]{1,0:T(8,128)S(1)}, f32[32,128]{1,0:T(8,128)S(1)}, bf16[32,32,128]{2,1,0:T(8,128)(2,1)}, f32[64,128]{1,0:T(8,128)S(1)}, /*index=5*/f32[128,128]{1,0:T(8,128)S(1)}) custom-call(s32[16,4]{1,0:T(8,128)S(1)} %copy.16.refs_0_, f32[2]{0:T(128)S(1)} %copy-done.2, ...), custom_call_target="tpu_custom_call" | custom-call | tf_op jit(solution)/shard_map/advance_mid/pallas_call | solution.py:566
  115.2 2.6 all-to-all-start.4
  117.8 4.4 %factor.5 = (f32[64,128]{1,0:T(8,128)S(1)}, f32[64,128]{1,0:T(8,128)S(1)}, f32[3,64,64]{2,1,0:T(8,128)S(1)}) custom-call(f32[128,128]{1,0:T(8,128)S(1)} %get-tuple-element.76.gram, f32[64,128]{1,0:T(8,128)S(1)} %broadcast_in_dim.15.inner, f32[64,128]{1,0:T(8,128)S(1)} %add_convert_fusion._lag.refs_4_.lag, f32[64,128]{1,0:T(8,128)S(1)} %get-tuple-element.77.both), custom_call_target="tpu_custom_call" | custom-call | flops 100000000 | bytes 10000000 | tf_op jit(solution)/shard_map/factor/pallas_call | solution.py:352
  122.2 6.3 %all-to-all-done.4.received = bf16[32,32,128]{2,1,0:T(8,128)(2,1)S(1)} async-done(((bf16[32,32,128]{2,1,0:T(8,128)(2,1)}), bf16[32,32,128]{2,1,0:T(8,128)(2,1)S(1)}, u32[]{:S(2)}, u32[]{:S(2)}) %all-to-all-start.4) | async-done | bytes 262176 | tf_op jit(solution)/shard_map/all_to_all | solution.py:685
  128.5 0.1 route.6
  128.5 9.8 %all_to_all.71.refs_2_ = f32[32,8,128]{2,1,0:T(8,128)S(1)} all-to-all(f32[32,8,128]{2,1,0:T(8,128)S(1)} %get-tuple-element.79), channel_id=1, replica_groups=mesh['row'=4,'col'=8] {'row','col'}, dimensions={0} | all-to-all | bytes 262144 | tf_op jit(solution)/shard_map/all_to_all | solution.py:685
  138.3 7.7 %advance_mid.5 = (bf16[384,2048]{1,0:T(8,128)(2,1)}, f32[128,256]{1,0:T(8,128)S(1)}, f32[32,128]{1,0:T(8,128)S(1)}, bf16[32,32,128]{2,1,0:T(8,128)(2,1)}, f32[64,128]{1,0:T(8,128)S(1)}, /*index=5*/f32[128,128]{1,0:T(8,128)S(1)}) custom-call(s32[16,4]{1,0:T(8,128)S(1)} %copy.16.refs_0_, f32[2]{0:T(128)S(1)} %copy-done.2, ...), custom_call_target="tpu_custom_call" | custom-call | tf_op jit(solution)/shard_map/advance_mid/pallas_call | solution.py:566
  146.1 2.6 all-to-all-start.6
  148.7 4.4 %factor.6 = (f32[64,128]{1,0:T(8,128)S(1)}, f32[64,128]{1,0:T(8,128)S(1)}, f32[3,64,64]{2,1,0:T(8,128)S(1)}) custom-call(f32[128,128]{1,0:T(8,128)S(1)} %get-tuple-element.85.gram, f32[64,128]{1,0:T(8,128)S(1)} %get-tuple-element.86.inner, f32[64,128]{1,0:T(8,128)S(1)} %get-tuple-element.78._lag.refs_4_.lag, f32[64,128]{1,0:T(8,128)S(1)} %get-tuple-element.87.both), custom_call_target="tpu_custom_call" | custom-call | flops 100000000 | bytes 10000000 | tf_op jit(solution)/shard_map/factor/pallas_call | solution.py:352
  153.1 6.3 %all-to-all-done.6.received = bf16[32,32,128]{2,1,0:T(8,128)(2,1)S(1)} async-done(((bf16[32,32,128]{2,1,0:T(8,128)(2,1)}), bf16[32,32,128]{2,1,0:T(8,128)(2,1)S(1)}, u32[]{:S(2)}, u32[]{:S(2)}) %all-to-all-start.6) | async-done | bytes 262176 | tf_op jit(solution)/shard_map/all_to_all | solution.py:685
  159.3 0.1 route.7
  159.4 9.8 %all_to_all.72.refs_2_ = f32[32,8,128]{2,1,0:T(8,128)S(1)} all-to-all(f32[32,8,128]{2,1,0:T(8,128)S(1)} %get-tuple-element.89), channel_id=1, replica_groups=mesh['row'=4,'col'=8] {'row','col'}, dimensions={0} | all-to-all | bytes 262144 | tf_op jit(solution)/shard_map/all_to_all | solution.py:685
  169.2 7.7 %advance_mid.6 = (bf16[384,2048]{1,0:T(8,128)(2,1)}, f32[128,256]{1,0:T(8,128)S(1)}, f32[32,128]{1,0:T(8,128)S(1)}, bf16[32,32,128]{2,1,0:T(8,128)(2,1)}, f32[64,128]{1,0:T(8,128)S(1)}, /*index=5*/f32[128,128]{1,0:T(8,128)S(1)}) custom-call(s32[16,4]{1,0:T(8,128)S(1)} %copy.16.refs_0_, f32[2]{0:T(128)S(1)} %copy-done.2, ...), custom_call_target="tpu_custom_call" | custom-call | tf_op jit(solution)/shard_map/advance_mid/pallas_call | solution.py:566
  177.0 2.6 all-to-all-start.8
  179.6 4.4 %factor.7 = (f32[64,128]{1,0:T(8,128)S(1)}, f32[64,128]{1,0:T(8,128)S(1)}, f32[3,64,64]{2,1,0:T(8,128)S(1)}) custom-call(f32[128,128]{1,0:T(8,128)S(1)} %get-tuple-element.95.gram, f32[64,128]{1,0:T(8,128)S(1)} %get-tuple-element.96.inner, f32[64,128]{1,0:T(8,128)S(1)} %get-tuple-element.88._lag.refs_4_.lag, f32[64,128]{1,0:T(8,128)S(1)} %get-tuple-element.97.both), custom_call_target="tpu_custom_call" | custom-call | flops 100000000 | bytes 10000000 | tf_op jit(solution)/shard_map/factor/pallas_call | solution.py:352
  183.9 6.3 %all-to-all-done.8.received = bf16[32,32,128]{2,1,0:T(8,128)(2,1)S(1)} async-done(((bf16[32,32,128]{2,1,0:T(8,128)(2,1)}), bf16[32,32,128]{2,1,0:T(8,128)(2,1)S(1)}, u32[]{:S(2)}, u32[]{:S(2)}) %all-to-all-start.8) | async-done | bytes 262176 | tf_op jit(solution)/shard_map/all_to_all | solution.py:685
  190.2 0.1 route.8
  190.3 9.8 %all_to_all.73.refs_2_ = f32[32,8,128]{2,1,0:T(8,128)S(1)} all-to-all(f32[32,8,128]{2,1,0:T(8,128)S(1)} %get-tuple-element.99), channel_id=1, replica_groups=mesh['row'=4,'col'=8] {'row','col'}, dimensions={0} | all-to-all | bytes 262144 | tf_op jit(solution)/shard_map/all_to_all | solution.py:685
  200.1 7.7 %advance_mid.7 = (bf16[384,2048]{1,0:T(8,128)(2,1)}, f32[128,256]{1,0:T(8,128)S(1)}, f32[32,128]{1,0:T(8,128)S(1)}, bf16[32,32,128]{2,1,0:T(8,128)(2,1)}, f32[64,128]{1,0:T(8,128)S(1)}, /*index=5*/f32[128,128]{1,0:T(8,128)S(1)}) custom-call(s32[16,4]{1,0:T(8,128)S(1)} %copy.16.refs_0_, f32[2]{0:T(128)S(1)} %copy-done.2, ...), custom_call_target="tpu_custom_call" | custom-call | tf_op jit(solution)/shard_map/advance_mid/pallas_call | solution.py:566
  207.8 2.6 all-to-all-start.10
  210.5 4.4 %factor.8 = (f32[64,128]{1,0:T(8,128)S(1)}, f32[64,128]{1,0:T(8,128)S(1)}, f32[3,64,64]{2,1,0:T(8,128)S(1)}) custom-call(f32[128,128]{1,0:T(8,128)S(1)} %get-tuple-element.105.gram, f32[64,128]{1,0:T(8,128)S(1)} %get-tuple-element.106.inner, f32[64,128]{1,0:T(8,128)S(1)} %get-tuple-element.98._lag.refs_4_.lag, f32[64,128]{1,0:T(8,128)S(1)} %get-tuple-element.107.both), custom_call_target="tpu_custom_call" | custom-call | flops 100000000 | bytes 10000000 | tf_op jit(solution)/shard_map/factor/pallas_call | solution.py:352
  214.8 6.3 %all-to-all-done.10.received = bf16[32,32,128]{2,1,0:T(8,128)(2,1)S(1)} async-done(((bf16[32,32,128]{2,1,0:T(8,128)(2,1)}), bf16[32,32,128]{2,1,0:T(8,128)(2,1)S(1)}, u32[]{:S(2)}, u32[]{:S(2)}) %all-to-all-start.10) | async-done | bytes 262176 | tf_op jit(solution)/shard_map/all_to_all | solution.py:685
  221.1 0.1 route.9
  221.2 9.8 %all_to_all.74.refs_2_ = f32[32,8,128]{2,1,0:T(8,128)S(1)} all-to-all(f32[32,8,128]{2,1,0:T(8,128)S(1)} %get-tuple-element.109), channel_id=1, replica_groups=mesh['row'=4,'col'=8] {'row','col'}, dimensions={0} | all-to-all | bytes 262144 | tf_op jit(solution)/shard_map/all_to_all | solution.py:685
  231.0 6.9 %advance_last.1 = (bf16[384,2048]{1,0:T(8,128)(2,1)}, f32[128,128]{1,0:T(8,128)}, f32[64,128]{1,0:T(8,128)S(1)}, f32[128,128]{1,0:T(8,128)S(1)}) custom-call(s32[16,4]{1,0:T(8,128)S(1)} %copy.16.refs_0_, f32[2]{0:T(128)S(1)} %copy-done.2, f32[32,8,128]{2,1,0:T(8,128)S(1)} %all_to_all.74.refs_2_, f32[16,128]{1,0:T(8,128)S(1)} %get-tuple-element.110.refs_3_, ...), custom_call_target="tpu_custom_call" | custom-call | tf_op jit(solution)/shard_map/advance_last/pallas_call | solution.py:566
  237.9 2.6 all-to-all-start.12
  240.5 4.4 %factor.9 = (f32[64,128]{1,0:T(8,128)S(1)}, f32[64,128]{1,0:T(8,128)S(1)}, f32[3,64,64]{2,1,0:T(8,128)S(1)}) custom-call(f32[128,128]{1,0:T(8,128)S(1)} %get-tuple-element.115.gram, f32[64,128]{1,0:T(8,128)S(1)} %get-tuple-element.116.inner, f32[64,128]{1,0:T(8,128)S(1)} %get-tuple-element.108._lag.refs_4_.lag, f32[64,128]{1,0:T(8,128)S(1)} %get-tuple-element.117.both), custom_call_target="tpu_custom_call" | custom-call | flops 100000000 | bytes 10000000 | tf_op jit(solution)/shard_map/factor/pallas_call | solution.py:352
  244.9 2.9 %all-to-all-done.12.received = f32[32,4,128]{2,1,0:T(4,128)S(1)} async-done(((f32[32,4,128]{2,1,0:T(4,128)}), f32[32,4,128]{2,1,0:T(4,128)S(1)}, u32[]{:S(2)}, u32[]{:S(2)}) %all-to-all-start.12) | async-done | bytes 65568 | tf_op jit(solution)/shard_map/all_to_all | solution.py:685
  247.8 10.0 %all_to_all.75 = f32[32,4,128]{2,1,0:T(4,128)S(1)} all-to-all(f32[32,4,128]{2,1,0:T(4,128)S(1)} %repeat_sum.1), channel_id=1, replica_groups=mesh['row'=4,'col'=8] {'row','col'}, dimensions={0} | all-to-all | bytes 131072 | tf_op jit(solution)/shard_map/all_to_all | solution.py:685
  257.8 6.4 %finish.1 = (f32[64,2048]{1,0:T(8,128)}, f32[6,3,64,64]{3,2,1,0:T(8,128)}) custom-call(f32[128,128]{1,0:T(8,128)S(1)} %bitcast.10, f32[64,128]{1,0:T(8,128)S(1)} %get-tuple-element.119.inner, f32[64,128]{1,0:T(8,128)S(1)} %get-tuple-element.118._lag.lag, bf16[384,2048]{1,0:T(8,128)(2,1)} %get-tuple-element.120.state, ...), custom_call_target="tpu_custom_call" | custom-call | tf_op jit(solution)/shard_map/finish/pallas_call | solution.py:655
  (4 shorter events, 0.1 us)
Async XLA Ops:
  6.3 8.1 %copy-start.3 = (s32[1024]{0:T(1024)S(1)}, s32[1024]{0:T(1024)}, u32[]{:S(2)}) copy-start(s32[1024]{0:T(1024)} %param.12) | copy-start | bytes 12292
  6.3 8.2 %copy-start.1 = (f32[64,2048]{1,0:T(8,128)S(1)}, f32[64,2048]{1,0:T(8,128)}, u32[]{:S(2)}) copy-start(f32[64,2048]{1,0:T(8,128)} %refs_5_.1) | copy-start | bytes 1572868
  6.3 8.2 %copy-start.2 = (f32[2]{0:T(128)S(1)}, f32[2]{0:T(128)}, u32[]{:S(2)}) copy-start(f32[2]{0:T(128)} %refs_1_.11) | copy-start | bytes 28
  6.3 8.2 %copy-start.4 = (s32[128]{0:T(128)S(1)}, s32[128]{0:T(128)}, u32[]{:S(2)}) copy-start(s32[128]{0:T(128)} %param.11) | copy-start | bytes 1540
  6.3 56.0 %all-to-all-start = ((bf16[8,128,1024]{2,1,0:T(8,128)(2,1)}), bf16[8,128,1024]{2,1,0:T(8,128)(2,1)S(1)}, u32[]{:S(2)}, u32[]{:S(2)}) async-start(bf16[8,128,1024]{2,1,0:T(8,128)(2,1)} %by_owner.1), calls=%async_computation | async-start | bytes 4194304 | tf_op jit(solution)/shard_map/all_to_all | solution.py:697
  14.5 2.8 %copy-start = (bf16[3,16,4,128,128]{4,3,2,1,0:T(8,128)(2,1)S(1)}, bf16[3,16,4,128,128]{4,3,2,1,0:T(8,128)(2,1)}, u32[]{:S(2)}) copy-start(bf16[3,16,4,128,128]{4,3,2,1,0:T(8,128)(2,1)} %blocks.1) | copy-start | bytes 18874372
  17.3 14.9 %copy-start.5 = (s32[16,4]{0,1:T(4,128)S(1)}, s32[16,4]{0,1:T(4,128)}, u32[]{:S(2)}) copy-start(s32[16,4]{0,1:T(4,128)} %param.10) | copy-start | bytes 772
  26.3 47.8 %collective-permute-start.1 = (f32[64,128]{1,0:T(8,128)S(1)}, f32[64,128]{1,0:T(8,128)S(1)}, u32[]{:S(2)}, u32[]{:S(2)}) collective-permute-start(f32[64,128]{1,0:T(8,128)S(1)} %get-tuple-element.65), channel_id=1, source_target_pairs={{1,0},{2,1},{3,2},{4,3},{5,4},{6,5},{7,6},{8,7},{9,8},{10,9},{11,1... | collective-permute-start | bytes 98312 | tf_op jit(solution)/shard_map/ppermute | solution.py:690
  27.5 46.6 %collective-permute-start = (f32[64,128]{1,0:T(8,128)S(1)}, f32[64,128]{1,0:T(8,128)S(1)}, u32[]{:S(2)}, u32[]{:S(2)}) collective-permute-start(f32[64,128]{1,0:T(8,128)S(1)} %get-tuple-element.65), channel_id=1, source_target_pairs={{0,1},{1,2},{2,3},{3,4},{4,5},{5,6},{6,7},{7,8},{8,9},{9,10},{10,1... | collective-permute-start | bytes 98312 | tf_op jit(solution)/shard_map/ppermute | solution.py:690
  63.7 11.7 %all-to-all-start.1 = ((bf16[32,16,128]{2,1,0:T(8,128)(2,1)}), bf16[32,16,128]{2,1,0:T(8,128)(2,1)S(1)}, u32[]{:S(2)}, u32[]{:S(2)}) async-start(bf16[32,16,128]{2,1,0:T(8,128)(2,1)} %bitcast.4), calls=%async_computation.1 | async-start | bytes 262144 | tf_op jit(solution)/shard_map/all_to_all | solution.py:685
  82.3 15.2 %all-to-all-start.2 = ((bf16[32,32,128]{2,1,0:T(8,128)(2,1)}), bf16[32,32,128]{2,1,0:T(8,128)(2,1)S(1)}, u32[]{:S(2)}, u32[]{:S(2)}) async-start(bf16[32,32,128]{2,1,0:T(8,128)(2,1)} %get-tuple-element.69), calls=%async_computation.2 | async-start | bytes 524288 | tf_op jit(solution)/shard_map/all_to_all | solution.py:685
  115.2 13.3 %all-to-all-start.4 = ((bf16[32,32,128]{2,1,0:T(8,128)(2,1)}), bf16[32,32,128]{2,1,0:T(8,128)(2,1)S(1)}, u32[]{:S(2)}, u32[]{:S(2)}) async-start(bf16[32,32,128]{2,1,0:T(8,128)(2,1)} %get-tuple-element.75), calls=%async_computation.4 | async-start | bytes 524288 | tf_op jit(solution)/shard_map/all_to_all | solution.py:685
  146.1 13.3 %all-to-all-start.6 = ((bf16[32,32,128]{2,1,0:T(8,128)(2,1)}), bf16[32,32,128]{2,1,0:T(8,128)(2,1)S(1)}, u32[]{:S(2)}, u32[]{:S(2)}) async-start(bf16[32,32,128]{2,1,0:T(8,128)(2,1)} %get-tuple-element.84), calls=%async_computation.6 | async-start | bytes 524288 | tf_op jit(solution)/shard_map/all_to_all | solution.py:685
  177.0 13.3 %all-to-all-start.8 = ((bf16[32,32,128]{2,1,0:T(8,128)(2,1)}), bf16[32,32,128]{2,1,0:T(8,128)(2,1)S(1)}, u32[]{:S(2)}, u32[]{:S(2)}) async-start(bf16[32,32,128]{2,1,0:T(8,128)(2,1)} %get-tuple-element.94), calls=%async_computation.8 | async-start | bytes 524288 | tf_op jit(solution)/shard_map/all_to_all | solution.py:685
  207.8 13.3 %all-to-all-start.10 = ((bf16[32,32,128]{2,1,0:T(8,128)(2,1)}), bf16[32,32,128]{2,1,0:T(8,128)(2,1)S(1)}, u32[]{:S(2)}, u32[]{:S(2)}) async-start(bf16[32,32,128]{2,1,0:T(8,128)(2,1)} %get-tuple-element.104), calls=%async_computation.10 | async-start | bytes 524288 | tf_op jit(solution)/shard_map/all_to_all | solution.py:685
  237.9 9.9 %all-to-all-start.12 = ((f32[32,4,128]{2,1,0:T(4,128)}), f32[32,4,128]{2,1,0:T(4,128)S(1)}, u32[]{:S(2)}, u32[]{:S(2)}) async-start(f32[32,4,128]{2,1,0:T(4,128)} %bitcast.5), calls=%async_computation.12 | async-start | bytes 131072 | tf_op jit(solution)/shard_map/all_to_all | solution.py:685

commit v4 on v3

--- a/solution.py
+++ b/solution.py
@@ -43,18 +43,28 @@
     return high, (values - high.astype(F32)).astype(BF16)
 
 
-def by_owner_kernel(mass, out):
-    out[0] = mass[...]
+def by_owner_kernel(mass, out, held, sems):
+    wcap = out.shape[2]
+    reads, writes = [], []
+    for c in range(out.shape[0]):
+        reads.append(pltpu.make_async_copy(mass.at[:, pl.ds(c * wcap, wcap)], held.at[c], sems.at[0, c]))
+        writes.append(pltpu.make_async_copy(held.at[c], out.at[c], sems.at[1, c]))
+        reads[-1].start()
+    for read, write in zip(reads, writes):
+        read.wait()
+        write.start()
+    for write in writes:
+        write.wait()
 
 
 def by_owner(mass, n_col, wcap):
-    size = mass.shape[0]
+    shape = (n_col, mass.shape[0], wcap)
     return pl.pallas_call(
         by_owner_kernel,
-        grid=(n_col,),
-        in_specs=[pl.BlockSpec((size, wcap), lambda c: (0, c))],
-        out_specs=pl.BlockSpec((1, size, wcap), lambda c: (c, 0, 0)),
-        out_shape=pltpu.HBM((n_col, size, wcap), BF16),
+        in_specs=[HBM],
+        out_specs=HBM,
+        out_shape=pltpu.HBM(shape, BF16),
+        scratch_shapes=[pltpu.VMEM(shape, BF16), pltpu.SemaphoreType.DMA((2, n_col))],
         compiler_params=pltpu.CompilerParams(vmem_limit_bytes=LIMIT),
         name="by_owner",
     )(mass)

time: 265 us -> 262 us (0.989)
  Pallas kernels: 95.8 us -> 92.6 us
    pallas_call x1, Pallas kernels: 5.66 us -> 2.48 us  [by_owner(): pl.pallas_call(by_owner_kernel, in_specs=[HBM], out_specs=HBM, out_shape=...]
where the time goes in v4:
time: 262 us; the launch traced here: 261 us
  Pallas kernels  92.6 us (35%)
  waiting for transfers between devices  69.9 us (27%)
  blocking collectives  59.2 us (23%)
  starting transfers between devices  34.7 us (13%)
  local copies, waits for them, and re-layouts  2.99 us (1%)
    all_to_all x6, blocking collectives, exchange(): return lax.all_to_all(parts, AXES, 0, 0, tiled=True)  59.2 us
    pallas_call x6, Pallas kernels, advance(): pl.pallas_call(functools.partial(advance_kernel, mode, total, peers), in_...  44.7 us
    all_to_all x7, waiting for transfers between devices, exchange(): return lax.all_to_all(parts, AXES, 0, 0, tiled=True)  39.8 us
    all_to_all x1, waiting for transfers between devices, local(): mass = lax.all_to_all(blocks, 'col', 0, 0, tiled=True)  30.1 us
    pallas_call x5, Pallas kernels, factor(): pl.pallas_call(functools.partial(factor_kernel, total), in_specs=[VMEM] *...  21.9 us
    all_to_all x7, starting transfers between devices, exchange(): return lax.all_to_all(parts, AXES, 0, 0, tiled=True)  21.5 us
    pallas_call x1, Pallas kernels, combine(): pl.pallas_call(combine_kernel, grid=(block_rows,), in_specs=[SMEM, SMEM,...  9 us
    all_to_all x1, starting transfers between devices, local(): mass = lax.all_to_all(blocks, 'col', 0, 0, tiled=True)  7.4 us
  transfers between devices with their start and end apart: 10, of which 8 were waited for; matrix products, arithmetic and copies ran while one was open for 0% of the time, Pallas kernels for 15%

profile of v4, /device:TPU:0, one launch (start us, length us, event | category | flops | bytes accessed | tf_op | source)
XLA Modules:
  0.0 261.2 jit_solution(1959721182357078556)
XLA Ops:
  0.6 2.5 by_owner.1
  3.1 0.0 copy-start.3
  3.1 0.0 copy-start.1
  3.1 0.0 copy-start.2
  3.1 0.0 copy-start.4
  3.2 7.4 %all-to-all-start = ((bf16[8,128,1024]{2,1,0:T(8,128)(2,1)}), bf16[8,128,1024]{2,1,0:T(8,128)(2,1)S(1)}, u32[]{:S(2)}, u32[]{:S(2)}) async-start(bf16[8,128,1024]{2,1,0:T(8,128)(2,1)} %by_owner.1), calls=%async_computation | async-start | bytes 4194304 | tf_op jit(solution)/shard_map/all_to_all | solution.py:707
  11.2 0.0 copy-done.3
  11.2 0.1 copy.10.wet
  11.3 0.0 copy-done.1
  11.3 0.0 copy-done.2
  11.3 0.0 copy-done.4
  11.3 0.0 copy-start
  11.3 2.8 %copy-done = bf16[3,16,4,128,128]{4,3,2,1,0:T(8,128)(2,1)S(1)} copy-done((bf16[3,16,4,128,128]{4,3,2,1,0:T(8,128)(2,1)S(1)}, bf16[3,16,4,128,128]{4,3,2,1,0:T(8,128)(2,1)}, u32[]{:S(2)}) %copy-start) | copy-done | bytes 6291480
  14.1 0.0 copy-start.5
  14.1 9.0 %combine.1 = (bf16[16,512,256]{2,1,0:T(8,128)(2,1)}, bf16[2048,128]{1,0:T(8,128)(2,1)S(1)}, bf16[32,2048]{1,0:T(8,128)(2,1)S(1)}, f32[64,128]{1,0:T(8,128)S(1)}, bf16[64,1024]{1,0:T(8,128)(2,1)S(1)}) custom-call(f32[2]{0:T(128)S(1)} %copy-done.2, s32[1]{0:T(128)S(6)} %copy.17.count, s32[1,128]{1,0:T(1,128)S(1)} %bitcast.13, s32[32,1]{1,0:T(8,128)S(1)} %copy.10.wet, ...), custom_call_target="tpu_custom_call" | custom-call | tf_op jit(solution)/shard_map/combine/pallas_call | solution.py:108
  23.1 1.3 collective-permute-start.1
  24.4 4.6 %collective-permute-start = (f32[64,128]{1,0:T(8,128)S(1)}, f32[64,128]{1,0:T(8,128)S(1)}, u32[]{:S(2)}, u32[]{:S(2)}) collective-permute-start(f32[64,128]{1,0:T(8,128)S(1)} %get-tuple-element.65), channel_id=1, source_target_pairs={{0,1},{1,2},{2,3},{3,4},{4,5},{5,6},{6,7},{7,8},{8,9},{9,10},{10,1... | collective-permute-start | bytes 98312 | tf_op jit(solution)/shard_map/ppermute | solution.py:700
  29.0 0.0 copy-done.5
  29.0 0.1 copy.16.refs_0_
  29.1 30.1 %all-to-all-done = bf16[8,128,1024]{2,1,0:T(8,128)(2,1)S(1)} async-done(((bf16[8,128,1024]{2,1,0:T(8,128)(2,1)}), bf16[8,128,1024]{2,1,0:T(8,128)(2,1)S(1)}, u32[]{:S(2)}, u32[]{:S(2)}) %all-to-all-start) | async-done | bytes 2097184 | tf_op jit(solution)/shard_map/all_to_all | solution.py:707
  59.1 1.4 start_pressure.1
  60.6 3.9 %all-to-all-start.1 = ((bf16[32,16,128]{2,1,0:T(8,128)(2,1)}), bf16[32,16,128]{2,1,0:T(8,128)(2,1)S(1)}, u32[]{:S(2)}, u32[]{:S(2)}) async-start(bf16[32,16,128]{2,1,0:T(8,128)(2,1)} %bitcast.4), calls=%async_computation.1 | async-start | bytes 262144 | tf_op jit(solution)/shard_map/all_to_all | solution.py:695
  64.5 6.4 %spread.1.refs_9_.refs_11_ = bf16[1024,2048]{1,0:T(8,128)(2,1)} custom-call(s32[1]{0:T(128)S(6)} %copy.17.count, s32[1,1024]{1,0:T(1,128)S(1)} %bitcast.12, bf16[8,4,2,16,1024]{4,3,2,1,0:T(8,128)(2,1)S(1)} %bitcast.9), custom_call_target="tpu_custom_call" | custom-call | flops 4294967296 | bytes 4194304 | tf_op jit(solution)/shard_map/spread/pallas_call | solution.py:191
  70.9 0.0 collective-permute-done.1.refs_4_
  70.9 0.0 collective-permute-done.refs_3_
  71.0 1.3 all-to-all-done.1.refs_2_
  72.3 6.9 %advance_first.1 = (bf16[384,2048]{1,0:T(8,128)(2,1)}, f32[128,256]{1,0:T(8,128)S(1)}, f32[32,128]{1,0:T(8,128)S(1)}, bf16[32,32,128]{2,1,0:T(8,128)(2,1)}) custom-call(s32[16,4]{1,0:T(8,128)S(1)} %copy.16.refs_0_, f32[2]{0:T(128)S(1)} %copy-done.2, bf16[32,16,128]{2,1,0:T(8,128)(2,1)S(1)} %all-to-all-done.1.refs_2_, ...), custom_call_target="tpu_custom_call" | custom-call | tf_op jit(solution)/shard_map/advance_first/pallas_call | solution.py:576
  79.1 4.6 %all-to-all-start.2 = ((bf16[32,32,128]{2,1,0:T(8,128)(2,1)}), bf16[32,32,128]{2,1,0:T(8,128)(2,1)S(1)}, u32[]{:S(2)}, u32[]{:S(2)}) async-start(bf16[32,32,128]{2,1,0:T(8,128)(2,1)} %get-tuple-element.69), calls=%async_computation.2 | async-start | bytes 524288 | tf_op jit(solution)/shard_map/all_to_all | solution.py:695
  83.7 0.1 add_convert_fusion._lag.refs_4_.lag
  83.8 10.6 %all-to-all-done.2.received = bf16[32,32,128]{2,1,0:T(8,128)(2,1)S(1)} async-done(((bf16[32,32,128]{2,1,0:T(8,128)(2,1)}), bf16[32,32,128]{2,1,0:T(8,128)(2,1)S(1)}, u32[]{:S(2)}, u32[]{:S(2)}) %all-to-all-start.2) | async-done | bytes 262176 | tf_op jit(solution)/shard_map/all_to_all | solution.py:695
  94.3 0.1 route.5
  94.4 9.9 %all_to_all.70.refs_2_ = f32[32,8,128]{2,1,0:T(8,128)S(1)} all-to-all(f32[32,8,128]{2,1,0:T(8,128)S(1)} %get-tuple-element.70), channel_id=1, replica_groups=mesh['row'=4,'col'=8] {'row','col'}, dimensions={0} | all-to-all | bytes 262144 | tf_op jit(solution)/shard_map/all_to_all | solution.py:695
  104.3 7.7 %advance_mid.4 = (bf16[384,2048]{1,0:T(8,128)(2,1)}, f32[128,256]{1,0:T(8,128)S(1)}, f32[32,128]{1,0:T(8,128)S(1)}, bf16[32,32,128]{2,1,0:T(8,128)(2,1)}, f32[64,128]{1,0:T(8,128)S(1)}, /*index=5*/f32[128,128]{1,0:T(8,128)S(1)}) custom-call(s32[16,4]{1,0:T(8,128)S(1)} %copy.16.refs_0_, f32[2]{0:T(128)S(1)} %copy-done.2, ...), custom_call_target="tpu_custom_call" | custom-call | tf_op jit(solution)/shard_map/advance_mid/pallas_call | solution.py:576
  112.1 2.6 all-to-all-start.4
  114.7 4.4 %factor.5 = (f32[64,128]{1,0:T(8,128)S(1)}, f32[64,128]{1,0:T(8,128)S(1)}, f32[3,64,64]{2,1,0:T(8,128)S(1)}) custom-call(f32[128,128]{1,0:T(8,128)S(1)} %get-tuple-element.76.gram, f32[64,128]{1,0:T(8,128)S(1)} %broadcast_in_dim.15.inner, f32[64,128]{1,0:T(8,128)S(1)} %add_convert_fusion._lag.refs_4_.lag, f32[64,128]{1,0:T(8,128)S(1)} %get-tuple-element.77.both), custom_call_target="tpu_custom_call" | custom-call | flops 100000000 | bytes 10000000 | tf_op jit(solution)/shard_map/factor/pallas_call | solution.py:362
  119.1 6.3 %all-to-all-done.4.received = bf16[32,32,128]{2,1,0:T(8,128)(2,1)S(1)} async-done(((bf16[32,32,128]{2,1,0:T(8,128)(2,1)}), bf16[32,32,128]{2,1,0:T(8,128)(2,1)S(1)}, u32[]{:S(2)}, u32[]{:S(2)}) %all-to-all-start.4) | async-done | bytes 262176 | tf_op jit(solution)/shard_map/all_to_all | solution.py:695
  125.3 0.1 route.6
  125.4 9.8 %all_to_all.71.refs_2_ = f32[32,8,128]{2,1,0:T(8,128)S(1)} all-to-all(f32[32,8,128]{2,1,0:T(8,128)S(1)} %get-tuple-element.79), channel_id=1, replica_groups=mesh['row'=4,'col'=8] {'row','col'}, dimensions={0} | all-to-all | bytes 262144 | tf_op jit(solution)/shard_map/all_to_all | solution.py:695
  135.2 7.7 %advance_mid.5 = (bf16[384,2048]{1,0:T(8,128)(2,1)}, f32[128,256]{1,0:T(8,128)S(1)}, f32[32,128]{1,0:T(8,128)S(1)}, bf16[32,32,128]{2,1,0:T(8,128)(2,1)}, f32[64,128]{1,0:T(8,128)S(1)}, /*index=5*/f32[128,128]{1,0:T(8,128)S(1)}) custom-call(s32[16,4]{1,0:T(8,128)S(1)} %copy.16.refs_0_, f32[2]{0:T(128)S(1)} %copy-done.2, ...), custom_call_target="tpu_custom_call" | custom-call | tf_op jit(solution)/shard_map/advance_mid/pallas_call | solution.py:576
  142.9 2.6 all-to-all-start.6
  145.5 4.4 %factor.6 = (f32[64,128]{1,0:T(8,128)S(1)}, f32[64,128]{1,0:T(8,128)S(1)}, f32[3,64,64]{2,1,0:T(8,128)S(1)}) custom-call(f32[128,128]{1,0:T(8,128)S(1)} %get-tuple-element.85.gram, f32[64,128]{1,0:T(8,128)S(1)} %get-tuple-element.86.inner, f32[64,128]{1,0:T(8,128)S(1)} %get-tuple-element.78._lag.refs_4_.lag, f32[64,128]{1,0:T(8,128)S(1)} %get-tuple-element.87.both), custom_call_target="tpu_custom_call" | custom-call | flops 100000000 | bytes 10000000 | tf_op jit(solution)/shard_map/factor/pallas_call | solution.py:362
  149.9 6.3 %all-to-all-done.6.received = bf16[32,32,128]{2,1,0:T(8,128)(2,1)S(1)} async-done(((bf16[32,32,128]{2,1,0:T(8,128)(2,1)}), bf16[32,32,128]{2,1,0:T(8,128)(2,1)S(1)}, u32[]{:S(2)}, u32[]{:S(2)}) %all-to-all-start.6) | async-done | bytes 262176 | tf_op jit(solution)/shard_map/all_to_all | solution.py:695
  156.2 0.1 route.7
  156.3 9.8 %all_to_all.72.refs_2_ = f32[32,8,128]{2,1,0:T(8,128)S(1)} all-to-all(f32[32,8,128]{2,1,0:T(8,128)S(1)} %get-tuple-element.89), channel_id=1, replica_groups=mesh['row'=4,'col'=8] {'row','col'}, dimensions={0} | all-to-all | bytes 262144 | tf_op jit(solution)/shard_map/all_to_all | solution.py:695
  166.1 7.7 %advance_mid.6 = (bf16[384,2048]{1,0:T(8,128)(2,1)}, f32[128,256]{1,0:T(8,128)S(1)}, f32[32,128]{1,0:T(8,128)S(1)}, bf16[32,32,128]{2,1,0:T(8,128)(2,1)}, f32[64,128]{1,0:T(8,128)S(1)}, /*index=5*/f32[128,128]{1,0:T(8,128)S(1)}) custom-call(s32[16,4]{1,0:T(8,128)S(1)} %copy.16.refs_0_, f32[2]{0:T(128)S(1)} %copy-done.2, ...), custom_call_target="tpu_custom_call" | custom-call | tf_op jit(solution)/shard_map/advance_mid/pallas_call | solution.py:576
  173.8 2.6 all-to-all-start.8
  176.4 4.4 %factor.7 = (f32[64,128]{1,0:T(8,128)S(1)}, f32[64,128]{1,0:T(8,128)S(1)}, f32[3,64,64]{2,1,0:T(8,128)S(1)}) custom-call(f32[128,128]{1,0:T(8,128)S(1)} %get-tuple-element.95.gram, f32[64,128]{1,0:T(8,128)S(1)} %get-tuple-element.96.inner, f32[64,128]{1,0:T(8,128)S(1)} %get-tuple-element.88._lag.refs_4_.lag, f32[64,128]{1,0:T(8,128)S(1)} %get-tuple-element.97.both), custom_call_target="tpu_custom_call" | custom-call | flops 100000000 | bytes 10000000 | tf_op jit(solution)/shard_map/factor/pallas_call | solution.py:362
  180.8 6.3 %all-to-all-done.8.received = bf16[32,32,128]{2,1,0:T(8,128)(2,1)S(1)} async-done(((bf16[32,32,128]{2,1,0:T(8,128)(2,1)}), bf16[32,32,128]{2,1,0:T(8,128)(2,1)S(1)}, u32[]{:S(2)}, u32[]{:S(2)}) %all-to-all-start.8) | async-done | bytes 262176 | tf_op jit(solution)/shard_map/all_to_all | solution.py:695
  187.1 0.1 route.8
  187.1 9.8 %all_to_all.73.refs_2_ = f32[32,8,128]{2,1,0:T(8,128)S(1)} all-to-all(f32[32,8,128]{2,1,0:T(8,128)S(1)} %get-tuple-element.99), channel_id=1, replica_groups=mesh['row'=4,'col'=8] {'row','col'}, dimensions={0} | all-to-all | bytes 262144 | tf_op jit(solution)/shard_map/all_to_all | solution.py:695
  197.0 7.7 %advance_mid.7 = (bf16[384,2048]{1,0:T(8,128)(2,1)}, f32[128,256]{1,0:T(8,128)S(1)}, f32[32,128]{1,0:T(8,128)S(1)}, bf16[32,32,128]{2,1,0:T(8,128)(2,1)}, f32[64,128]{1,0:T(8,128)S(1)}, /*index=5*/f32[128,128]{1,0:T(8,128)S(1)}) custom-call(s32[16,4]{1,0:T(8,128)S(1)} %copy.16.refs_0_, f32[2]{0:T(128)S(1)} %copy-done.2, ...), custom_call_target="tpu_custom_call" | custom-call | tf_op jit(solution)/shard_map/advance_mid/pallas_call | solution.py:576
  204.7 2.6 all-to-all-start.10
  207.3 4.4 %factor.8 = (f32[64,128]{1,0:T(8,128)S(1)}, f32[64,128]{1,0:T(8,128)S(1)}, f32[3,64,64]{2,1,0:T(8,128)S(1)}) custom-call(f32[128,128]{1,0:T(8,128)S(1)} %get-tuple-element.105.gram, f32[64,128]{1,0:T(8,128)S(1)} %get-tuple-element.106.inner, f32[64,128]{1,0:T(8,128)S(1)} %get-tuple-element.98._lag.refs_4_.lag, f32[64,128]{1,0:T(8,128)S(1)} %get-tuple-element.107.both), custom_call_target="tpu_custom_call" | custom-call | flops 100000000 | bytes 10000000 | tf_op jit(solution)/shard_map/factor/pallas_call | solution.py:362
  211.7 6.3 %all-to-all-done.10.received = bf16[32,32,128]{2,1,0:T(8,128)(2,1)S(1)} async-done(((bf16[32,32,128]{2,1,0:T(8,128)(2,1)}), bf16[32,32,128]{2,1,0:T(8,128)(2,1)S(1)}, u32[]{:S(2)}, u32[]{:S(2)}) %all-to-all-start.10) | async-done | bytes 262176 | tf_op jit(solution)/shard_map/all_to_all | solution.py:695
  218.0 0.1 route.9
  218.0 9.8 %all_to_all.74.refs_2_ = f32[32,8,128]{2,1,0:T(8,128)S(1)} all-to-all(f32[32,8,128]{2,1,0:T(8,128)S(1)} %get-tuple-element.109), channel_id=1, replica_groups=mesh['row'=4,'col'=8] {'row','col'}, dimensions={0} | all-to-all | bytes 262144 | tf_op jit(solution)/shard_map/all_to_all | solution.py:695
  227.8 6.9 %advance_last.1 = (bf16[384,2048]{1,0:T(8,128)(2,1)}, f32[128,128]{1,0:T(8,128)}, f32[64,128]{1,0:T(8,128)S(1)}, f32[128,128]{1,0:T(8,128)S(1)}) custom-call(s32[16,4]{1,0:T(8,128)S(1)} %copy.16.refs_0_, f32[2]{0:T(128)S(1)} %copy-done.2, f32[32,8,128]{2,1,0:T(8,128)S(1)} %all_to_all.74.refs_2_, f32[16,128]{1,0:T(8,128)S(1)} %get-tuple-element.110.refs_3_, ...), custom_call_target="tpu_custom_call" | custom-call | tf_op jit(solution)/shard_map/advance_last/pallas_call | solution.py:576
  234.7 2.6 all-to-all-start.12
  237.3 4.4 %factor.9 = (f32[64,128]{1,0:T(8,128)S(1)}, f32[64,128]{1,0:T(8,128)S(1)}, f32[3,64,64]{2,1,0:T(8,128)S(1)}) custom-call(f32[128,128]{1,0:T(8,128)S(1)} %get-tuple-element.115.gram, f32[64,128]{1,0:T(8,128)S(1)} %get-tuple-element.116.inner, f32[64,128]{1,0:T(8,128)S(1)} %get-tuple-element.108._lag.refs_4_.lag, f32[64,128]{1,0:T(8,128)S(1)} %get-tuple-element.117.both), custom_call_target="tpu_custom_call" | custom-call | flops 100000000 | bytes 10000000 | tf_op jit(solution)/shard_map/factor/pallas_call | solution.py:362
  241.7 2.9 %all-to-all-done.12.received = f32[32,4,128]{2,1,0:T(4,128)S(1)} async-done(((f32[32,4,128]{2,1,0:T(4,128)}), f32[32,4,128]{2,1,0:T(4,128)S(1)}, u32[]{:S(2)}, u32[]{:S(2)}) %all-to-all-start.12) | async-done | bytes 65568 | tf_op jit(solution)/shard_map/all_to_all | solution.py:695
  244.7 10.0 %all_to_all.75 = f32[32,4,128]{2,1,0:T(4,128)S(1)} all-to-all(f32[32,4,128]{2,1,0:T(4,128)S(1)} %repeat_sum.1), channel_id=1, replica_groups=mesh['row'=4,'col'=8] {'row','col'}, dimensions={0} | all-to-all | bytes 131072 | tf_op jit(solution)/shard_map/all_to_all | solution.py:695
  254.7 6.4 %finish.1 = (f32[64,2048]{1,0:T(8,128)}, f32[6,3,64,64]{3,2,1,0:T(8,128)}) custom-call(f32[128,128]{1,0:T(8,128)S(1)} %bitcast.10, f32[64,128]{1,0:T(8,128)S(1)} %get-tuple-element.119.inner, f32[64,128]{1,0:T(8,128)S(1)} %get-tuple-element.118._lag.lag, bf16[384,2048]{1,0:T(8,128)(2,1)} %get-tuple-element.120.state, ...), custom_call_target="tpu_custom_call" | custom-call | tf_op jit(solution)/shard_map/finish/pallas_call | solution.py:665
  (4 shorter events, 0.1 us)
Async XLA Ops:
  3.1 8.1 %copy-start.3 = (s32[1024]{0:T(1024)S(1)}, s32[1024]{0:T(1024)}, u32[]{:S(2)}) copy-start(s32[1024]{0:T(1024)} %param.12) | copy-start | bytes 12292
  3.1 8.2 %copy-start.1 = (f32[64,2048]{1,0:T(8,128)S(1)}, f32[64,2048]{1,0:T(8,128)}, u32[]{:S(2)}) copy-start(f32[64,2048]{1,0:T(8,128)} %refs_5_.1) | copy-start | bytes 1572868
  3.1 8.2 %copy-start.2 = (f32[2]{0:T(128)S(1)}, f32[2]{0:T(128)}, u32[]{:S(2)}) copy-start(f32[2]{0:T(128)} %refs_1_.11) | copy-start | bytes 28
  3.1 8.2 %copy-start.4 = (s32[128]{0:T(128)S(1)}, s32[128]{0:T(128)}, u32[]{:S(2)}) copy-start(s32[128]{0:T(128)} %param.11) | copy-start | bytes 1540
  3.2 56.0 %all-to-all-start = ((bf16[8,128,1024]{2,1,0:T(8,128)(2,1)}), bf16[8,128,1024]{2,1,0:T(8,128)(2,1)S(1)}, u32[]{:S(2)}, u32[]{:S(2)}) async-start(bf16[8,128,1024]{2,1,0:T(8,128)(2,1)} %by_owner.1), calls=%async_computation | async-start | bytes 4194304 | tf_op jit(solution)/shard_map/all_to_all | solution.py:707
  11.3 2.8 %copy-start = (bf16[3,16,4,128,128]{4,3,2,1,0:T(8,128)(2,1)S(1)}, bf16[3,16,4,128,128]{4,3,2,1,0:T(8,128)(2,1)}, u32[]{:S(2)}) copy-start(bf16[3,16,4,128,128]{4,3,2,1,0:T(8,128)(2,1)} %blocks.1) | copy-start | bytes 18874372
  14.1 14.9 %copy-start.5 = (s32[16,4]{0,1:T(4,128)S(1)}, s32[16,4]{0,1:T(4,128)}, u32[]{:S(2)}) copy-start(s32[16,4]{0,1:T(4,128)} %param.10) | copy-start | bytes 772
  23.1 47.8 %collective-permute-start.1 = (f32[64,128]{1,0:T(8,128)S(1)}, f32[64,128]{1,0:T(8,128)S(1)}, u32[]{:S(2)}, u32[]{:S(2)}) collective-permute-start(f32[64,128]{1,0:T(8,128)S(1)} %get-tuple-element.65), channel_id=1, source_target_pairs={{1,0},{2,1},{3,2},{4,3},{5,4},{6,5},{7,6},{8,7},{9,8},{10,9},{11,1... | collective-permute-start | bytes 98312 | tf_op jit(solution)/shard_map/ppermute | solution.py:700
  24.4 46.5 %collective-permute-start = (f32[64,128]{1,0:T(8,128)S(1)}, f32[64,128]{1,0:T(8,128)S(1)}, u32[]{:S(2)}, u32[]{:S(2)}) collective-permute-start(f32[64,128]{1,0:T(8,128)S(1)} %get-tuple-element.65), channel_id=1, source_target_pairs={{0,1},{1,2},{2,3},{3,4},{4,5},{5,6},{6,7},{7,8},{8,9},{9,10},{10,1... | collective-permute-start | bytes 98312 | tf_op jit(solution)/shard_map/ppermute | solution.py:700
  60.6 11.7 %all-to-all-start.1 = ((bf16[32,16,128]{2,1,0:T(8,128)(2,1)}), bf16[32,16,128]{2,1,0:T(8,128)(2,1)S(1)}, u32[]{:S(2)}, u32[]{:S(2)}) async-start(bf16[32,16,128]{2,1,0:T(8,128)(2,1)} %bitcast.4), calls=%async_computation.1 | async-start | bytes 262144 | tf_op jit(solution)/shard_map/all_to_all | solution.py:695
  79.1 15.2 %all-to-all-start.2 = ((bf16[32,32,128]{2,1,0:T(8,128)(2,1)}), bf16[32,32,128]{2,1,0:T(8,128)(2,1)S(1)}, u32[]{:S(2)}, u32[]{:S(2)}) async-start(bf16[32,32,128]{2,1,0:T(8,128)(2,1)} %get-tuple-element.69), calls=%async_computation.2 | async-start | bytes 524288 | tf_op jit(solution)/shard_map/all_to_all | solution.py:695
  112.1 13.3 %all-to-all-start.4 = ((bf16[32,32,128]{2,1,0:T(8,128)(2,1)}), bf16[32,32,128]{2,1,0:T(8,128)(2,1)S(1)}, u32[]{:S(2)}, u32[]{:S(2)}) async-start(bf16[32,32,128]{2,1,0:T(8,128)(2,1)} %get-tuple-element.75), calls=%async_computation.4 | async-start | bytes 524288 | tf_op jit(solution)/shard_map/all_to_all | solution.py:695
  142.9 13.3 %all-to-all-start.6 = ((bf16[32,32,128]{2,1,0:T(8,128)(2,1)}), bf16[32,32,128]{2,1,0:T(8,128)(2,1)S(1)}, u32[]{:S(2)}, u32[]{:S(2)}) async-start(bf16[32,32,128]{2,1,0:T(8,128)(2,1)} %get-tuple-element.84), calls=%async_computation.6 | async-start | bytes 524288 | tf_op jit(solution)/shard_map/all_to_all | solution.py:695
  173.8 13.3 %all-to-all-start.8 = ((bf16[32,32,128]{2,1,0:T(8,128)(2,1)}), bf16[32,32,128]{2,1,0:T(8,128)(2,1)S(1)}, u32[]{:S(2)}, u32[]{:S(2)}) async-start(bf16[32,32,128]{2,1,0:T(8,128)(2,1)} %get-tuple-element.94), calls=%async_computation.8 | async-start | bytes 524288 | tf_op jit(solution)/shard_map/all_to_all | solution.py:695
  204.7 13.3 %all-to-all-start.10 = ((bf16[32,32,128]{2,1,0:T(8,128)(2,1)}), bf16[32,32,128]{2,1,0:T(8,128)(2,1)S(1)}, u32[]{:S(2)}, u32[]{:S(2)}) async-start(bf16[32,32,128]{2,1,0:T(8,128)(2,1)} %get-tuple-element.104), calls=%async_computation.10 | async-start | bytes 524288 | tf_op jit(solution)/shard_map/all_to_all | solution.py:695
  234.7 9.9 %all-to-all-start.12 = ((f32[32,4,128]{2,1,0:T(4,128)}), f32[32,4,128]{2,1,0:T(4,128)S(1)}, u32[]{:S(2)}, u32[]{:S(2)}) async-start(f32[32,4,128]{2,1,0:T(4,128)} %bitcast.5), calls=%async_computation.12 | async-start | bytes 131072 | tf_op jit(solution)/shard_map/all_to_all | solution.py:695

commit v5 on v4

--- a/solution.py
+++ b/solution.py
@@ -78,9 +78,7 @@
             + rates[0] * blocks[1, 0, k].astype(F32)
             - rates[1] * blocks[2, 0, k].astype(F32)
         ).T
-        high = whole.astype(BF16)
-        mixed[0, k * size : (k + 1) * size, :size] = high
-        mixed[0, k * size : (k + 1) * size, size:] = (whole - high.astype(F32)).astype(BF16)
+        mixed[0, k * size : (k + 1) * size] = whole.astype(BF16)
 
     @pl.when(pl.program_id(0) == 0)
     def _():
@@ -118,14 +116,14 @@
             pl.BlockSpec((3, 1, nnz, size, size), lambda i: (0, i, 0, 0, 0)),
         ],
         out_specs=[
-            pl.BlockSpec((1, nnz * size, 2 * size), lambda i: (i, 0, 0)),
+            pl.BlockSpec((1, nnz * size, size), lambda i: (i, 0, 0)),
             whole((width, rim.shape[1])),
             whole((wet.shape[0], width)),
             whole((vectors, rim.shape[1])),
             whole((vectors, slots.shape[1])),
         ],
         out_shape=[
-            pltpu.HBM((block_rows, nnz * size, 2 * size), BF16),
+            pltpu.HBM((block_rows, nnz * size, size), BF16),
             jax.ShapeDtypeStruct((width, rim.shape[1]), BF16),
             jax.ShapeDtypeStruct((wet.shape[0], width), BF16),
             jax.ShapeDtypeStruct((vectors, rim.shape[1]), F32),
@@ -394,9 +392,7 @@
 
 def block_row(ids, extended, mixed, i):
     picked = jnp.concatenate([extended[ids[i, k]] for k in range(ids.shape[1])], 1)
-    pair = jnp.dot(picked, mixed[i], preferred_element_type=F32)
-    size = pair.shape[1] // 2
-    return pair[:, :size] + pair[:, size:]
+    return jnp.dot(picked, mixed[i], preferred_element_type=F32)
 
 
 def advance_kernel(mode, total, peers, *refs):

time: 262 us -> 256 us (0.977)
  Pallas kernels: 92.6 us -> 86.5 us
    pallas_call x6, Pallas kernels: 44.7 us -> 39.1 us  [advance(): pl.pallas_call(functools.partial(advance_kernel, mode, total, peers), in_...]
where the time goes in v5:
time: 256 us
  Pallas kernels  86.5 us (34%)
  waiting for transfers between devices  70.4 us (28%)
  blocking collectives  59.2 us (23%)
  starting transfers between devices  34.7 us (14%)
  local copies, waits for them, and re-layouts  2.99 us (1%)
    all_to_all x6, blocking collectives, exchange(): return lax.all_to_all(parts, AXES, 0, 0, tiled=True)  59.2 us
    all_to_all x7, waiting for transfers between devices, exchange(): return lax.all_to_all(parts, AXES, 0, 0, tiled=True)  39.9 us
    pallas_call x6, Pallas kernels, advance(): pl.pallas_call(functools.partial(advance_kernel, mode, total, peers), in_...  39.1 us
    all_to_all x1, waiting for transfers between devices, local(): mass = lax.all_to_all(blocks, 'col', 0, 0, tiled=True)  30.5 us
    pallas_call x5, Pallas kernels, factor(): pl.pallas_call(functools.partial(factor_kernel, total), in_specs=[VMEM] *...  21.9 us
    all_to_all x7, starting transfers between devices, exchange(): return lax.all_to_all(parts, AXES, 0, 0, tiled=True)  21.5 us
    pallas_call x1, Pallas kernels, combine(): pl.pallas_call(combine_kernel, grid=(block_rows,), in_specs=[SMEM, SMEM,...  8.53 us
    all_to_all x1, starting transfers between devices, local(): mass = lax.all_to_all(blocks, 'col', 0, 0, tiled=True)  7.4 us
  transfers between devices with their start and end apart: 10, of which 8 were waited for; matrix products, arithmetic and copies ran while one was open for 0% of the time, Pallas kernels for 15%

profile of v5, /device:TPU:0, one launch (start us, length us, event | category | flops | bytes accessed | tf_op | source)
XLA Modules:
  0.0 255.5 jit_solution(1559988619027485108)
XLA Ops:
  0.6 2.5 by_owner.1
  3.1 0.0 copy-start.3
  3.1 0.0 copy-start.1
  3.1 0.0 copy-start.2
  3.1 0.0 copy-start.4
  3.1 7.4 %all-to-all-start = ((bf16[8,128,1024]{2,1,0:T(8,128)(2,1)}), bf16[8,128,1024]{2,1,0:T(8,128)(2,1)S(1)}, u32[]{:S(2)}, u32[]{:S(2)}) async-start(bf16[8,128,1024]{2,1,0:T(8,128)(2,1)} %by_owner.1), calls=%async_computation | async-start | bytes 4194304 | tf_op jit(solution)/shard_map/all_to_all | solution.py:703
  11.2 0.0 copy-done.3
  11.2 0.1 copy.10.wet
  11.3 0.0 copy-done.1
  11.3 0.0 copy-done.2
  11.3 0.0 copy-done.4
  11.3 0.0 copy-start
  11.3 2.8 %copy-done = bf16[3,16,4,128,128]{4,3,2,1,0:T(8,128)(2,1)S(1)} copy-done((bf16[3,16,4,128,128]{4,3,2,1,0:T(8,128)(2,1)S(1)}, bf16[3,16,4,128,128]{4,3,2,1,0:T(8,128)(2,1)}, u32[]{:S(2)}) %copy-start) | copy-done | bytes 6291480
  14.1 0.0 copy-start.5
  14.1 8.5 %combine.1 = (bf16[16,512,128]{2,1,0:T(8,128)(2,1)}, bf16[2048,128]{1,0:T(8,128)(2,1)S(1)}, bf16[32,2048]{1,0:T(8,128)(2,1)S(1)}, f32[64,128]{1,0:T(8,128)S(1)}, bf16[64,1024]{1,0:T(8,128)(2,1)S(1)}) custom-call(f32[2]{0:T(128)S(1)} %copy-done.2, s32[1]{0:T(128)S(6)} %copy.17.count, s32[1,128]{1,0:T(1,128)S(1)} %bitcast.13, s32[32,1]{1,0:T(8,128)S(1)} %copy.10.wet, ...), custom_call_target="tpu_custom_call" | custom-call | tf_op jit(solution)/shard_map/combine/pallas_call | solution.py:106
  22.6 1.3 collective-permute-start.1
  23.9 4.6 %collective-permute-start = (f32[64,128]{1,0:T(8,128)S(1)}, f32[64,128]{1,0:T(8,128)S(1)}, u32[]{:S(2)}, u32[]{:S(2)}) collective-permute-start(f32[64,128]{1,0:T(8,128)S(1)} %get-tuple-element.65), channel_id=1, source_target_pairs={{0,1},{1,2},{2,3},{3,4},{4,5},{5,6},{6,7},{7,8},{8,9},{9,10},{10,1... | collective-permute-start | bytes 98312 | tf_op jit(solution)/shard_map/ppermute | solution.py:696
  28.5 0.0 copy-done.5
  28.5 0.1 copy.16.refs_0_
  28.6 30.5 %all-to-all-done = bf16[8,128,1024]{2,1,0:T(8,128)(2,1)S(1)} async-done(((bf16[8,128,1024]{2,1,0:T(8,128)(2,1)}), bf16[8,128,1024]{2,1,0:T(8,128)(2,1)S(1)}, u32[]{:S(2)}, u32[]{:S(2)}) %all-to-all-start) | async-done | bytes 2097184 | tf_op jit(solution)/shard_map/all_to_all | solution.py:703
  59.1 1.4 start_pressure.1
  60.5 3.9 %all-to-all-start.1 = ((bf16[32,16,128]{2,1,0:T(8,128)(2,1)}), bf16[32,16,128]{2,1,0:T(8,128)(2,1)S(1)}, u32[]{:S(2)}, u32[]{:S(2)}) async-start(bf16[32,16,128]{2,1,0:T(8,128)(2,1)} %bitcast.4), calls=%async_computation.1 | async-start | bytes 262144 | tf_op jit(solution)/shard_map/all_to_all | solution.py:691
  64.5 6.4 %spread.1.refs_9_.refs_11_ = bf16[1024,2048]{1,0:T(8,128)(2,1)} custom-call(s32[1]{0:T(128)S(6)} %copy.17.count, s32[1,1024]{1,0:T(1,128)S(1)} %bitcast.12, bf16[8,4,2,16,1024]{4,3,2,1,0:T(8,128)(2,1)S(1)} %bitcast.9), custom_call_target="tpu_custom_call" | custom-call | flops 4294967296 | bytes 4194304 | tf_op jit(solution)/shard_map/spread/pallas_call | solution.py:189
  70.9 0.0 collective-permute-done.1.refs_4_
  70.9 0.0 collective-permute-done.refs_3_
  70.9 1.3 all-to-all-done.1.refs_2_
  72.2 5.9 %advance_first.1 = (bf16[384,2048]{1,0:T(8,128)(2,1)}, f32[128,256]{1,0:T(8,128)S(1)}, f32[32,128]{1,0:T(8,128)S(1)}, bf16[32,32,128]{2,1,0:T(8,128)(2,1)}) custom-call(s32[16,4]{1,0:T(8,128)S(1)} %copy.16.refs_0_, f32[2]{0:T(128)S(1)} %copy-done.2, bf16[32,16,128]{2,1,0:T(8,128)(2,1)S(1)} %all-to-all-done.1.refs_2_, ...), custom_call_target="tpu_custom_call" | custom-call | tf_op jit(solution)/shard_map/advance_first/pallas_call | solution.py:572
  78.2 4.5 %all-to-all-start.2 = ((bf16[32,32,128]{2,1,0:T(8,128)(2,1)}), bf16[32,32,128]{2,1,0:T(8,128)(2,1)S(1)}, u32[]{:S(2)}, u32[]{:S(2)}) async-start(bf16[32,32,128]{2,1,0:T(8,128)(2,1)} %get-tuple-element.69), calls=%async_computation.2 | async-start | bytes 524288 | tf_op jit(solution)/shard_map/all_to_all | solution.py:691
  82.7 0.1 add_convert_fusion._lag.refs_4_.lag
  82.8 10.6 %all-to-all-done.2.received = bf16[32,32,128]{2,1,0:T(8,128)(2,1)S(1)} async-done(((bf16[32,32,128]{2,1,0:T(8,128)(2,1)}), bf16[32,32,128]{2,1,0:T(8,128)(2,1)S(1)}, u32[]{:S(2)}, u32[]{:S(2)}) %all-to-all-start.2) | async-done | bytes 262176 | tf_op jit(solution)/shard_map/all_to_all | solution.py:691
  93.4 0.1 route.5
  93.4 9.9 %all_to_all.70.refs_2_ = f32[32,8,128]{2,1,0:T(8,128)S(1)} all-to-all(f32[32,8,128]{2,1,0:T(8,128)S(1)} %get-tuple-element.70), channel_id=1, replica_groups=mesh['row'=4,'col'=8] {'row','col'}, dimensions={0} | all-to-all | bytes 262144 | tf_op jit(solution)/shard_map/all_to_all | solution.py:691
  103.3 6.8 %advance_mid.4 = (bf16[384,2048]{1,0:T(8,128)(2,1)}, f32[128,256]{1,0:T(8,128)S(1)}, f32[32,128]{1,0:T(8,128)S(1)}, bf16[32,32,128]{2,1,0:T(8,128)(2,1)}, f32[64,128]{1,0:T(8,128)S(1)}, /*index=5*/f32[128,128]{1,0:T(8,128)S(1)}) custom-call(s32[16,4]{1,0:T(8,128)S(1)} %copy.16.refs_0_, f32[2]{0:T(128)S(1)} %copy-done.2, ...), custom_call_target="tpu_custom_call" | custom-call | tf_op jit(solution)/shard_map/advance_mid/pallas_call | solution.py:572
  110.1 2.6 %all-to-all-start.4 = ((bf16[32,32,128]{2,1,0:T(8,128)(2,1)}), bf16[32,32,128]{2,1,0:T(8,128)(2,1)S(1)}, u32[]{:S(2)}, u32[]{:S(2)}) async-start(bf16[32,32,128]{2,1,0:T(8,128)(2,1)} %get-tuple-element.75), calls=%async_computation.4 | async-start | bytes 524288 | tf_op jit(solution)/shard_map/all_to_all | solution.py:691
  112.7 4.4 %factor.5 = (f32[64,128]{1,0:T(8,128)S(1)}, f32[64,128]{1,0:T(8,128)S(1)}, f32[3,64,64]{2,1,0:T(8,128)S(1)}) custom-call(f32[128,128]{1,0:T(8,128)S(1)} %get-tuple-element.76.gram, f32[64,128]{1,0:T(8,128)S(1)} %broadcast_in_dim.15.inner, f32[64,128]{1,0:T(8,128)S(1)} %add_convert_fusion._lag.refs_4_.lag, f32[64,128]{1,0:T(8,128)S(1)} %get-tuple-element.77.both), custom_call_target="tpu_custom_call" | custom-call | flops 100000000 | bytes 10000000 | tf_op jit(solution)/shard_map/factor/pallas_call | solution.py:360
  117.1 6.3 %all-to-all-done.4.received = bf16[32,32,128]{2,1,0:T(8,128)(2,1)S(1)} async-done(((bf16[32,32,128]{2,1,0:T(8,128)(2,1)}), bf16[32,32,128]{2,1,0:T(8,128)(2,1)S(1)}, u32[]{:S(2)}, u32[]{:S(2)}) %all-to-all-start.4) | async-done | bytes 262176 | tf_op jit(solution)/shard_map/all_to_all | solution.py:691
  123.4 0.1 route.6
  123.4 9.8 %all_to_all.71.refs_2_ = f32[32,8,128]{2,1,0:T(8,128)S(1)} all-to-all(f32[32,8,128]{2,1,0:T(8,128)S(1)} %get-tuple-element.79), channel_id=1, replica_groups=mesh['row'=4,'col'=8] {'row','col'}, dimensions={0} | all-to-all | bytes 262144 | tf_op jit(solution)/shard_map/all_to_all | solution.py:691
  133.3 6.8 %advance_mid.5 = (bf16[384,2048]{1,0:T(8,128)(2,1)}, f32[128,256]{1,0:T(8,128)S(1)}, f32[32,128]{1,0:T(8,128)S(1)}, bf16[32,32,128]{2,1,0:T(8,128)(2,1)}, f32[64,128]{1,0:T(8,128)S(1)}, /*index=5*/f32[128,128]{1,0:T(8,128)S(1)}) custom-call(s32[16,4]{1,0:T(8,128)S(1)} %copy.16.refs_0_, f32[2]{0:T(128)S(1)} %copy-done.2, ...), custom_call_target="tpu_custom_call" | custom-call | tf_op jit(solution)/shard_map/advance_mid/pallas_call | solution.py:572
  140.0 2.6 %all-to-all-start.6 = ((bf16[32,32,128]{2,1,0:T(8,128)(2,1)}), bf16[32,32,128]{2,1,0:T(8,128)(2,1)S(1)}, u32[]{:S(2)}, u32[]{:S(2)}) async-start(bf16[32,32,128]{2,1,0:T(8,128)(2,1)} %get-tuple-element.84), calls=%async_computation.6 | async-start | bytes 524288 | tf_op jit(solution)/shard_map/all_to_all | solution.py:691
  142.6 4.4 %factor.6 = (f32[64,128]{1,0:T(8,128)S(1)}, f32[64,128]{1,0:T(8,128)S(1)}, f32[3,64,64]{2,1,0:T(8,128)S(1)}) custom-call(f32[128,128]{1,0:T(8,128)S(1)} %get-tuple-element.85.gram, f32[64,128]{1,0:T(8,128)S(1)} %get-tuple-element.86.inner, f32[64,128]{1,0:T(8,128)S(1)} %get-tuple-element.78._lag.refs_4_.lag, f32[64,128]{1,0:T(8,128)S(1)} %get-tuple-element.87.both), custom_call_target="tpu_custom_call" | custom-call | flops 100000000 | bytes 10000000 | tf_op jit(solution)/shard_map/factor/pallas_call | solution.py:360
  147.0 6.3 %all-to-all-done.6.received = bf16[32,32,128]{2,1,0:T(8,128)(2,1)S(1)} async-done(((bf16[32,32,128]{2,1,0:T(8,128)(2,1)}), bf16[32,32,128]{2,1,0:T(8,128)(2,1)S(1)}, u32[]{:S(2)}, u32[]{:S(2)}) %all-to-all-start.6) | async-done | bytes 262176 | tf_op jit(solution)/shard_map/all_to_all | solution.py:691
  153.3 0.1 route.7
  153.4 9.8 %all_to_all.72.refs_2_ = f32[32,8,128]{2,1,0:T(8,128)S(1)} all-to-all(f32[32,8,128]{2,1,0:T(8,128)S(1)} %get-tuple-element.89), channel_id=1, replica_groups=mesh['row'=4,'col'=8] {'row','col'}, dimensions={0} | all-to-all | bytes 262144 | tf_op jit(solution)/shard_map/all_to_all | solution.py:691
  163.2 6.8 %advance_mid.6 = (bf16[384,2048]{1,0:T(8,128)(2,1)}, f32[128,256]{1,0:T(8,128)S(1)}, f32[32,128]{1,0:T(8,128)S(1)}, bf16[32,32,128]{2,1,0:T(8,128)(2,1)}, f32[64,128]{1,0:T(8,128)S(1)}, /*index=5*/f32[128,128]{1,0:T(8,128)S(1)}) custom-call(s32[16,4]{1,0:T(8,128)S(1)} %copy.16.refs_0_, f32[2]{0:T(128)S(1)} %copy-done.2, ...), custom_call_target="tpu_custom_call" | custom-call | tf_op jit(solution)/shard_map/advance_mid/pallas_call | solution.py:572
  170.0 2.6 %all-to-all-start.8 = ((bf16[32,32,128]{2,1,0:T(8,128)(2,1)}), bf16[32,32,128]{2,1,0:T(8,128)(2,1)S(1)}, u32[]{:S(2)}, u32[]{:S(2)}) async-start(bf16[32,32,128]{2,1,0:T(8,128)(2,1)} %get-tuple-element.94), calls=%async_computation.8 | async-start | bytes 524288 | tf_op jit(solution)/shard_map/all_to_all | solution.py:691
  172.6 4.4 %factor.7 = (f32[64,128]{1,0:T(8,128)S(1)}, f32[64,128]{1,0:T(8,128)S(1)}, f32[3,64,64]{2,1,0:T(8,128)S(1)}) custom-call(f32[128,128]{1,0:T(8,128)S(1)} %get-tuple-element.95.gram, f32[64,128]{1,0:T(8,128)S(1)} %get-tuple-element.96.inner, f32[64,128]{1,0:T(8,128)S(1)} %get-tuple-element.88._lag.refs_4_.lag, f32[64,128]{1,0:T(8,128)S(1)} %get-tuple-element.97.both), custom_call_target="tpu_custom_call" | custom-call | flops 100000000 | bytes 10000000 | tf_op jit(solution)/shard_map/factor/pallas_call | solution.py:360
  176.9 6.3 %all-to-all-done.8.received = bf16[32,32,128]{2,1,0:T(8,128)(2,1)S(1)} async-done(((bf16[32,32,128]{2,1,0:T(8,128)(2,1)}), bf16[32,32,128]{2,1,0:T(8,128)(2,1)S(1)}, u32[]{:S(2)}, u32[]{:S(2)}) %all-to-all-start.8) | async-done | bytes 262176 | tf_op jit(solution)/shard_map/all_to_all | solution.py:691
  183.2 0.1 route.8
  183.3 9.8 %all_to_all.73.refs_2_ = f32[32,8,128]{2,1,0:T(8,128)S(1)} all-to-all(f32[32,8,128]{2,1,0:T(8,128)S(1)} %get-tuple-element.99), channel_id=1, replica_groups=mesh['row'=4,'col'=8] {'row','col'}, dimensions={0} | all-to-all | bytes 262144 | tf_op jit(solution)/shard_map/all_to_all | solution.py:691
  193.1 6.8 %advance_mid.7 = (bf16[384,2048]{1,0:T(8,128)(2,1)}, f32[128,256]{1,0:T(8,128)S(1)}, f32[32,128]{1,0:T(8,128)S(1)}, bf16[32,32,128]{2,1,0:T(8,128)(2,1)}, f32[64,128]{1,0:T(8,128)S(1)}, /*index=5*/f32[128,128]{1,0:T(8,128)S(1)}) custom-call(s32[16,4]{1,0:T(8,128)S(1)} %copy.16.refs_0_, f32[2]{0:T(128)S(1)} %copy-done.2, ...), custom_call_target="tpu_custom_call" | custom-call | tf_op jit(solution)/shard_map/advance_mid/pallas_call | solution.py:572
  199.9 2.6 %all-to-all-start.10 = ((bf16[32,32,128]{2,1,0:T(8,128)(2,1)}), bf16[32,32,128]{2,1,0:T(8,128)(2,1)S(1)}, u32[]{:S(2)}, u32[]{:S(2)}) async-start(bf16[32,32,128]{2,1,0:T(8,128)(2,1)} %get-tuple-element.104), calls=%async_computation.10 | async-start | bytes 524288 | tf_op jit(solution)/shard_map/all_to_all | solution.py:691
  202.5 4.4 %factor.8 = (f32[64,128]{1,0:T(8,128)S(1)}, f32[64,128]{1,0:T(8,128)S(1)}, f32[3,64,64]{2,1,0:T(8,128)S(1)}) custom-call(f32[128,128]{1,0:T(8,128)S(1)} %get-tuple-element.105.gram, f32[64,128]{1,0:T(8,128)S(1)} %get-tuple-element.106.inner, f32[64,128]{1,0:T(8,128)S(1)} %get-tuple-element.98._lag.refs_4_.lag, f32[64,128]{1,0:T(8,128)S(1)} %get-tuple-element.107.both), custom_call_target="tpu_custom_call" | custom-call | flops 100000000 | bytes 10000000 | tf_op jit(solution)/shard_map/factor/pallas_call | solution.py:360
  206.9 6.3 %all-to-all-done.10.received = bf16[32,32,128]{2,1,0:T(8,128)(2,1)S(1)} async-done(((bf16[32,32,128]{2,1,0:T(8,128)(2,1)}), bf16[32,32,128]{2,1,0:T(8,128)(2,1)S(1)}, u32[]{:S(2)}, u32[]{:S(2)}) %all-to-all-start.10) | async-done | bytes 262176 | tf_op jit(solution)/shard_map/all_to_all | solution.py:691
  213.1 0.1 route.9
  213.2 9.8 %all_to_all.74.refs_2_ = f32[32,8,128]{2,1,0:T(8,128)S(1)} all-to-all(f32[32,8,128]{2,1,0:T(8,128)S(1)} %get-tuple-element.109), channel_id=1, replica_groups=mesh['row'=4,'col'=8] {'row','col'}, dimensions={0} | all-to-all | bytes 262144 | tf_op jit(solution)/shard_map/all_to_all | solution.py:691
  223.0 6.0 %advance_last.1 = (bf16[384,2048]{1,0:T(8,128)(2,1)}, f32[128,128]{1,0:T(8,128)}, f32[64,128]{1,0:T(8,128)S(1)}, f32[128,128]{1,0:T(8,128)S(1)}) custom-call(s32[16,4]{1,0:T(8,128)S(1)} %copy.16.refs_0_, f32[2]{0:T(128)S(1)} %copy-done.2, f32[32,8,128]{2,1,0:T(8,128)S(1)} %all_to_all.74.refs_2_, f32[16,128]{1,0:T(8,128)S(1)} %get-tuple-element.110.refs_3_, ...), custom_call_target="tpu_custom_call" | custom-call | tf_op jit(solution)/shard_map/advance_last/pallas_call | solution.py:572
  229.1 2.6 %all-to-all-start.12 = ((f32[32,4,128]{2,1,0:T(4,128)}), f32[32,4,128]{2,1,0:T(4,128)S(1)}, u32[]{:S(2)}, u32[]{:S(2)}) async-start(f32[32,4,128]{2,1,0:T(4,128)} %bitcast.5), calls=%async_computation.12 | async-start | bytes 131072 | tf_op jit(solution)/shard_map/all_to_all | solution.py:691
  231.6 4.4 %factor.9 = (f32[64,128]{1,0:T(8,128)S(1)}, f32[64,128]{1,0:T(8,128)S(1)}, f32[3,64,64]{2,1,0:T(8,128)S(1)}) custom-call(f32[128,128]{1,0:T(8,128)S(1)} %get-tuple-element.115.gram, f32[64,128]{1,0:T(8,128)S(1)} %get-tuple-element.116.inner, f32[64,128]{1,0:T(8,128)S(1)} %get-tuple-element.108._lag.refs_4_.lag, f32[64,128]{1,0:T(8,128)S(1)} %get-tuple-element.117.both), custom_call_target="tpu_custom_call" | custom-call | flops 100000000 | bytes 10000000 | tf_op jit(solution)/shard_map/factor/pallas_call | solution.py:360
  236.0 2.9 %all-to-all-done.12.received = f32[32,4,128]{2,1,0:T(4,128)S(1)} async-done(((f32[32,4,128]{2,1,0:T(4,128)}), f32[32,4,128]{2,1,0:T(4,128)S(1)}, u32[]{:S(2)}, u32[]{:S(2)}) %all-to-all-start.12) | async-done | bytes 65568 | tf_op jit(solution)/shard_map/all_to_all | solution.py:691
  239.0 10.0 %all_to_all.75 = f32[32,4,128]{2,1,0:T(4,128)S(1)} all-to-all(f32[32,4,128]{2,1,0:T(4,128)S(1)} %repeat_sum.1), channel_id=1, replica_groups=mesh['row'=4,'col'=8] {'row','col'}, dimensions={0} | all-to-all | bytes 131072 | tf_op jit(solution)/shard_map/all_to_all | solution.py:691
  249.0 6.4 %finish.1 = (f32[64,2048]{1,0:T(8,128)}, f32[6,3,64,64]{3,2,1,0:T(8,128)}) custom-call(f32[128,128]{1,0:T(8,128)S(1)} %bitcast.10, f32[64,128]{1,0:T(8,128)S(1)} %get-tuple-element.119.inner, f32[64,128]{1,0:T(8,128)S(1)} %get-tuple-element.118._lag.lag, bf16[384,2048]{1,0:T(8,128)(2,1)} %get-tuple-element.120.state, ...), custom_call_target="tpu_custom_call" | custom-call | tf_op jit(solution)/shard_map/finish/pallas_call | solution.py:661
  (4 shorter events, 0.1 us)
Async XLA Ops:
  3.1 8.1 %copy-start.3 = (s32[1024]{0:T(1024)S(1)}, s32[1024]{0:T(1024)}, u32[]{:S(2)}) copy-start(s32[1024]{0:T(1024)} %param.12) | copy-start | bytes 12292
  3.1 8.2 %copy-start.1 = (f32[64,2048]{1,0:T(8,128)S(1)}, f32[64,2048]{1,0:T(8,128)}, u32[]{:S(2)}) copy-start(f32[64,2048]{1,0:T(8,128)} %refs_5_.1) | copy-start | bytes 1572868
  3.1 8.2 %copy-start.2 = (f32[2]{0:T(128)S(1)}, f32[2]{0:T(128)}, u32[]{:S(2)}) copy-start(f32[2]{0:T(128)} %refs_1_.11) | copy-start | bytes 28
  3.1 8.2 %copy-start.4 = (s32[128]{0:T(128)S(1)}, s32[128]{0:T(128)}, u32[]{:S(2)}) copy-start(s32[128]{0:T(128)} %param.11) | copy-start | bytes 1540
  3.1 56.0 %all-to-all-start = ((bf16[8,128,1024]{2,1,0:T(8,128)(2,1)}), bf16[8,128,1024]{2,1,0:T(8,128)(2,1)S(1)}, u32[]{:S(2)}, u32[]{:S(2)}) async-start(bf16[8,128,1024]{2,1,0:T(8,128)(2,1)} %by_owner.1), calls=%async_computation | async-start | bytes 4194304 | tf_op jit(solution)/shard_map/all_to_all | solution.py:703
  11.3 2.8 %copy-start = (bf16[3,16,4,128,128]{4,3,2,1,0:T(8,128)(2,1)S(1)}, bf16[3,16,4,128,128]{4,3,2,1,0:T(8,128)(2,1)}, u32[]{:S(2)}) copy-start(bf16[3,16,4,128,128]{4,3,2,1,0:T(8,128)(2,1)} %blocks.1) | copy-start | bytes 18874372
  14.1 14.4 %copy-start.5 = (s32[16,4]{0,1:T(4,128)S(1)}, s32[16,4]{0,1:T(4,128)}, u32[]{:S(2)}) copy-start(s32[16,4]{0,1:T(4,128)} %param.10) | copy-start | bytes 772
  22.6 48.3 %collective-permute-start.1 = (f32[64,128]{1,0:T(8,128)S(1)}, f32[64,128]{1,0:T(8,128)S(1)}, u32[]{:S(2)}, u32[]{:S(2)}) collective-permute-start(f32[64,128]{1,0:T(8,128)S(1)} %get-tuple-element.65), channel_id=1, source_target_pairs={{1,0},{2,1},{3,2},{4,3},{5,4},{6,5},{7,6},{8,7},{9,8},{10,9},{11,1... | collective-permute-start | bytes 98312 | tf_op jit(solution)/shard_map/ppermute | solution.py:696
  23.9 47.0 %collective-permute-start = (f32[64,128]{1,0:T(8,128)S(1)}, f32[64,128]{1,0:T(8,128)S(1)}, u32[]{:S(2)}, u32[]{:S(2)}) collective-permute-start(f32[64,128]{1,0:T(8,128)S(1)} %get-tuple-element.65), channel_id=1, source_target_pairs={{0,1},{1,2},{2,3},{3,4},{4,5},{5,6},{6,7},{7,8},{8,9},{9,10},{10,1... | collective-permute-start | bytes 98312 | tf_op jit(solution)/shard_map/ppermute | solution.py:696
  60.5 11.7 %all-to-all-start.1 = ((bf16[32,16,128]{2,1,0:T(8,128)(2,1)}), bf16[32,16,128]{2,1,0:T(8,128)(2,1)S(1)}, u32[]{:S(2)}, u32[]{:S(2)}) async-start(bf16[32,16,128]{2,1,0:T(8,128)(2,1)} %bitcast.4), calls=%async_computation.1 | async-start | bytes 262144 | tf_op jit(solution)/shard_map/all_to_all | solution.py:691
  78.2 15.2 %all-to-all-start.2 = ((bf16[32,32,128]{2,1,0:T(8,128)(2,1)}), bf16[32,32,128]{2,1,0:T(8,128)(2,1)S(1)}, u32[]{:S(2)}, u32[]{:S(2)}) async-start(bf16[32,32,128]{2,1,0:T(8,128)(2,1)} %get-tuple-element.69), calls=%async_computation.2 | async-start | bytes 524288 | tf_op jit(solution)/shard_map/all_to_all | solution.py:691
  110.1 13.3 %all-to-all-start.4 = ((bf16[32,32,128]{2,1,0:T(8,128)(2,1)}), bf16[32,32,128]{2,1,0:T(8,128)(2,1)S(1)}, u32[]{:S(2)}, u32[]{:S(2)}) async-start(bf16[32,32,128]{2,1,0:T(8,128)(2,1)} %get-tuple-element.75), calls=%async_computation.4 | async-start | bytes 524288 | tf_op jit(solution)/shard_map/all_to_all | solution.py:691
  140.0 13.3 %all-to-all-start.6 = ((bf16[32,32,128]{2,1,0:T(8,128)(2,1)}), bf16[32,32,128]{2,1,0:T(8,128)(2,1)S(1)}, u32[]{:S(2)}, u32[]{:S(2)}) async-start(bf16[32,32,128]{2,1,0:T(8,128)(2,1)} %get-tuple-element.84), calls=%async_computation.6 | async-start | bytes 524288 | tf_op jit(solution)/shard_map/all_to_all | solution.py:691
  170.0 13.3 %all-to-all-start.8 = ((bf16[32,32,128]{2,1,0:T(8,128)(2,1)}), bf16[32,32,128]{2,1,0:T(8,128)(2,1)S(1)}, u32[]{:S(2)}, u32[]{:S(2)}) async-start(bf16[32,32,128]{2,1,0:T(8,128)(2,1)} %get-tuple-element.94), calls=%async_computation.8 | async-start | bytes 524288 | tf_op jit(solution)/shard_map/all_to_all | solution.py:691
  199.9 13.3 %all-to-all-start.10 = ((bf16[32,32,128]{2,1,0:T(8,128)(2,1)}), bf16[32,32,128]{2,1,0:T(8,128)(2,1)S(1)}, u32[]{:S(2)}, u32[]{:S(2)}) async-start(bf16[32,32,128]{2,1,0:T(8,128)(2,1)} %get-tuple-element.104), calls=%async_computation.10 | async-start | bytes 524288 | tf_op jit(solution)/shard_map/all_to_all | solution.py:691
  229.1 9.9 %all-to-all-start.12 = ((f32[32,4,128]{2,1,0:T(4,128)}), f32[32,4,128]{2,1,0:T(4,128)S(1)}, u32[]{:S(2)}, u32[]{:S(2)}) async-start(f32[32,4,128]{2,1,0:T(4,128)} %bitcast.5), calls=%async_computation.12 | async-start | bytes 131072 | tf_op jit(solution)/shard_map/all_to_all | solution.py:691

commit v6 on v5

--- a/solution.py
+++ b/solution.py
@@ -433,7 +433,6 @@
         for h in range(2):
             part = spread_in.at[pl.ds(h * spread.shape[1], spread.shape[1])]
             load_spread.append(pltpu.make_async_copy(part, spread.at[h], sems.at[3 + h]))
-            load_spread[-1].start()
 
     if mode == "first":
         edge = jnp.concatenate([below[...], above[...]], 1)
@@ -444,6 +443,8 @@
         wet_out[:, :n] = wet
         wet_out[:, n:] = jnp.zeros_like(wet)
         load.wait()
+        for copy in load_spread:
+            copy.start()
         residual = stack[...]
         terms[4 * n :, :] = jnp.zeros((2 * n, width), BF16)
     else:
@@ -464,6 +465,8 @@
             wet_out[:, :n] = wet
             wet_out[:, n:] = exact_rows(wet_held[:, :n], pull)
         load.wait()
+        for copy in load_spread:
+            copy.start()
         mixture = jnp.dot(weights[...], stack[...], preferred_element_type=F32)
         residual = mixture[:n] + mixture[n : 2 * n]
         terms[4 * n : 5 * n, :], terms[5 * n :, :] = halves(mixture[2 * n : 3 * n] + mixture[3 * n :])

time: 256 us -> 258 us (level)
  no operation moved by 1% of the time
where the time goes in v6:
time: 258 us; the launch traced here: 257 us
  Pallas kernels  87.7 us (34%)
  waiting for transfers between devices  70.4 us (27%)
  blocking collectives  59.2 us (23%)
  starting transfers between devices  34.7 us (13%)
  local copies, waits for them, and re-layouts  2.99 us (1%)
    all_to_all x6, blocking collectives, exchange(): return lax.all_to_all(parts, AXES, 0, 0, tiled=True)  59.2 us
    pallas_call x6, Pallas kernels, advance(): pl.pallas_call(functools.partial(advance_kernel, mode, total, peers), in_...  40.3 us
    all_to_all x7, waiting for transfers between devices, exchange(): return lax.all_to_all(parts, AXES, 0, 0, tiled=True)  39.9 us
    all_to_all x1, waiting for transfers between devices, local(): mass = lax.all_to_all(blocks, 'col', 0, 0, tiled=True)  30.5 us
    pallas_call x5, Pallas kernels, factor(): pl.pallas_call(functools.partial(factor_kernel, total), in_specs=[VMEM] *...  21.9 us
    all_to_all x7, starting transfers between devices, exchange(): return lax.all_to_all(parts, AXES, 0, 0, tiled=True)  21.5 us
    pallas_call x1, Pallas kernels, combine(): pl.pallas_call(combine_kernel, grid=(block_rows,), in_specs=[SMEM, SMEM,...  8.53 us
    all_to_all x1, starting transfers between devices, local(): mass = lax.all_to_all(blocks, 'col', 0, 0, tiled=True)  7.4 us
  transfers between devices with their start and end apart: 10, of which 8 were waited for; matrix products, arithmetic and copies ran while one was open for 0% of the time, Pallas kernels for 15%

profile of v6, /device:TPU:0, one launch (start us, length us, event | category | flops | bytes accessed | tf_op | source)
XLA Modules:
  0.0 256.8 jit_solution(12967464461736987403)
XLA Ops:
  0.6 2.5 by_owner.1
  3.1 0.0 copy-start.3
  3.1 0.0 copy-start.1
  3.1 0.0 copy-start.2
  3.1 0.0 copy-start.4
  3.1 7.4 %all-to-all-start = ((bf16[8,128,1024]{2,1,0:T(8,128)(2,1)}), bf16[8,128,1024]{2,1,0:T(8,128)(2,1)S(1)}, u32[]{:S(2)}, u32[]{:S(2)}) async-start(bf16[8,128,1024]{2,1,0:T(8,128)(2,1)} %by_owner.1), calls=%async_computation | async-start | bytes 4194304 | tf_op jit(solution)/shard_map/all_to_all | solution.py:706
  11.2 0.0 copy-done.3
  11.2 0.1 copy.10.wet
  11.3 0.0 copy-done.1
  11.3 0.0 copy-done.2
  11.3 0.0 copy-done.4
  11.3 0.0 copy-start
  11.3 2.8 %copy-done = bf16[3,16,4,128,128]{4,3,2,1,0:T(8,128)(2,1)S(1)} copy-done((bf16[3,16,4,128,128]{4,3,2,1,0:T(8,128)(2,1)S(1)}, bf16[3,16,4,128,128]{4,3,2,1,0:T(8,128)(2,1)}, u32[]{:S(2)}) %copy-start) | copy-done | bytes 6291480
  14.1 0.0 copy-start.5
  14.1 8.5 %combine.1 = (bf16[16,512,128]{2,1,0:T(8,128)(2,1)}, bf16[2048,128]{1,0:T(8,128)(2,1)S(1)}, bf16[32,2048]{1,0:T(8,128)(2,1)S(1)}, f32[64,128]{1,0:T(8,128)S(1)}, bf16[64,1024]{1,0:T(8,128)(2,1)S(1)}) custom-call(f32[2]{0:T(128)S(1)} %copy-done.2, s32[1]{0:T(128)S(6)} %copy.17.count, s32[1,128]{1,0:T(1,128)S(1)} %bitcast.13, s32[32,1]{1,0:T(8,128)S(1)} %copy.10.wet, ...), custom_call_target="tpu_custom_call" | custom-call | tf_op jit(solution)/shard_map/combine/pallas_call | solution.py:106
  22.6 1.3 collective-permute-start.1
  23.9 4.6 %collective-permute-start = (f32[64,128]{1,0:T(8,128)S(1)}, f32[64,128]{1,0:T(8,128)S(1)}, u32[]{:S(2)}, u32[]{:S(2)}) collective-permute-start(f32[64,128]{1,0:T(8,128)S(1)} %get-tuple-element.65), channel_id=1, source_target_pairs={{0,1},{1,2},{2,3},{3,4},{4,5},{5,6},{6,7},{7,8},{8,9},{9,10},{10,1... | collective-permute-start | bytes 98312 | tf_op jit(solution)/shard_map/ppermute | solution.py:699
  28.5 0.0 copy-done.5
  28.5 0.1 copy.16.refs_0_
  28.6 30.5 %all-to-all-done = bf16[8,128,1024]{2,1,0:T(8,128)(2,1)S(1)} async-done(((bf16[8,128,1024]{2,1,0:T(8,128)(2,1)}), bf16[8,128,1024]{2,1,0:T(8,128)(2,1)S(1)}, u32[]{:S(2)}, u32[]{:S(2)}) %all-to-all-start) | async-done | bytes 2097184 | tf_op jit(solution)/shard_map/all_to_all | solution.py:706
  59.1 1.4 start_pressure.1
  60.5 3.9 %all-to-all-start.1 = ((bf16[32,16,128]{2,1,0:T(8,128)(2,1)}), bf16[32,16,128]{2,1,0:T(8,128)(2,1)S(1)}, u32[]{:S(2)}, u32[]{:S(2)}) async-start(bf16[32,16,128]{2,1,0:T(8,128)(2,1)} %bitcast.4), calls=%async_computation.1 | async-start | bytes 262144 | tf_op jit(solution)/shard_map/all_to_all | solution.py:694
  64.5 6.4 %spread.1.refs_9_.refs_11_ = bf16[1024,2048]{1,0:T(8,128)(2,1)} custom-call(s32[1]{0:T(128)S(6)} %copy.17.count, s32[1,1024]{1,0:T(1,128)S(1)} %bitcast.12, bf16[8,4,2,16,1024]{4,3,2,1,0:T(8,128)(2,1)S(1)} %bitcast.9), custom_call_target="tpu_custom_call" | custom-call | flops 4294967296 | bytes 4194304 | tf_op jit(solution)/shard_map/spread/pallas_call | solution.py:189
  70.9 0.0 collective-permute-done.1.refs_4_
  70.9 0.0 collective-permute-done.refs_3_
  70.9 1.3 all-to-all-done.1.refs_2_
  72.2 6.2 %advance_first.1 = (bf16[384,2048]{1,0:T(8,128)(2,1)}, f32[128,256]{1,0:T(8,128)S(1)}, f32[32,128]{1,0:T(8,128)S(1)}, bf16[32,32,128]{2,1,0:T(8,128)(2,1)}) custom-call(s32[16,4]{1,0:T(8,128)S(1)} %copy.16.refs_0_, f32[2]{0:T(128)S(1)} %copy-done.2, bf16[32,16,128]{2,1,0:T(8,128)(2,1)S(1)} %all-to-all-done.1.refs_2_, ...), custom_call_target="tpu_custom_call" | custom-call | tf_op jit(solution)/shard_map/advance_first/pallas_call | solution.py:575
  78.5 4.5 %all-to-all-start.2 = ((bf16[32,32,128]{2,1,0:T(8,128)(2,1)}), bf16[32,32,128]{2,1,0:T(8,128)(2,1)S(1)}, u32[]{:S(2)}, u32[]{:S(2)}) async-start(bf16[32,32,128]{2,1,0:T(8,128)(2,1)} %get-tuple-element.69), calls=%async_computation.2 | async-start | bytes 524288 | tf_op jit(solution)/shard_map/all_to_all | solution.py:694
  83.0 0.1 add_convert_fusion._lag.refs_4_.lag
  83.1 10.6 %all-to-all-done.2.received = bf16[32,32,128]{2,1,0:T(8,128)(2,1)S(1)} async-done(((bf16[32,32,128]{2,1,0:T(8,128)(2,1)}), bf16[32,32,128]{2,1,0:T(8,128)(2,1)S(1)}, u32[]{:S(2)}, u32[]{:S(2)}) %all-to-all-start.2) | async-done | bytes 262176 | tf_op jit(solution)/shard_map/all_to_all | solution.py:694
  93.6 0.1 route.5
  93.7 9.9 %all_to_all.70.refs_2_ = f32[32,8,128]{2,1,0:T(8,128)S(1)} all-to-all(f32[32,8,128]{2,1,0:T(8,128)S(1)} %get-tuple-element.70), channel_id=1, replica_groups=mesh['row'=4,'col'=8] {'row','col'}, dimensions={0} | all-to-all | bytes 262144 | tf_op jit(solution)/shard_map/all_to_all | solution.py:694
  103.6 7.0 %advance_mid.4 = (bf16[384,2048]{1,0:T(8,128)(2,1)}, f32[128,256]{1,0:T(8,128)S(1)}, f32[32,128]{1,0:T(8,128)S(1)}, bf16[32,32,128]{2,1,0:T(8,128)(2,1)}, f32[64,128]{1,0:T(8,128)S(1)}, /*index=5*/f32[128,128]{1,0:T(8,128)S(1)}) custom-call(s32[16,4]{1,0:T(8,128)S(1)} %copy.16.refs_0_, f32[2]{0:T(128)S(1)} %copy-done.2, ...), custom_call_target="tpu_custom_call" | custom-call | tf_op jit(solution)/shard_map/advance_mid/pallas_call | solution.py:575
  110.6 2.6 %all-to-all-start.4 = ((bf16[32,32,128]{2,1,0:T(8,128)(2,1)}), bf16[32,32,128]{2,1,0:T(8,128)(2,1)S(1)}, u32[]{:S(2)}, u32[]{:S(2)}) async-start(bf16[32,32,128]{2,1,0:T(8,128)(2,1)} %get-tuple-element.75), calls=%async_computation.4 | async-start | bytes 524288 | tf_op jit(solution)/shard_map/all_to_all | solution.py:694
  113.3 4.4 %factor.5 = (f32[64,128]{1,0:T(8,128)S(1)}, f32[64,128]{1,0:T(8,128)S(1)}, f32[3,64,64]{2,1,0:T(8,128)S(1)}) custom-call(f32[128,128]{1,0:T(8,128)S(1)} %get-tuple-element.76.gram, f32[64,128]{1,0:T(8,128)S(1)} %broadcast_in_dim.15.inner, f32[64,128]{1,0:T(8,128)S(1)} %add_convert_fusion._lag.refs_4_.lag, f32[64,128]{1,0:T(8,128)S(1)} %get-tuple-element.77.both), custom_call_target="tpu_custom_call" | custom-call | flops 100000000 | bytes 10000000 | tf_op jit(solution)/shard_map/factor/pallas_call | solution.py:360
  117.6 6.3 %all-to-all-done.4.received = bf16[32,32,128]{2,1,0:T(8,128)(2,1)S(1)} async-done(((bf16[32,32,128]{2,1,0:T(8,128)(2,1)}), bf16[32,32,128]{2,1,0:T(8,128)(2,1)S(1)}, u32[]{:S(2)}, u32[]{:S(2)}) %all-to-all-start.4) | async-done | bytes 262176 | tf_op jit(solution)/shard_map/all_to_all | solution.py:694
  123.9 0.1 route.6
  124.0 9.8 %all_to_all.71.refs_2_ = f32[32,8,128]{2,1,0:T(8,128)S(1)} all-to-all(f32[32,8,128]{2,1,0:T(8,128)S(1)} %get-tuple-element.79), channel_id=1, replica_groups=mesh['row'=4,'col'=8] {'row','col'}, dimensions={0} | all-to-all | bytes 262144 | tf_op jit(solution)/shard_map/all_to_all | solution.py:694
  133.8 7.0 %advance_mid.5 = (bf16[384,2048]{1,0:T(8,128)(2,1)}, f32[128,256]{1,0:T(8,128)S(1)}, f32[32,128]{1,0:T(8,128)S(1)}, bf16[32,32,128]{2,1,0:T(8,128)(2,1)}, f32[64,128]{1,0:T(8,128)S(1)}, /*index=5*/f32[128,128]{1,0:T(8,128)S(1)}) custom-call(s32[16,4]{1,0:T(8,128)S(1)} %copy.16.refs_0_, f32[2]{0:T(128)S(1)} %copy-done.2, ...), custom_call_target="tpu_custom_call" | custom-call | tf_op jit(solution)/shard_map/advance_mid/pallas_call | solution.py:575
  140.8 2.6 %all-to-all-start.6 = ((bf16[32,32,128]{2,1,0:T(8,128)(2,1)}), bf16[32,32,128]{2,1,0:T(8,128)(2,1)S(1)}, u32[]{:S(2)}, u32[]{:S(2)}) async-start(bf16[32,32,128]{2,1,0:T(8,128)(2,1)} %get-tuple-element.84), calls=%async_computation.6 | async-start | bytes 524288 | tf_op jit(solution)/shard_map/all_to_all | solution.py:694
  143.4 4.4 %factor.6 = (f32[64,128]{1,0:T(8,128)S(1)}, f32[64,128]{1,0:T(8,128)S(1)}, f32[3,64,64]{2,1,0:T(8,128)S(1)}) custom-call(f32[128,128]{1,0:T(8,128)S(1)} %get-tuple-element.85.gram, f32[64,128]{1,0:T(8,128)S(1)} %get-tuple-element.86.inner, f32[64,128]{1,0:T(8,128)S(1)} %get-tuple-element.78._lag.refs_4_.lag, f32[64,128]{1,0:T(8,128)S(1)} %get-tuple-element.87.both), custom_call_target="tpu_custom_call" | custom-call | flops 100000000 | bytes 10000000 | tf_op jit(solution)/shard_map/factor/pallas_call | solution.py:360
  147.8 6.3 %all-to-all-done.6.received = bf16[32,32,128]{2,1,0:T(8,128)(2,1)S(1)} async-done(((bf16[32,32,128]{2,1,0:T(8,128)(2,1)}), bf16[32,32,128]{2,1,0:T(8,128)(2,1)S(1)}, u32[]{:S(2)}, u32[]{:S(2)}) %all-to-all-start.6) | async-done | bytes 262176 | tf_op jit(solution)/shard_map/all_to_all | solution.py:694
  154.0 0.1 route.7
  154.1 9.8 %all_to_all.72.refs_2_ = f32[32,8,128]{2,1,0:T(8,128)S(1)} all-to-all(f32[32,8,128]{2,1,0:T(8,128)S(1)} %get-tuple-element.89), channel_id=1, replica_groups=mesh['row'=4,'col'=8] {'row','col'}, dimensions={0} | all-to-all | bytes 262144 | tf_op jit(solution)/shard_map/all_to_all | solution.py:694
  163.9 7.0 %advance_mid.6 = (bf16[384,2048]{1,0:T(8,128)(2,1)}, f32[128,256]{1,0:T(8,128)S(1)}, f32[32,128]{1,0:T(8,128)S(1)}, bf16[32,32,128]{2,1,0:T(8,128)(2,1)}, f32[64,128]{1,0:T(8,128)S(1)}, /*index=5*/f32[128,128]{1,0:T(8,128)S(1)}) custom-call(s32[16,4]{1,0:T(8,128)S(1)} %copy.16.refs_0_, f32[2]{0:T(128)S(1)} %copy-done.2, ...), custom_call_target="tpu_custom_call" | custom-call | tf_op jit(solution)/shard_map/advance_mid/pallas_call | solution.py:575
  170.9 2.6 %all-to-all-start.8 = ((bf16[32,32,128]{2,1,0:T(8,128)(2,1)}), bf16[32,32,128]{2,1,0:T(8,128)(2,1)S(1)}, u32[]{:S(2)}, u32[]{:S(2)}) async-start(bf16[32,32,128]{2,1,0:T(8,128)(2,1)} %get-tuple-element.94), calls=%async_computation.8 | async-start | bytes 524288 | tf_op jit(solution)/shard_map/all_to_all | solution.py:694
  173.5 4.4 %factor.7 = (f32[64,128]{1,0:T(8,128)S(1)}, f32[64,128]{1,0:T(8,128)S(1)}, f32[3,64,64]{2,1,0:T(8,128)S(1)}) custom-call(f32[128,128]{1,0:T(8,128)S(1)} %get-tuple-element.95.gram, f32[64,128]{1,0:T(8,128)S(1)} %get-tuple-element.96.inner, f32[64,128]{1,0:T(8,128)S(1)} %get-tuple-element.88._lag.refs_4_.lag, f32[64,128]{1,0:T(8,128)S(1)} %get-tuple-element.97.both), custom_call_target="tpu_custom_call" | custom-call | flops 100000000 | bytes 10000000 | tf_op jit(solution)/shard_map/factor/pallas_call | solution.py:360
  177.9 6.3 %all-to-all-done.8.received = bf16[32,32,128]{2,1,0:T(8,128)(2,1)S(1)} async-done(((bf16[32,32,128]{2,1,0:T(8,128)(2,1)}), bf16[32,32,128]{2,1,0:T(8,128)(2,1)S(1)}, u32[]{:S(2)}, u32[]{:S(2)}) %all-to-all-start.8) | async-done | bytes 262176 | tf_op jit(solution)/shard_map/all_to_all | solution.py:694
  184.2 0.1 route.8
  184.3 9.8 %all_to_all.73.refs_2_ = f32[32,8,128]{2,1,0:T(8,128)S(1)} all-to-all(f32[32,8,128]{2,1,0:T(8,128)S(1)} %get-tuple-element.99), channel_id=1, replica_groups=mesh['row'=4,'col'=8] {'row','col'}, dimensions={0} | all-to-all | bytes 262144 | tf_op jit(solution)/shard_map/all_to_all | solution.py:694
  194.1 7.0 %advance_mid.7 = (bf16[384,2048]{1,0:T(8,128)(2,1)}, f32[128,256]{1,0:T(8,128)S(1)}, f32[32,128]{1,0:T(8,128)S(1)}, bf16[32,32,128]{2,1,0:T(8,128)(2,1)}, f32[64,128]{1,0:T(8,128)S(1)}, /*index=5*/f32[128,128]{1,0:T(8,128)S(1)}) custom-call(s32[16,4]{1,0:T(8,128)S(1)} %copy.16.refs_0_, f32[2]{0:T(128)S(1)} %copy-done.2, ...), custom_call_target="tpu_custom_call" | custom-call | tf_op jit(solution)/shard_map/advance_mid/pallas_call | solution.py:575
  201.1 2.6 %all-to-all-start.10 = ((bf16[32,32,128]{2,1,0:T(8,128)(2,1)}), bf16[32,32,128]{2,1,0:T(8,128)(2,1)S(1)}, u32[]{:S(2)}, u32[]{:S(2)}) async-start(bf16[32,32,128]{2,1,0:T(8,128)(2,1)} %get-tuple-element.104), calls=%async_computation.10 | async-start | bytes 524288 | tf_op jit(solution)/shard_map/all_to_all | solution.py:694
  203.7 4.4 %factor.8 = (f32[64,128]{1,0:T(8,128)S(1)}, f32[64,128]{1,0:T(8,128)S(1)}, f32[3,64,64]{2,1,0:T(8,128)S(1)}) custom-call(f32[128,128]{1,0:T(8,128)S(1)} %get-tuple-element.105.gram, f32[64,128]{1,0:T(8,128)S(1)} %get-tuple-element.106.inner, f32[64,128]{1,0:T(8,128)S(1)} %get-tuple-element.98._lag.refs_4_.lag, f32[64,128]{1,0:T(8,128)S(1)} %get-tuple-element.107.both), custom_call_target="tpu_custom_call" | custom-call | flops 100000000 | bytes 10000000 | tf_op jit(solution)/shard_map/factor/pallas_call | solution.py:360
  208.1 6.3 %all-to-all-done.10.received = bf16[32,32,128]{2,1,0:T(8,128)(2,1)S(1)} async-done(((bf16[32,32,128]{2,1,0:T(8,128)(2,1)}), bf16[32,32,128]{2,1,0:T(8,128)(2,1)S(1)}, u32[]{:S(2)}, u32[]{:S(2)}) %all-to-all-start.10) | async-done | bytes 262176 | tf_op jit(solution)/shard_map/all_to_all | solution.py:694
  214.3 0.1 route.9
  214.4 9.8 %all_to_all.74.refs_2_ = f32[32,8,128]{2,1,0:T(8,128)S(1)} all-to-all(f32[32,8,128]{2,1,0:T(8,128)S(1)} %get-tuple-element.109), channel_id=1, replica_groups=mesh['row'=4,'col'=8] {'row','col'}, dimensions={0} | all-to-all | bytes 262144 | tf_op jit(solution)/shard_map/all_to_all | solution.py:694
  224.2 6.0 %advance_last.1 = (bf16[384,2048]{1,0:T(8,128)(2,1)}, f32[128,128]{1,0:T(8,128)}, f32[64,128]{1,0:T(8,128)S(1)}, f32[128,128]{1,0:T(8,128)S(1)}) custom-call(s32[16,4]{1,0:T(8,128)S(1)} %copy.16.refs_0_, f32[2]{0:T(128)S(1)} %copy-done.2, f32[32,8,128]{2,1,0:T(8,128)S(1)} %all_to_all.74.refs_2_, f32[16,128]{1,0:T(8,128)S(1)} %get-tuple-element.110.refs_3_, ...), custom_call_target="tpu_custom_call" | custom-call | tf_op jit(solution)/shard_map/advance_last/pallas_call | solution.py:575
  230.3 2.6 %all-to-all-start.12 = ((f32[32,4,128]{2,1,0:T(4,128)}), f32[32,4,128]{2,1,0:T(4,128)S(1)}, u32[]{:S(2)}, u32[]{:S(2)}) async-start(f32[32,4,128]{2,1,0:T(4,128)} %bitcast.5), calls=%async_computation.12 | async-start | bytes 131072 | tf_op jit(solution)/shard_map/all_to_all | solution.py:694
  232.9 4.4 %factor.9 = (f32[64,128]{1,0:T(8,128)S(1)}, f32[64,128]{1,0:T(8,128)S(1)}, f32[3,64,64]{2,1,0:T(8,128)S(1)}) custom-call(f32[128,128]{1,0:T(8,128)S(1)} %get-tuple-element.115.gram, f32[64,128]{1,0:T(8,128)S(1)} %get-tuple-element.116.inner, f32[64,128]{1,0:T(8,128)S(1)} %get-tuple-element.108._lag.refs_4_.lag, f32[64,128]{1,0:T(8,128)S(1)} %get-tuple-element.117.both), custom_call_target="tpu_custom_call" | custom-call | flops 100000000 | bytes 10000000 | tf_op jit(solution)/shard_map/factor/pallas_call | solution.py:360
  237.2 2.9 %all-to-all-done.12.received = f32[32,4,128]{2,1,0:T(4,128)S(1)} async-done(((f32[32,4,128]{2,1,0:T(4,128)}), f32[32,4,128]{2,1,0:T(4,128)S(1)}, u32[]{:S(2)}, u32[]{:S(2)}) %all-to-all-start.12) | async-done | bytes 65568 | tf_op jit(solution)/shard_map/all_to_all | solution.py:694
  240.2 10.0 %all_to_all.75 = f32[32,4,128]{2,1,0:T(4,128)S(1)} all-to-all(f32[32,4,128]{2,1,0:T(4,128)S(1)} %repeat_sum.1), channel_id=1, replica_groups=mesh['row'=4,'col'=8] {'row','col'}, dimensions={0} | all-to-all | bytes 131072 | tf_op jit(solution)/shard_map/all_to_all | solution.py:694
  250.2 6.4 %finish.1 = (f32[64,2048]{1,0:T(8,128)}, f32[6,3,64,64]{3,2,1,0:T(8,128)}) custom-call(f32[128,128]{1,0:T(8,128)S(1)} %bitcast.10, f32[64,128]{1,0:T(8,128)S(1)} %get-tuple-element.119.inner, f32[64,128]{1,0:T(8,128)S(1)} %get-tuple-element.118._lag.lag, bf16[384,2048]{1,0:T(8,128)(2,1)} %get-tuple-element.120.state, ...), custom_call_target="tpu_custom_call" | custom-call | tf_op jit(solution)/shard_map/finish/pallas_call | solution.py:664
  (4 shorter events, 0.1 us)
Async XLA Ops:
  3.1 8.1 %copy-start.3 = (s32[1024]{0:T(1024)S(1)}, s32[1024]{0:T(1024)}, u32[]{:S(2)}) copy-start(s32[1024]{0:T(1024)} %param.12) | copy-start | bytes 12292
  3.1 8.2 %copy-start.1 = (f32[64,2048]{1,0:T(8,128)S(1)}, f32[64,2048]{1,0:T(8,128)}, u32[]{:S(2)}) copy-start(f32[64,2048]{1,0:T(8,128)} %refs_5_.1) | copy-start | bytes 1572868
  3.1 8.2 %copy-start.2 = (f32[2]{0:T(128)S(1)}, f32[2]{0:T(128)}, u32[]{:S(2)}) copy-start(f32[2]{0:T(128)} %refs_1_.11) | copy-start | bytes 28
  3.1 8.2 %copy-start.4 = (s32[128]{0:T(128)S(1)}, s32[128]{0:T(128)}, u32[]{:S(2)}) copy-start(s32[128]{0:T(128)} %param.11) | copy-start | bytes 1540
  3.1 56.0 %all-to-all-start = ((bf16[8,128,1024]{2,1,0:T(8,128)(2,1)}), bf16[8,128,1024]{2,1,0:T(8,128)(2,1)S(1)}, u32[]{:S(2)}, u32[]{:S(2)}) async-start(bf16[8,128,1024]{2,1,0:T(8,128)(2,1)} %by_owner.1), calls=%async_computation | async-start | bytes 4194304 | tf_op jit(solution)/shard_map/all_to_all | solution.py:706
  11.3 2.8 %copy-start = (bf16[3,16,4,128,128]{4,3,2,1,0:T(8,128)(2,1)S(1)}, bf16[3,16,4,128,128]{4,3,2,1,0:T(8,128)(2,1)}, u32[]{:S(2)}) copy-start(bf16[3,16,4,128,128]{4,3,2,1,0:T(8,128)(2,1)} %blocks.1) | copy-start | bytes 18874372
  14.1 14.4 %copy-start.5 = (s32[16,4]{0,1:T(4,128)S(1)}, s32[16,4]{0,1:T(4,128)}, u32[]{:S(2)}) copy-start(s32[16,4]{0,1:T(4,128)} %param.10) | copy-start | bytes 772
  22.6 48.3 %collective-permute-start.1 = (f32[64,128]{1,0:T(8,128)S(1)}, f32[64,128]{1,0:T(8,128)S(1)}, u32[]{:S(2)}, u32[]{:S(2)}) collective-permute-start(f32[64,128]{1,0:T(8,128)S(1)} %get-tuple-element.65), channel_id=1, source_target_pairs={{1,0},{2,1},{3,2},{4,3},{5,4},{6,5},{7,6},{8,7},{9,8},{10,9},{11,1... | collective-permute-start | bytes 98312 | tf_op jit(solution)/shard_map/ppermute | solution.py:699
  23.9 47.0 %collective-permute-start = (f32[64,128]{1,0:T(8,128)S(1)}, f32[64,128]{1,0:T(8,128)S(1)}, u32[]{:S(2)}, u32[]{:S(2)}) collective-permute-start(f32[64,128]{1,0:T(8,128)S(1)} %get-tuple-element.65), channel_id=1, source_target_pairs={{0,1},{1,2},{2,3},{3,4},{4,5},{5,6},{6,7},{7,8},{8,9},{9,10},{10,1... | collective-permute-start | bytes 98312 | tf_op jit(solution)/shard_map/ppermute | solution.py:699
  60.5 11.7 %all-to-all-start.1 = ((bf16[32,16,128]{2,1,0:T(8,128)(2,1)}), bf16[32,16,128]{2,1,0:T(8,128)(2,1)S(1)}, u32[]{:S(2)}, u32[]{:S(2)}) async-start(bf16[32,16,128]{2,1,0:T(8,128)(2,1)} %bitcast.4), calls=%async_computation.1 | async-start | bytes 262144 | tf_op jit(solution)/shard_map/all_to_all | solution.py:694
  78.5 15.2 %all-to-all-start.2 = ((bf16[32,32,128]{2,1,0:T(8,128)(2,1)}), bf16[32,32,128]{2,1,0:T(8,128)(2,1)S(1)}, u32[]{:S(2)}, u32[]{:S(2)}) async-start(bf16[32,32,128]{2,1,0:T(8,128)(2,1)} %get-tuple-element.69), calls=%async_computation.2 | async-start | bytes 524288 | tf_op jit(solution)/shard_map/all_to_all | solution.py:694
  110.6 13.3 %all-to-all-start.4 = ((bf16[32,32,128]{2,1,0:T(8,128)(2,1)}), bf16[32,32,128]{2,1,0:T(8,128)(2,1)S(1)}, u32[]{:S(2)}, u32[]{:S(2)}) async-start(bf16[32,32,128]{2,1,0:T(8,128)(2,1)} %get-tuple-element.75), calls=%async_computation.4 | async-start | bytes 524288 | tf_op jit(solution)/shard_map/all_to_all | solution.py:694
  140.8 13.3 %all-to-all-start.6 = ((bf16[32,32,128]{2,1,0:T(8,128)(2,1)}), bf16[32,32,128]{2,1,0:T(8,128)(2,1)S(1)}, u32[]{:S(2)}, u32[]{:S(2)}) async-start(bf16[32,32,128]{2,1,0:T(8,128)(2,1)} %get-tuple-element.84), calls=%async_computation.6 | async-start | bytes 524288 | tf_op jit(solution)/shard_map/all_to_all | solution.py:694
  170.9 13.3 %all-to-all-start.8 = ((bf16[32,32,128]{2,1,0:T(8,128)(2,1)}), bf16[32,32,128]{2,1,0:T(8,128)(2,1)S(1)}, u32[]{:S(2)}, u32[]{:S(2)}) async-start(bf16[32,32,128]{2,1,0:T(8,128)(2,1)} %get-tuple-element.94), calls=%async_computation.8 | async-start | bytes 524288 | tf_op jit(solution)/shard_map/all_to_all | solution.py:694
  201.1 13.3 %all-to-all-start.10 = ((bf16[32,32,128]{2,1,0:T(8,128)(2,1)}), bf16[32,32,128]{2,1,0:T(8,128)(2,1)S(1)}, u32[]{:S(2)}, u32[]{:S(2)}) async-start(bf16[32,32,128]{2,1,0:T(8,128)(2,1)} %get-tuple-element.104), calls=%async_computation.10 | async-start | bytes 524288 | tf_op jit(solution)/shard_map/all_to_all | solution.py:694
  230.3 9.9 %all-to-all-start.12 = ((f32[32,4,128]{2,1,0:T(4,128)}), f32[32,4,128]{2,1,0:T(4,128)S(1)}, u32[]{:S(2)}, u32[]{:S(2)}) async-start(f32[32,4,128]{2,1,0:T(4,128)} %bitcast.5), calls=%async_computation.12 | async-start | bytes 131072 | tf_op jit(solution)/shard_map/all_to_all | solution.py:694
